TPU v7x, 32 devices: a whole 2x2x4 slice. The times are simulated.
32 devices in a mesh: section: 8 (over z, y), dp: 4 (over x, core).
Axes of the slice: x: 2, y: 2, z: 4, core: 2. Of those that a mesh axis runs over, the one named last changes fastest.
Arguments:
- tokens: bfloat16 [4, 4, 128, 768], P(None, 'dp'), may hold values from -6 to 6
- cotangent: bfloat16 [4, 4, 128, 768], P(None, 'dp'), may hold values from -6 to 6
- document_lengths: int32 [4, 4, 4], P(None, 'dp'), may hold values from 1 to 64, 128 in all within a row
- valid_counts: int32 [4, 4], P(None, 'dp'), may hold values from 64 to 128
- first_gain: bfloat16 [16, 768], P('section'), may hold values from 0.5 to 1.5
- first_shift: bfloat16 [16, 768], P('section'), may hold values from -1 to 1
- joint_weight: bfloat16 [16, 768, 2304], P('section'), may hold values from -0.21875 to 0.21875
- query_value_offsets: bfloat16 [16, 1536], P('section'), may hold values from -1 to 1
- output_weight: bfloat16 [16, 768, 768], P('section'), may hold values from -0.625 to 0.625
- output_bias: bfloat16 [16, 768], P('section'), may hold values from -1 to 1
- second_gain: bfloat16 [16, 768], P('section'), may hold values from 0.5 to 1.5
- second_shift: bfloat16 [16, 768], P('section'), may hold values from -1 to 1
- expand_weight: bfloat16 [16, 768, 3072], P('section'), may hold values from -0.21875 to 0.21875
- expand_bias: bfloat16 [16, 3072], P('section'), may hold values from -1 to 1
- contract_weight: bfloat16 [16, 3072, 768], P('section'), may hold values from -0.109375 to 0.109375
- contract_bias: bfloat16 [16, 768], P('section'), may hold values from -1 to 1
Outputs:
- final_hidden: float32 [4, 4, 128, 768], P(None, 'dp', None, 'section')
- input_gradient: float32 [4, 4, 128, 768], P(None, 'dp', None, 'section')
- first_gain_gradient: float32 [16, 768], P('section', 'dp')
- first_shift_gradient: float32 [16, 768], P('section', 'dp')
- joint_weight_gradient: float32 [16, 768, 2304], P('section', 'dp')
- query_value_bias_gradient: float32 [16, 1536], P('section', 'dp')
- output_weight_gradient: float32 [16, 768, 768], P('section', 'dp')
- output_bias_gradient: float32 [16, 768], P('section', 'dp')
- second_gain_gradient: float32 [16, 768], P('section', 'dp')
- second_shift_gradient: float32 [16, 768], P('section', 'dp')
- expand_weight_gradient: float32 [16, 768, 3072], P('section', 'dp')
- expand_bias_gradient: float32 [16, 3072], P('section', 'dp')
- contract_weight_gradient: float32 [16, 3072, 768], P('section', 'dp')
- contract_bias_gradient: float32 [16, 768], P('section', 'dp')
Inputs may be any that keep to these rules, and one draw needn't show every extreme that they name: `document_lengths`: the 4 document lengths of a row sum to 128.
All inputs are finite; a program needn't handle non-finite values.
Results may differ from a plain program's by a relative error of at most 0.024.
Values sent between devices are 32-bit elements; how exact they have to be, the bound alone decides.
No kernel may reach another device: no remote copies, remote signals or barrier semaphores. Data moves between devices by JAX's collectives and lax.ppermute only.
A program may use at most 256 MiB of HBM per device.

v0:
```python
from functools import partial

import jax
import jax.numpy as jnp
from jax import lax
from jax.sharding import PartitionSpec as P

HEAD_DIM = 64
LAYERS = 2


def from_behind(block, axis, distance):
    devices = range(lax.axis_size(axis))
    route = [(i - distance, i) for i in devices if i - distance in devices]
    return lax.ppermute(block, axis, route)


def layer_norm(values, gain, offset):
    center = jnp.mean(values, axis=-1, keepdims=True)
    centered = values - center
    spread = jnp.mean(centered * centered, axis=-1, keepdims=True)
    return centered * lax.rsqrt(spread + 1e-05) * gain + offset


def project(left_operand, right_operand):
    return jnp.einsum(
        "rld,de->rle", left_operand, right_operand, preferred_element_type=jnp.float32
    )


def back_project(gradient, right_operand):
    return jnp.einsum("rle,de->rld", gradient, right_operand, preferred_element_type=jnp.float32)


def weight_product(left_operand, gradient):
    return jnp.einsum("rld,rle->de", left_operand, gradient, preferred_element_type=jnp.float32)


def split_heads(joint_low):
    row_count, length, triple = joint_low.shape
    feature_count = triple // 3
    pieces = joint_low.reshape(row_count, length, 3, feature_count // HEAD_DIM, HEAD_DIM)
    return (pieces[:, :, 0], pieces[:, :, 1], pieces[:, :, 2])


def attend(joint_low, allowed):
    row_count, length, triple = joint_low.shape
    queries, keys_low, values_low = split_heads(joint_low)
    scores = jnp.einsum(
        "rqhd,rkhd->rhqk", queries, keys_low, preferred_element_type=jnp.float32
    ) * HEAD_DIM ** (-0.5)
    masked = jnp.where(allowed[:, None], scores, -1e30)
    probabilities = jax.nn.softmax(masked, axis=-1)
    mixture = jnp.einsum(
        "rhqk,rkhd->rqhd",
        probabilities.astype(jnp.bfloat16),
        values_low,
        preferred_element_type=jnp.float32,
    )
    return (
        masked,
        probabilities,
        mixture.reshape(row_count, length, triple // 3).astype(jnp.bfloat16),
    )


def attend_back(joint_low, allowed, masked, probabilities, gradient_attended):
    row_count, length, triple = joint_low.shape
    queries, keys_low, values_low = split_heads(joint_low)
    gradient_split = gradient_attended.reshape(queries.shape)
    gradient_values = jnp.einsum(
        "rhqk,rqhd->rkhd",
        probabilities.astype(jnp.bfloat16),
        gradient_split,
        preferred_element_type=jnp.float32,
    )
    gradient_probs = jnp.einsum(
        "rqhd,rkhd->rhqk", gradient_split, values_low, preferred_element_type=jnp.float32
    )
    _, softmax_back = jax.vjp(partial(jax.nn.softmax, axis=-1), masked)
    score_gradient = jnp.where(allowed[:, None], softmax_back(gradient_probs)[0], 0.0).astype(
        jnp.bfloat16
    )
    gradient_queries = jnp.einsum(
        "rhqk,rkhd->rqhd", score_gradient, keys_low, preferred_element_type=jnp.float32
    ) * HEAD_DIM ** (-0.5)
    gradient_keys = jnp.einsum(
        "rhqk,rqhd->rkhd", score_gradient, queries, preferred_element_type=jnp.float32
    ) * HEAD_DIM ** (-0.5)
    stacked = jnp.stack([gradient_queries, gradient_keys, gradient_values], axis=2)
    return stacked.reshape(row_count, length, triple)


def layer_parts(hidden, params, allowed, branch_scale):
    (
        first_gain,
        first_shift,
        joint_weight,
        query_value_offsets,
        output_weight,
        output_bias,
        second_gain,
        second_shift,
        expand_weight,
        expand_bias,
        contract_weight,
        contract_bias,
    ) = params
    feature_count = hidden.shape[-1]
    normed_low = layer_norm(
        hidden, first_gain.astype(jnp.float32), first_shift.astype(jnp.float32)
    ).astype(jnp.bfloat16)
    bias_wide = query_value_offsets.astype(jnp.float32)
    bias_full = jnp.concatenate(
        [
            bias_wide[:feature_count],
            jnp.zeros_like(bias_wide[:feature_count]),
            bias_wide[feature_count:],
        ]
    )
    joint_low = (project(normed_low, joint_weight) + bias_full).astype(jnp.bfloat16)
    masked, probabilities, attended_low = attend(joint_low, allowed)
    after_attention = hidden + branch_scale * (
        project(attended_low, output_weight) + output_bias.astype(jnp.float32)
    )
    second_low = layer_norm(
        after_attention, second_gain.astype(jnp.float32), second_shift.astype(jnp.float32)
    ).astype(jnp.bfloat16)
    hidden_pre = project(second_low, expand_weight) + expand_bias.astype(jnp.float32)
    activated_low = jax.nn.gelu(hidden_pre, approximate=True).astype(jnp.bfloat16)
    output = after_attention + branch_scale * (
        project(activated_low, contract_weight) + contract_bias.astype(jnp.float32)
    )
    return (
        normed_low,
        joint_low,
        masked,
        probabilities,
        attended_low,
        after_attention,
        second_low,
        hidden_pre,
        activated_low,
        output,
    )


def layer_back(hidden, gradient_out, params, allowed, branch_scale):
    (
        first_gain,
        first_shift,
        joint_weight,
        query_value_offsets,
        output_weight,
        output_bias,
        second_gain,
        second_shift,
        expand_weight,
        expand_bias,
        contract_weight,
        contract_bias,
    ) = params
    feature_count = hidden.shape[-1]
    (
        normed_low,
        joint_low,
        masked,
        probabilities,
        attended_low,
        after_attention,
        second_low,
        hidden_pre,
        activated_low,
        output,
    ) = layer_parts(hidden, params, allowed, branch_scale)
    gradient_branch = (branch_scale * gradient_out).astype(jnp.bfloat16)
    contract_weight_term = weight_product(activated_low, gradient_branch)
    contract_bias_term = jnp.sum(gradient_branch.astype(jnp.float32), axis=(0, 1))
    gradient_act = back_project(gradient_branch, contract_weight)
    _, gelu_back = jax.vjp(partial(jax.nn.gelu, approximate=True), hidden_pre)
    gradient_pre = gelu_back(gradient_act)[0].astype(jnp.bfloat16)
    expand_weight_term = weight_product(second_low, gradient_pre)
    expand_bias_term = jnp.sum(gradient_pre.astype(jnp.float32), axis=(0, 1))
    second_norm_gradient = back_project(gradient_pre, expand_weight)
    _, second_norm_back = jax.vjp(
        layer_norm,
        after_attention,
        second_gain.astype(jnp.float32),
        second_shift.astype(jnp.float32),
    )
    gradient_after_norm, second_gain_term, second_shift_partial = second_norm_back(
        second_norm_gradient
    )
    gradient_after = gradient_out + gradient_after_norm
    gradient_mixed = (branch_scale * gradient_after).astype(jnp.bfloat16)
    output_weight_term = weight_product(attended_low, gradient_mixed)
    output_bias_term = jnp.sum(gradient_mixed.astype(jnp.float32), axis=(0, 1))
    gradient_attended = back_project(gradient_mixed, output_weight).astype(jnp.bfloat16)
    gradient_joint = attend_back(
        joint_low, allowed, masked, probabilities, gradient_attended
    ).astype(jnp.bfloat16)
    joint_weight_term = weight_product(normed_low, gradient_joint)
    joint_sums = jnp.sum(gradient_joint.astype(jnp.float32), axis=(0, 1))
    query_value_term = jnp.concatenate(
        [joint_sums[:feature_count], joint_sums[2 * feature_count :]]
    )
    gradient_normed = back_project(gradient_joint, joint_weight)
    _, first_norm_back = jax.vjp(
        layer_norm, hidden, first_gain.astype(jnp.float32), first_shift.astype(jnp.float32)
    )
    gradient_hidden_norm, first_gain_term, first_shift_term = first_norm_back(gradient_normed)
    gradient_hidden = gradient_after + gradient_hidden_norm
    return (
        gradient_hidden,
        (
            first_gain_term,
            first_shift_term,
            joint_weight_term,
            query_value_term,
            output_weight_term,
            output_bias_term,
            second_gain_term,
            second_shift_partial,
            expand_weight_term,
            expand_bias_term,
            contract_weight_term,
            contract_bias_term,
        ),
    )


def body(
    tokens,
    cotangent,
    document_lengths,
    valid_counts,
    first_gain,
    first_shift,
    joint_weight,
    query_value_offsets,
    output_weight,
    output_bias,
    second_gain,
    second_shift,
    expand_weight,
    expand_bias,
    contract_weight,
    contract_bias,
):
    weights = (
        first_gain,
        first_shift,
        joint_weight,
        query_value_offsets,
        output_weight,
        output_bias,
        second_gain,
        second_shift,
        expand_weight,
        expand_bias,
        contract_weight,
        contract_bias,
    )
    sections = lax.axis_size("section")
    replicas = lax.axis_size("dp")
    section_index = lax.axis_index("section")
    micro_count, row_count, length, feature_count = tokens.shape
    branch_scale = (LAYERS * sections) ** (-0.5)
    positions = jnp.arange(length, dtype=jnp.int32)
    document_ends = jnp.cumsum(document_lengths, axis=-1)
    segment = jnp.sum(
        (positions[None, None, :, None] >= document_ends[:, :, None, :]).astype(jnp.int32), axis=-1
    )
    causal = positions[:, None] >= positions[None, :]
    live_tokens = (positions[None, None, :] < valid_counts[:, :, None]).astype(jnp.float32)
    first_section = section_index == 0
    last_section = section_index == sections - 1

    def allowed_of(slot_index):
        row_segments = segment[slot_index]
        return (row_segments[:, :, None] == row_segments[:, None, :]) & causal[None]

    def layer_slice(layer_index):
        return tuple((weight_array[layer_index] for weight_array in weights))

    def forward_work(operands):
        arrived_hidden, stored, last_layer_rows, slot_index = operands
        allowed = allowed_of(slot_index)
        section_input = jnp.where(
            first_section, tokens[slot_index].astype(jnp.float32), arrived_hidden
        )
        middle = layer_parts(section_input, layer_slice(0), allowed, branch_scale)[-1]
        output = layer_parts(middle, layer_slice(1), allowed, branch_scale)[-1]
        stored = stored.at[slot_index].set(jnp.stack([section_input, middle]))
        last_layer_rows = last_layer_rows.at[slot_index].set(output)
        return (stored, last_layer_rows, output)

    def forward_skip(operands):
        arrived_hidden, stored, last_layer_rows, slot_index = operands
        return (stored, last_layer_rows, jnp.zeros_like(arrived_hidden))

    def seed_of(arrived_gradient, slot_index):
        return jnp.where(
            last_section,
            cotangent[slot_index].astype(jnp.float32) * live_tokens[slot_index][:, :, None],
            arrived_gradient,
        )

    def backward_work(operands):
        arrived_gradient, stored, gradients, summed, input_rows, slot_index = operands
        allowed = allowed_of(slot_index)
        seed_gradient = seed_of(arrived_gradient, slot_index)
        stored_pair = stored[slot_index]
        gradient_middle, upper_terms = layer_back(
            stored_pair[1], seed_gradient, layer_slice(1), allowed, branch_scale
        )
        gradient_start, lower_terms = layer_back(
            stored_pair[0], gradient_middle, layer_slice(0), allowed, branch_scale
        )
        gradients = tuple(
            (
                running.at[0].add(lower_term).at[1].add(upper_term)
                for running, lower_term, upper_term in zip(gradients, lower_terms, upper_terms)
            )
        )
        input_rows = input_rows.at[slot_index].set(gradient_start)
        return (gradients, summed, input_rows, gradient_start)

    def backward_skip(operands):
        arrived_gradient, stored, gradients, summed, input_rows, slot_index = operands
        return (gradients, summed, input_rows, jnp.zeros_like(arrived_gradient))

    def tick(carry, tick_index):
        sent_hidden, sent_gradient, stored, gradients, summed, last_layer_rows, input_rows = carry
        arrived_hidden = from_behind(sent_hidden, "section", 1)
        arrived_gradient = from_behind(sent_gradient, "section", -1)
        front_index = tick_index - section_index
        front_live = (front_index >= 0) & (front_index < micro_count)
        stored, last_layer_rows, sent_hidden = lax.cond(
            front_live,
            forward_work,
            forward_skip,
            (arrived_hidden, stored, last_layer_rows, jnp.clip(front_index, 0, micro_count - 1)),
        )
        back_index = tick_index - 2 * sections + 1 + section_index
        back_live = (back_index >= 0) & (back_index < micro_count)
        operands = (
            arrived_gradient,
            stored,
            gradients,
            summed,
            input_rows,
            jnp.clip(back_index, 0, micro_count - 1),
        )
        gradients, summed, input_rows, sent_gradient = lax.cond(
            back_live, backward_work, backward_skip, operands
        )
        return (
            (sent_hidden, sent_gradient, stored, gradients, summed, last_layer_rows, input_rows),
            None,
        )

    empty_rows = jnp.zeros((row_count, length, feature_count), jnp.float32)
    stored_start = jnp.zeros((micro_count, 2, row_count, length, feature_count), jnp.float32)
    gradient_start = tuple((jnp.zeros(weight_array.shape, jnp.float32) for weight_array in weights))
    summed_start = tuple(
        (
            jnp.zeros(
                (weight_array.shape[0], weight_array.shape[1] // replicas) + weight_array.shape[2:],
                jnp.float32,
            )
            for weight_array in weights
        )
    )
    buffer_start = jnp.zeros((micro_count, row_count, length, feature_count), jnp.float32)
    tick_count = micro_count + 2 * sections - 1
    carry_start = (
        empty_rows,
        empty_rows,
        stored_start,
        gradient_start,
        summed_start,
        buffer_start,
        buffer_start,
    )
    carry_end, _ = lax.scan(tick, carry_start, jnp.arange(tick_count, dtype=jnp.int32))
    last_layer_rows = jnp.where(last_section, carry_end[5], 0.0)
    input_rows = jnp.where(first_section, carry_end[6], 0.0)
    final_hidden, input_gradient = (
        lax.psum_scatter(last_layer_rows, "section", scatter_dimension=3, tiled=True),
        lax.psum_scatter(input_rows, "section", scatter_dimension=3, tiled=True),
    )
    summed = lax.psum_scatter(carry_end[3], "dp", scatter_dimension=1, tiled=True)
    return (
        final_hidden,
        input_gradient,
        summed[0],
        summed[1],
        summed[2],
        summed[3],
        summed[4],
        summed[5],
        summed[6],
        summed[7],
        summed[8],
        summed[9],
        summed[10],
        summed[11],
    )


def solution(mesh):
    return jax.shard_map(
        body,
        mesh=mesh,
        in_specs=(
            P(None, "dp", None, None),
            P(None, "dp", None, None),
            P(None, "dp", None),
            P(None, "dp"),
            P("section", None),
            P("section", None),
            P("section", None, None),
            P("section", None),
            P("section", None, None),
            P("section", None),
            P("section", None),
            P("section", None),
            P("section", None, None),
            P("section", None),
            P("section", None, None),
            P("section", None),
        ),
        out_specs=(
            P(None, "dp", None, "section"),
            P(None, "dp", None, "section"),
            P("section", "dp"),
            P("section", "dp"),
            P("section", "dp", None),
            P("section", "dp"),
            P("section", "dp", None),
            P("section", "dp"),
            P("section", "dp"),
            P("section", "dp"),
            P("section", "dp", None),
            P("section", "dp"),
            P("section", "dp", None),
            P("section", "dp"),
        ),
        check_vma=False,
    )
```

profile of v0, /device:TPU:0, one launch (start us, length us, event | category | flops | bytes accessed | tf_op | source)
XLA Modules:
  0.0 3959.4 jit_solution(13160607606210497488)
XLA Ops:
  45.0 3131.1 %while.75 = (s32[]{:T(128)}, f32[1,128,768]{2,1,0:T(8,128)}, f32[1,128,768]{2,1,0:T(8,128)}, f32[4,2,1,128,768]{4,3,1,2,0:T(8,128)}, f32[2,768]{1,0:T(2,128)}, /...) while((s32[]{:T(128)}, f32[1,128,768]{2,1,0:T(8,128)}, ...), condition=%wide.region_60.61_spmd.clone.clone, body=%wide.region_2.60_spmd.clone.clone.sunk | while | flops 13825432576 | bytes 506530048 | solution.py:386
  67.2 54.9 %conditional.8 = (f32[4,2,1,128,768]{4,3,1,2,0:T(8,128)}, f32[4,1,128,768]{3,2,1,0:T(8,128)}, f32[1,128,768]{2,1,0:T(8,128)}) conditional(s32[]{:T(128)} %convert_element_type.826, (f32[4,2,1,128,768]{4,3,1,2,0:T(8,128)}, f32[4,1,128,768]{3,2,1,0:T(8,128)}) %tuple.265, (s32[]{:T(128)}, pred[]{:T(512)}, bf16[4,1,128,768]{3,2,1,0:T(8,128)(2,1)}, ...), branch_computations={%region_3.3_spmd, %region_4.18_spmd} | conditional | flops 3793124096 | bytes 50287380 | solution.py:339
  133.4 54.9 %conditional.8 = (f32[4,2,1,128,768]{4,3,1,2,0:T(8,128)}, f32[4,1,128,768]{3,2,1,0:T(8,128)}, f32[1,128,768]{2,1,0:T(8,128)}) conditional(s32[]{:T(128)} %convert_element_type.826, (f32[4,2,1,128,768]{4,3,1,2,0:T(8,128)}, f32[4,1,128,768]{3,2,1,0:T(8,128)}) %tuple.265, (s32[]{:T(128)}, pred[]{:T(512)}, bf16[4,1,128,768]{3,2,1,0:T(8,128)(2,1)}, ...), branch_computations={%region_3.3_spmd, %region_4.18_spmd} | conditional | flops 3793124096 | bytes 50287380 | solution.py:339
  209.0 54.9 %conditional.8 = (f32[4,2,1,128,768]{4,3,1,2,0:T(8,128)}, f32[4,1,128,768]{3,2,1,0:T(8,128)}, f32[1,128,768]{2,1,0:T(8,128)}) conditional(s32[]{:T(128)} %convert_element_type.826, (f32[4,2,1,128,768]{4,3,1,2,0:T(8,128)}, f32[4,1,128,768]{3,2,1,0:T(8,128)}) %tuple.265, (s32[]{:T(128)}, pred[]{:T(512)}, bf16[4,1,128,768]{3,2,1,0:T(8,128)(2,1)}, ...), branch_computations={%region_3.3_spmd, %region_4.18_spmd} | conditional | flops 3793124096 | bytes 50287380 | solution.py:339
  283.8 54.9 %conditional.8 = (f32[4,2,1,128,768]{4,3,1,2,0:T(8,128)}, f32[4,1,128,768]{3,2,1,0:T(8,128)}, f32[1,128,768]{2,1,0:T(8,128)}) conditional(s32[]{:T(128)} %convert_element_type.826, (f32[4,2,1,128,768]{4,3,1,2,0:T(8,128)}, f32[4,1,128,768]{3,2,1,0:T(8,128)}) %tuple.265, (s32[]{:T(128)}, pred[]{:T(512)}, bf16[4,1,128,768]{3,2,1,0:T(8,128)(2,1)}, ...), branch_computations={%region_3.3_spmd, %region_4.18_spmd} | conditional | flops 3793124096 | bytes 50287380 | solution.py:339
  359.7 58.4 %collective-permute-start = (f32[1,128,768]{2,1,0:T(8,128)}, f32[1,128,768]{2,1,0:T(8,128)S(1)}, u32[]{:S(2)}, u32[]{:S(2)}) collective-permute-start(f32[1,128,768]{2,1,0:T(8,128)} %get-tuple-element.2450), channel_id=1, source_target_pairs={{0,4},{4,8},{8,12},{12,16},{16,20},{20,24},{24,28},{1,5},{5,9},{9,... | collective-permute-start | bytes 1179656 | tf_op jit(solution)/shard_map/while/body/eval_jaxpr/ppermute | solution.py:15
  445.2 48.2 %collective-permute-done.1 = f32[1,128,768]{2,1,0:T(8,128)} collective-permute-done((f32[1,128,768]{2,1,0:T(8,128)}, f32[1,128,768]{2,1,0:T(8,128)}, u32[]{:S(2)}, u32[]{:S(2)}) %collective-permute-start.1) | collective-permute-done | bytes 393248 | tf_op jit(solution)/shard_map/while/body/eval_jaxpr/ppermute | solution.py:15
  517.5 56.5 %collective-permute-start = (f32[1,128,768]{2,1,0:T(8,128)}, f32[1,128,768]{2,1,0:T(8,128)S(1)}, u32[]{:S(2)}, u32[]{:S(2)}) collective-permute-start(f32[1,128,768]{2,1,0:T(8,128)} %get-tuple-element.2450), channel_id=1, source_target_pairs={{0,4},{4,8},{8,12},{12,16},{16,20},{20,24},{24,28},{1,5},{5,9},{9,... | collective-permute-start | bytes 1179656 | tf_op jit(solution)/shard_map/while/body/eval_jaxpr/ppermute | solution.py:15
  601.4 48.5 %collective-permute-done.1 = f32[1,128,768]{2,1,0:T(8,128)} collective-permute-done((f32[1,128,768]{2,1,0:T(8,128)}, f32[1,128,768]{2,1,0:T(8,128)}, u32[]{:S(2)}, u32[]{:S(2)}) %collective-permute-start.1) | collective-permute-done | bytes 393248 | tf_op jit(solution)/shard_map/while/body/eval_jaxpr/ppermute | solution.py:15
  676.3 51.6 %collective-permute-start = (f32[1,128,768]{2,1,0:T(8,128)}, f32[1,128,768]{2,1,0:T(8,128)S(1)}, u32[]{:S(2)}, u32[]{:S(2)}) collective-permute-start(f32[1,128,768]{2,1,0:T(8,128)} %get-tuple-element.2450), channel_id=1, source_target_pairs={{0,4},{4,8},{8,12},{12,16},{16,20},{20,24},{24,28},{1,5},{5,9},{9,... | collective-permute-start | bytes 1179656 | tf_op jit(solution)/shard_map/while/body/eval_jaxpr/ppermute | solution.py:15
  739.9 173.3 %collective-permute-start = (f32[1,128,768]{2,1,0:T(8,128)}, f32[1,128,768]{2,1,0:T(8,128)S(1)}, u32[]{:S(2)}, u32[]{:S(2)}) collective-permute-start(f32[1,128,768]{2,1,0:T(8,128)} %get-tuple-element.2450), channel_id=1, source_target_pairs={{0,4},{4,8},{8,12},{12,16},{16,20},{20,24},{24,28},{1,5},{5,9},{9,... | collective-permute-start | bytes 1179656 | tf_op jit(solution)/shard_map/while/body/eval_jaxpr/ppermute | solution.py:15
  919.8 256.0 %collective-permute-done.1 = f32[1,128,768]{2,1,0:T(8,128)} collective-permute-done((f32[1,128,768]{2,1,0:T(8,128)}, f32[1,128,768]{2,1,0:T(8,128)}, u32[]{:S(2)}, u32[]{:S(2)}) %collective-permute-start.1) | collective-permute-done | bytes 393248 | tf_op jit(solution)/shard_map/while/body/eval_jaxpr/ppermute | solution.py:15
  1176.6 206.4 %collective-permute-start = (f32[1,128,768]{2,1,0:T(8,128)}, f32[1,128,768]{2,1,0:T(8,128)S(1)}, u32[]{:S(2)}, u32[]{:S(2)}) collective-permute-start(f32[1,128,768]{2,1,0:T(8,128)} %get-tuple-element.2450), channel_id=1, source_target_pairs={{0,4},{4,8},{8,12},{12,16},{16,20},{20,24},{24,28},{1,5},{5,9},{9,... | collective-permute-start | bytes 1179656 | tf_op jit(solution)/shard_map/while/body/eval_jaxpr/ppermute | solution.py:15
  1389.5 217.4 %collective-permute-done.1 = f32[1,128,768]{2,1,0:T(8,128)} collective-permute-done((f32[1,128,768]{2,1,0:T(8,128)}, f32[1,128,768]{2,1,0:T(8,128)}, u32[]{:S(2)}, u32[]{:S(2)}) %collective-permute-start.1) | collective-permute-done | bytes 393248 | tf_op jit(solution)/shard_map/while/body/eval_jaxpr/ppermute | solution.py:15
  1607.7 245.7 %collective-permute-start = (f32[1,128,768]{2,1,0:T(8,128)}, f32[1,128,768]{2,1,0:T(8,128)S(1)}, u32[]{:S(2)}, u32[]{:S(2)}) collective-permute-start(f32[1,128,768]{2,1,0:T(8,128)} %get-tuple-element.2450), channel_id=1, source_target_pairs={{0,4},{4,8},{8,12},{12,16},{16,20},{20,24},{24,28},{1,5},{5,9},{9,... | collective-permute-start | bytes 1179656 | tf_op jit(solution)/shard_map/while/body/eval_jaxpr/ppermute | solution.py:15
  1860.0 208.6 %collective-permute-done.1 = f32[1,128,768]{2,1,0:T(8,128)} collective-permute-done((f32[1,128,768]{2,1,0:T(8,128)}, f32[1,128,768]{2,1,0:T(8,128)}, u32[]{:S(2)}, u32[]{:S(2)}) %collective-permute-start.1) | collective-permute-done | bytes 393248 | tf_op jit(solution)/shard_map/while/body/eval_jaxpr/ppermute | solution.py:15
  2069.4 207.0 %collective-permute-start = (f32[1,128,768]{2,1,0:T(8,128)}, f32[1,128,768]{2,1,0:T(8,128)S(1)}, u32[]{:S(2)}, u32[]{:S(2)}) collective-permute-start(f32[1,128,768]{2,1,0:T(8,128)} %get-tuple-element.2450), channel_id=1, source_target_pairs={{0,4},{4,8},{8,12},{12,16},{16,20},{20,24},{24,28},{1,5},{5,9},{9,... | collective-permute-start | bytes 1179656 | tf_op jit(solution)/shard_map/while/body/eval_jaxpr/ppermute | solution.py:15
  2296.4 195.4 %conditional.9 = (f32[2,768]{1,0:T(2,128)}, f32[2,768]{1,0:T(2,128)}, f32[2,768,2304]{2,1,0:T(8,128)}, f32[2,1536]{1,0:T(2,128)}, f32[2,768,768]{2,1,0:T(8,128)}...) conditional(s32[]{:T(128)} %convert_element_type.827, ...), branch_computations={%region_19.19_spmd, %region_20.59_spmd} | conditional | flops 10032290816 | bytes 453077440 | solution.py:355
  2521.4 195.9 %conditional.9 = (f32[2,768]{1,0:T(2,128)}, f32[2,768]{1,0:T(2,128)}, f32[2,768,2304]{2,1,0:T(8,128)}, f32[2,1536]{1,0:T(2,128)}, f32[2,768,768]{2,1,0:T(8,128)}...) conditional(s32[]{:T(128)} %convert_element_type.827, ...), branch_computations={%region_19.19_spmd, %region_20.59_spmd} | conditional | flops 10032290816 | bytes 453077440 | solution.py:355
  2746.6 195.8 %conditional.9 = (f32[2,768]{1,0:T(2,128)}, f32[2,768]{1,0:T(2,128)}, f32[2,768,2304]{2,1,0:T(8,128)}, f32[2,1536]{1,0:T(2,128)}, f32[2,768,768]{2,1,0:T(8,128)}...) conditional(s32[]{:T(128)} %convert_element_type.827, ...), branch_computations={%region_19.19_spmd, %region_20.59_spmd} | conditional | flops 10032290816 | bytes 453077440 | solution.py:355
  2970.7 195.9 %conditional.9 = (f32[2,768]{1,0:T(2,128)}, f32[2,768]{1,0:T(2,128)}, f32[2,768,2304]{2,1,0:T(8,128)}, f32[2,1536]{1,0:T(2,128)}, f32[2,768,768]{2,1,0:T(8,128)}...) conditional(s32[]{:T(128)} %convert_element_type.827, ...), branch_computations={%region_19.19_spmd, %region_20.59_spmd} | conditional | flops 10032290816 | bytes 453077440 | solution.py:355
  3220.9 21.8 reduce-scatter.45.cloned.1.call-done
  3244.3 21.7 reduce-scatter.49.cloned.1.call-done
  3290.7 21.7 reduce-scatter.53.cloned.1.call-done
  3313.9 24.2 reduce-scatter.47.cloned.1.call-done
  3339.7 29.0 reduce-scatter.55.cloned.1.call-done
  3370.4 68.1 %reduce-scatter.31.cloned.1.call-done = f32[4,1,128,96]{2,3,1,0:T(8,128)} async-done(((f32[4,1,128,768]{2,3,1,0:T(8,128)}), f32[4,1,128,96]{2,3,1,0:T(8,128)}) %reduce-scatter.31.cloned.1.call-update) | async-done | bytes 196624 | tf_op jit(solution)/shard_map/reduce_scatter | solution.py:390
  3438.5 68.5 %reduce-scatter.33.cloned.1.call-done = f32[4,1,128,96]{2,3,1,0:T(8,128)} async-done(((f32[4,1,128,768]{2,3,1,0:T(8,128)}), f32[4,1,128,96]{2,3,1,0:T(8,128)}) %reduce-scatter.33.cloned.1.call-update) | async-done | bytes 196624 | tf_op jit(solution)/shard_map/reduce_scatter | solution.py:391
  3507.0 49.9 %reduce-scatter.37.cloned.1.call-done = f32[2,192,768]{2,1,0:T(8,128)} async-done(((f32[2,768,768]{2,1,0:T(8,128)}), f32[2,192,768]{2,1,0:T(8,128)}) %reduce-scatter.37.cloned.1.call-update) | async-done | bytes 1179664 | tf_op jit(solution)/shard_map/reduce_scatter | solution.py:393
  3556.9 113.5 %reduce-scatter.35.cloned.1.call-done = f32[2,192,2304]{2,1,0:T(8,128)} async-done(((f32[2,768,2304]{2,1,0:T(8,128)}), f32[2,192,2304]{2,1,0:T(8,128)}) %reduce-scatter.35.cloned.1.call-update) | async-done | bytes 3538960 | tf_op jit(solution)/shard_map/reduce_scatter | solution.py:393
  3670.4 141.0 %reduce-scatter.41.cloned.1.call-done = f32[2,768,768]{2,1,0:T(8,128)} async-done(((f32[2,3072,768]{2,1,0:T(8,128)}), f32[2,768,768]{2,1,0:T(8,128)}) %reduce-scatter.41.cloned.1.call-update) | async-done | bytes 4718608 | tf_op jit(solution)/shard_map/reduce_scatter | solution.py:393
  3811.5 140.9 %reduce-scatter.39.cloned.1.call-done = f32[2,192,3072]{2,1,0:T(8,128)} async-done(((f32[2,768,3072]{2,1,0:T(8,128)}), f32[2,192,3072]{2,1,0:T(8,128)}) %reduce-scatter.39.cloned.1.call-update) | async-done | bytes 4718608 | tf_op jit(solution)/shard_map/reduce_scatter | solution.py:393
  (1838 shorter events, 1426.8 us)
Async XLA Ops:
  7.2 3190.9 %reduce-scatter.57.cloned.1.call-start = ((), (), s32[]{:S(2)}) async-start(), calls=%async_computation.27 | async-start | bytes 491520
  45.2 21.9 collective-permute-start
  50.1 71.9 %collective-permute-start.1 = (f32[1,128,768]{2,1,0:T(8,128)}, f32[1,128,768]{2,1,0:T(8,128)}, u32[]{:S(2)}, u32[]{:S(2)}) collective-permute-start(f32[1,128,768]{2,1,0:T(8,128)} %get-tuple-element.2451), channel_id=1, source_target_pairs={{4,0},{8,4},{12,8},{16,12},{20,16},{24,20},{28,24},{5,1},{9,5},{13... | collective-permute-start | bytes 1179656 | tf_op jit(solution)/shard_map/while/body/eval_jaxpr/ppermute | solution.py:15
  125.4 62.9 %collective-permute-start.1 = (f32[1,128,768]{2,1,0:T(8,128)}, f32[1,128,768]{2,1,0:T(8,128)}, u32[]{:S(2)}, u32[]{:S(2)}) collective-permute-start(f32[1,128,768]{2,1,0:T(8,128)} %get-tuple-element.2451), channel_id=1, source_target_pairs={{4,0},{8,4},{12,8},{16,12},{20,16},{24,20},{28,24},{5,1},{9,5},{13... | collective-permute-start | bytes 1179656 | tf_op jit(solution)/shard_map/while/body/eval_jaxpr/ppermute | solution.py:15
  193.4 70.5 %collective-permute-start.1 = (f32[1,128,768]{2,1,0:T(8,128)}, f32[1,128,768]{2,1,0:T(8,128)}, u32[]{:S(2)}, u32[]{:S(2)}) collective-permute-start(f32[1,128,768]{2,1,0:T(8,128)} %get-tuple-element.2451), channel_id=1, source_target_pairs={{4,0},{8,4},{12,8},{16,12},{20,16},{24,20},{28,24},{5,1},{9,5},{13... | collective-permute-start | bytes 1179656 | tf_op jit(solution)/shard_map/while/body/eval_jaxpr/ppermute | solution.py:15
  269.0 69.6 %collective-permute-start.1 = (f32[1,128,768]{2,1,0:T(8,128)}, f32[1,128,768]{2,1,0:T(8,128)}, u32[]{:S(2)}, u32[]{:S(2)}) collective-permute-start(f32[1,128,768]{2,1,0:T(8,128)} %get-tuple-element.2451), channel_id=1, source_target_pairs={{4,0},{8,4},{12,8},{16,12},{20,16},{24,20},{28,24},{5,1},{9,5},{13... | collective-permute-start | bytes 1179656 | tf_op jit(solution)/shard_map/while/body/eval_jaxpr/ppermute | solution.py:15
  359.7 72.8 %collective-permute-start = (f32[1,128,768]{2,1,0:T(8,128)}, f32[1,128,768]{2,1,0:T(8,128)S(1)}, u32[]{:S(2)}, u32[]{:S(2)}) collective-permute-start(f32[1,128,768]{2,1,0:T(8,128)} %get-tuple-element.2450), channel_id=1, source_target_pairs={{0,4},{4,8},{8,12},{12,16},{16,20},{20,24},{24,28},{1,5},{5,9},{9,... | collective-permute-start | bytes 1179656 | tf_op jit(solution)/shard_map/while/body/eval_jaxpr/ppermute | solution.py:15
  438.4 55.0 %collective-permute-start.1 = (f32[1,128,768]{2,1,0:T(8,128)}, f32[1,128,768]{2,1,0:T(8,128)}, u32[]{:S(2)}, u32[]{:S(2)}) collective-permute-start(f32[1,128,768]{2,1,0:T(8,128)} %get-tuple-element.2451), channel_id=1, source_target_pairs={{4,0},{8,4},{12,8},{16,12},{20,16},{24,20},{28,24},{5,1},{9,5},{13... | collective-permute-start | bytes 1179656 | tf_op jit(solution)/shard_map/while/body/eval_jaxpr/ppermute | solution.py:15
  517.5 62.8 %collective-permute-start = (f32[1,128,768]{2,1,0:T(8,128)}, f32[1,128,768]{2,1,0:T(8,128)S(1)}, u32[]{:S(2)}, u32[]{:S(2)}) collective-permute-start(f32[1,128,768]{2,1,0:T(8,128)} %get-tuple-element.2450), channel_id=1, source_target_pairs={{0,4},{4,8},{8,12},{12,16},{16,20},{20,24},{24,28},{1,5},{5,9},{9,... | collective-permute-start | bytes 1179656 | tf_op jit(solution)/shard_map/while/body/eval_jaxpr/ppermute | solution.py:15
  594.8 55.1 %collective-permute-start.1 = (f32[1,128,768]{2,1,0:T(8,128)}, f32[1,128,768]{2,1,0:T(8,128)}, u32[]{:S(2)}, u32[]{:S(2)}) collective-permute-start(f32[1,128,768]{2,1,0:T(8,128)} %get-tuple-element.2451), channel_id=1, source_target_pairs={{4,0},{8,4},{12,8},{16,12},{20,16},{24,20},{28,24},{5,1},{9,5},{13... | collective-permute-start | bytes 1179656 | tf_op jit(solution)/shard_map/while/body/eval_jaxpr/ppermute | solution.py:15
  676.3 58.7 %collective-permute-start = (f32[1,128,768]{2,1,0:T(8,128)}, f32[1,128,768]{2,1,0:T(8,128)S(1)}, u32[]{:S(2)}, u32[]{:S(2)}) collective-permute-start(f32[1,128,768]{2,1,0:T(8,128)} %get-tuple-element.2450), channel_id=1, source_target_pairs={{0,4},{4,8},{8,12},{12,16},{16,20},{20,24},{24,28},{1,5},{5,9},{9,... | collective-permute-start | bytes 1179656 | tf_op jit(solution)/shard_map/while/body/eval_jaxpr/ppermute | solution.py:15
  739.9 179.1 %collective-permute-start = (f32[1,128,768]{2,1,0:T(8,128)}, f32[1,128,768]{2,1,0:T(8,128)S(1)}, u32[]{:S(2)}, u32[]{:S(2)}) collective-permute-start(f32[1,128,768]{2,1,0:T(8,128)} %get-tuple-element.2450), channel_id=1, source_target_pairs={{0,4},{4,8},{8,12},{12,16},{16,20},{20,24},{24,28},{1,5},{5,9},{9,... | collective-permute-start | bytes 1179656 | tf_op jit(solution)/shard_map/while/body/eval_jaxpr/ppermute | solution.py:15
  913.2 262.6 %collective-permute-start.1 = (f32[1,128,768]{2,1,0:T(8,128)}, f32[1,128,768]{2,1,0:T(8,128)}, u32[]{:S(2)}, u32[]{:S(2)}) collective-permute-start(f32[1,128,768]{2,1,0:T(8,128)} %get-tuple-element.2451), channel_id=1, source_target_pairs={{4,0},{8,4},{12,8},{16,12},{20,16},{24,20},{28,24},{5,1},{9,5},{13... | collective-permute-start | bytes 1179656 | tf_op jit(solution)/shard_map/while/body/eval_jaxpr/ppermute | solution.py:15
  1176.6 212.2 %collective-permute-start = (f32[1,128,768]{2,1,0:T(8,128)}, f32[1,128,768]{2,1,0:T(8,128)S(1)}, u32[]{:S(2)}, u32[]{:S(2)}) collective-permute-start(f32[1,128,768]{2,1,0:T(8,128)} %get-tuple-element.2450), channel_id=1, source_target_pairs={{0,4},{4,8},{8,12},{12,16},{16,20},{20,24},{24,28},{1,5},{5,9},{9,... | collective-permute-start | bytes 1179656 | tf_op jit(solution)/shard_map/while/body/eval_jaxpr/ppermute | solution.py:15
  1383.0 223.9 %collective-permute-start.1 = (f32[1,128,768]{2,1,0:T(8,128)}, f32[1,128,768]{2,1,0:T(8,128)}, u32[]{:S(2)}, u32[]{:S(2)}) collective-permute-start(f32[1,128,768]{2,1,0:T(8,128)} %get-tuple-element.2451), channel_id=1, source_target_pairs={{4,0},{8,4},{12,8},{16,12},{20,16},{24,20},{28,24},{5,1},{9,5},{13... | collective-permute-start | bytes 1179656 | tf_op jit(solution)/shard_map/while/body/eval_jaxpr/ppermute | solution.py:15
  1607.7 251.5 %collective-permute-start = (f32[1,128,768]{2,1,0:T(8,128)}, f32[1,128,768]{2,1,0:T(8,128)S(1)}, u32[]{:S(2)}, u32[]{:S(2)}) collective-permute-start(f32[1,128,768]{2,1,0:T(8,128)} %get-tuple-element.2450), channel_id=1, source_target_pairs={{0,4},{4,8},{8,12},{12,16},{16,20},{20,24},{24,28},{1,5},{5,9},{9,... | collective-permute-start | bytes 1179656 | tf_op jit(solution)/shard_map/while/body/eval_jaxpr/ppermute | solution.py:15
  1853.4 215.2 %collective-permute-start.1 = (f32[1,128,768]{2,1,0:T(8,128)}, f32[1,128,768]{2,1,0:T(8,128)}, u32[]{:S(2)}, u32[]{:S(2)}) collective-permute-start(f32[1,128,768]{2,1,0:T(8,128)} %get-tuple-element.2451), channel_id=1, source_target_pairs={{4,0},{8,4},{12,8},{16,12},{20,16},{24,20},{28,24},{5,1},{9,5},{13... | collective-permute-start | bytes 1179656 | tf_op jit(solution)/shard_map/while/body/eval_jaxpr/ppermute | solution.py:15
  2069.4 212.8 %collective-permute-start = (f32[1,128,768]{2,1,0:T(8,128)}, f32[1,128,768]{2,1,0:T(8,128)S(1)}, u32[]{:S(2)}, u32[]{:S(2)}) collective-permute-start(f32[1,128,768]{2,1,0:T(8,128)} %get-tuple-element.2450), channel_id=1, source_target_pairs={{0,4},{4,8},{8,12},{12,16},{16,20},{20,24},{24,28},{1,5},{5,9},{9,... | collective-permute-start | bytes 1179656 | tf_op jit(solution)/shard_map/while/body/eval_jaxpr/ppermute | solution.py:15
  2949.2 20.7 collective-permute-start
  3177.8 41.6 %reduce-scatter.43.cloned.1.call-start = ((), (), s32[]{:S(2)}) async-start(), calls=%async_computation.20 | async-start | bytes 491520
  3179.5 63.2 %reduce-scatter.45.cloned.1.call-start = ((), (), s32[]{:S(2)}) async-start(), calls=%async_computation.21 | async-start | bytes 491520
  3180.5 85.4 %reduce-scatter.49.cloned.1.call-start = ((), (), s32[]{:S(2)}) async-start(), calls=%async_computation.23 | async-start | bytes 491520
  3181.6 107.5 %reduce-scatter.51.cloned.1.call-start = ((), (), s32[]{:S(2)}) async-start(), calls=%async_computation.24 | async-start | bytes 491520
  3182.6 129.7 %reduce-scatter.53.cloned.1.call-start = ((), (), s32[]{:S(2)}) async-start(), calls=%async_computation.25 | async-start | bytes 491520
  3183.7 154.4 %reduce-scatter.47.cloned.1.call-start = ((), (), s32[]{:S(2)}) async-start(), calls=%async_computation.22 | async-start | bytes 983040
  3184.9 183.7 %reduce-scatter.55.cloned.1.call-start = ((), (), s32[]{:S(2)}) async-start(), calls=%async_computation.26 | async-start | bytes 1966080
  3186.7 251.8 %reduce-scatter.31.cloned.1.call-start = ((), (), s32[]{:S(2)}) async-start(), calls=%async_computation.14 | async-start | bytes 1769472 | tf_op jit(solution)/shard_map/reduce_scatter | solution.py:390
  3189.7 317.3 %reduce-scatter.33.cloned.1.call-start = ((), (), s32[]{:S(2)}) async-start(), calls=%async_computation.15 | async-start | bytes 1769472 | tf_op jit(solution)/shard_map/reduce_scatter | solution.py:391
  3195.4 361.5 %reduce-scatter.37.cloned.1.call-start = ((), (), s32[]{:S(2)}) async-start(), calls=%async_computation.17 | async-start | bytes 5898240 | tf_op jit(solution)/shard_map/reduce_scatter | solution.py:393
  3196.2 474.3 %reduce-scatter.35.cloned.1.call-start = ((), (), s32[]{:S(2)}) async-start(), calls=%async_computation.16 | async-start | bytes 17694720 | tf_op jit(solution)/shard_map/reduce_scatter | solution.py:393
  3196.7 614.7 %reduce-scatter.41.cloned.1.call-start = ((), (), s32[]{:S(2)}) async-start(), calls=%async_computation.19 | async-start | bytes 23592960 | tf_op jit(solution)/shard_map/reduce_scatter | solution.py:393
  3197.5 754.8 %reduce-scatter.39.cloned.1.call-start = ((), (), s32[]{:S(2)}) async-start(), calls=%async_computation.18 | async-start | bytes 23592960 | tf_op jit(solution)/shard_map/reduce_scatter | solution.py:393
  (475 other events, 2951.4 us)
Sparse Core Ops, SparseCore 0:
  3177.9 18.0 reduce-scatter.56
  3198.5 20.8 reduce-scatter.42
  3221.9 20.8 reduce-scatter.44
  3245.1 20.8 reduce-scatter.48
  3268.3 20.8 reduce-scatter.50
  3291.5 20.8 reduce-scatter.52
  3314.8 23.1 reduce-scatter.46
  3340.6 28.0 reduce-scatter.54
  3372.7 65.7 reduce-scatter.30
  3442.4 64.6 reduce-scatter.32
  3510.1 46.7 reduce-scatter.36
  3559.9 110.4 reduce-scatter.34
  3673.6 137.8 reduce-scatter.40
  3814.5 137.8 reduce-scatter.38
where the time goes:
time: 3980 us; the launch traced here: 3960 us
  waiting for transfers between devices  1660 us (42%)
  starting transfers between devices  1080 us (27%)
  matrix products  573 us (14%)
  local copies, waits for them, and re-layouts  288 us (7%)
  other arithmetic  286 us (7%)
  loops' own time  64.9 us (2%)
    ppermute x38, starting transfers between devices, from_behind(): return lax.ppermute(block, axis, route)  1070 us
    ppermute x38, waiting for transfers between devices, from_behind(): return lax.ppermute(block, axis, route)  913 us
    reduce_scatter x4, waiting for transfers between devices, body(): lax.psum_scatter(carry_end[3], 'dp', scatter_dimension=1, tiled=True)  445 us
    dot_general x32, matrix products, weight_product(): jnp.einsum('rld,rle->de', left_operand, gradient, preferred_element_type=...  210 us
    unnamed x22, waiting for transfers between devices  162 us
    dot_general x48, matrix products, project(): jnp.einsum('rld,de->rle', left_operand, right_operand, preferred_element_...  159 us
    dot_general x32, matrix products, back_project(): jnp.einsum('rle,de->rld', gradient, right_operand, preferred_element_type...  119 us
    scatter-add x64, local copies, waits for them, and re-layouts, backward_work(): running.at[0].add(lower_term).at[1].add(upper_term)  85.1 us
  transfers between devices with their start and end apart: 52, of which 37 were waited for; matrix products, arithmetic and copies ran while one was open for 8% of the time, Pallas kernels for 0%

commit v1 on v0

v1 whole, which is shorter than its diff:
```python
from functools import partial

import jax
import jax.numpy as jnp
from jax import lax
from jax.experimental import pallas as pl
from jax.experimental.pallas import tpu as pltpu
from jax.sharding import PartitionSpec as P

HEAD_DIM = 64
LAYERS = 2
PAIR = 2 * HEAD_DIM
CHUNK = 768
EPS = 1e-05
BF16 = jnp.bfloat16
F32 = jnp.float32
ANY = pl.BlockSpec(memory_space=pl.ANY)
SMEM = pl.BlockSpec(memory_space=pltpu.SMEM)
TANH_SCALE = 0.7978845608028654


def mm(left, right):
    return lax.dot_general(left, right, (((1,), (0,)), ((), ())), preferred_element_type=F32)


def mm_nt(left, right):
    return lax.dot_general(left, right, (((1,), (1,)), ((), ())), preferred_element_type=F32)


def mm_tn(left, right):
    return lax.dot_general(left, right, (((0,), (0,)), ((), ())), preferred_element_type=F32)


def norm_parts(values):
    center = jnp.mean(values, axis=-1, keepdims=True)
    centered = values - center
    scale = lax.rsqrt(jnp.mean(centered * centered, axis=-1, keepdims=True) + EPS)
    return centered * scale, scale


def norm_back(normed, scale, gain, gradient):
    weighted = gradient * gain
    mean_weighted = jnp.mean(weighted, axis=-1, keepdims=True)
    mean_product = jnp.mean(weighted * normed, axis=-1, keepdims=True)
    return scale * (weighted - mean_weighted - normed * mean_product)


def stack_halves(block):
    low_lanes = lax.broadcasted_iota(jnp.int32, block.shape, 1) < HEAD_DIM
    zero = jnp.zeros_like(block)
    return jnp.concatenate(
        [jnp.where(low_lanes, block, zero), jnp.where(low_lanes, zero, block)], axis=0
    )


def join_halves(stacked):
    length = stacked.shape[0] // 2
    low_lanes = lax.broadcasted_iota(jnp.int32, (length, PAIR), 1) < HEAD_DIM
    return jnp.where(low_lanes, stacked[:length], stacked[length:])


def pair_probabilities(queries, keys, allowed):
    scores = mm_nt(queries, keys) * HEAD_DIM ** (-0.5)
    scores = jnp.where(allowed, scores, -1e30)
    powers = jnp.exp(scores - jnp.max(scores, axis=-1, keepdims=True))
    return powers / jnp.sum(powers, axis=-1, keepdims=True)


def column_sum(values):
    return jnp.sum(values.astype(F32), axis=0, keepdims=True)


def forward_kernel(
    branch_scale,
    flags,
    tokens,
    arrived,
    allowed_rows,
    wj,
    wo,
    we,
    wc,
    vecs,
    bj,
    be,
    *refs,
):
    names = ("h", "g", "a", "t", "o", "c", "m", "d", "f")
    stash = dict(zip(names, refs[9:18]))
    sent = refs[18]
    (
        wj_v,
        wo_v,
        we_v,
        wc_v,
        vecs_v,
        bj_v,
        be_v,
        allow_v,
        h_v,
        g_v,
        a_v,
        t_v,
        o_v,
        c_v,
        m_v,
        d_v,
        w_sem,
        in_sem,
        out_sem,
    ) = refs[19:]
    active, slot, first, last = flags[0], flags[1], flags[2], flags[3]
    feature = h_v.shape[-1]
    hidden = we_v.shape[-1]

    @pl.when(active == 1)
    def _():
        small = [
            pltpu.make_async_copy(allowed_rows.at[slot], allow_v, in_sem.at[1]),
            pltpu.make_async_copy(vecs, vecs_v, in_sem.at[2]),
            pltpu.make_async_copy(bj, bj_v, in_sem.at[3]),
            pltpu.make_async_copy(be, be_v, in_sem.at[4]),
        ]

        @pl.when(first == 1)
        def _():
            pltpu.make_async_copy(tokens.at[slot], h_v.at[0], in_sem.at[0]).start()

        @pl.when(first == 0)
        def _():
            pltpu.make_async_copy(arrived, h_v.at[0], in_sem.at[0]).start()

        for copy in small:
            copy.start()
        sources = ((wj, wj_v), (wo, wo_v), (we, we_v), (wc, wc_v))
        for layer in range(LAYERS):
            for index, (source, target) in enumerate(sources):
                pltpu.make_async_copy(
                    source.at[layer], target.at[layer], w_sem.at[layer, index]
                ).start()

        def weight_wait(layer, index):
            source, target = sources[index]
            pltpu.make_async_copy(
                source.at[layer], target.at[layer], w_sem.at[layer, index]
            ).wait()

        def put(layer, index, name, value_ref):
            return pltpu.make_async_copy(
                value_ref.at[layer], stash[name].at[layer, slot], out_sem.at[layer, index]
            )

        pltpu.make_async_copy(arrived, h_v.at[0], in_sem.at[0]).wait()
        for copy in small:
            copy.wait()
        allowed = allow_v[...] > 0.5
        allowed = jnp.concatenate([allow_v[...], allow_v[...]], axis=0) > 0.5

        for layer in range(LAYERS):
            put(layer, 0, "h", h_v).start()
            row = h_v[layer]
            normed, _ = norm_parts(row)
            a_low = (
                normed * vecs_v[layer, 0:1, :] + vecs_v[layer, 1:2, :]
            ).astype(BF16)
            a_v[layer] = a_low
            put(layer, 2, "a", a_v).start()
            weight_wait(layer, 0)
            for start in range(0, 3 * feature, CHUNK):
                span = slice(start, start + CHUNK)
                t_v[layer, :, span] = (
                    mm(a_low, wj_v[layer, :, span]) + bj_v[layer, :, span]
                ).astype(BF16)
            put(layer, 3, "t", t_v).start()
            for start in range(0, feature, PAIR):
                queries = stack_halves(t_v[layer, :, start : start + PAIR])
                keys = t_v[layer, :, feature + start : feature + start + PAIR]
                values = t_v[layer, :, 2 * feature + start : 2 * feature + start + PAIR]
                chances = pair_probabilities(queries, keys, allowed).astype(BF16)
                o_v[layer, :, start : start + PAIR] = join_halves(mm(chances, values)).astype(BF16)
            put(layer, 4, "o", o_v).start()
            weight_wait(layer, 1)
            mixed = row + branch_scale * (mm(o_v[layer], wo_v[layer]) + vecs_v[layer, 2:3, :])
            g_v[layer] = mixed
            put(layer, 1, "g", g_v).start()
            normed, _ = norm_parts(mixed)
            c_low = (normed * vecs_v[layer, 3:4, :] + vecs_v[layer, 4:5, :]).astype(BF16)
            c_v[layer] = c_low
            put(layer, 5, "c", c_v).start()
            weight_wait(layer, 2)
            for start in range(0, hidden, CHUNK):
                span = slice(start, start + CHUNK)
                u = mm(c_low, we_v[layer, :, span]) + be_v[layer, :, span]
                square = u * u
                th = jnp.tanh(TANH_SCALE * (u + 0.044715 * (square * u)))
                half = 0.5 * (1.0 + th)
                m_v[layer, :, span] = (u * half).astype(BF16)
                slope = half + 0.5 * u * (1.0 - th * th) * (
                    TANH_SCALE * (1.0 + 3.0 * 0.044715 * square)
                )
                d_v[layer, :, span] = slope.astype(BF16)
            put(layer, 6, "m", m_v).start()
            put(layer, 7, "d", d_v).start()
            weight_wait(layer, 3)
            output = mixed + branch_scale * (mm(m_v[layer], wc_v[layer]) + vecs_v[layer, 5:6, :])
            h_v[layer + 1] = output
        out = pltpu.make_async_copy(h_v.at[LAYERS], sent, in_sem.at[0])
        out.start()

        @pl.when(last == 1)
        def _():
            final = pltpu.make_async_copy(h_v.at[LAYERS], stash["f"].at[slot], in_sem.at[1])
            final.start()
            final.wait()

        for layer in range(LAYERS):
            for index, (name, value_ref) in enumerate(
                (
                    ("h", h_v),
                    ("g", g_v),
                    ("a", a_v),
                    ("t", t_v),
                    ("o", o_v),
                    ("c", c_v),
                    ("m", m_v),
                    ("d", d_v),
                )
            ):
                put(layer, index, name, value_ref).wait()
        out.wait()


def forward_step(branch_scale, flags, tokens, arrived, allowed, weights, vectors, stash):
    length, feature = arrived.shape
    wj, wo, we, wc = weights
    vecs, bj, be = vectors
    hidden = we.shape[-1]
    params = (wj, wo, we, wc, vecs, bj, be)
    scratch = [
        pltpu.VMEM(wj.shape, BF16),
        pltpu.VMEM(wo.shape, BF16),
        pltpu.VMEM(we.shape, BF16),
        pltpu.VMEM(wc.shape, BF16),
        pltpu.VMEM(vecs.shape, F32),
        pltpu.VMEM(bj.shape, F32),
        pltpu.VMEM(be.shape, F32),
        pltpu.VMEM((length, length), F32),
        pltpu.VMEM((LAYERS + 1, length, feature), F32),
        pltpu.VMEM((LAYERS, length, feature), F32),
        pltpu.VMEM((LAYERS, length, feature), BF16),
        pltpu.VMEM((LAYERS, length, 3 * feature), BF16),
        pltpu.VMEM((LAYERS, length, feature), BF16),
        pltpu.VMEM((LAYERS, length, feature), BF16),
        pltpu.VMEM((LAYERS, length, hidden), BF16),
        pltpu.VMEM((LAYERS, length, hidden), BF16),
        pltpu.SemaphoreType.DMA((LAYERS, 4)),
        pltpu.SemaphoreType.DMA((5,)),
        pltpu.SemaphoreType.DMA((LAYERS, 8)),
    ]
    leading = 4 + len(params)
    outs = pl.pallas_call(
        partial(forward_kernel, branch_scale),
        out_shape=tuple(jax.ShapeDtypeStruct(s.shape, s.dtype) for s in stash)
        + (jax.ShapeDtypeStruct((length, feature), F32),),
        in_specs=[SMEM] + [ANY] * (leading - 1 + len(stash)),
        out_specs=tuple([ANY] * (len(stash) + 1)),
        scratch_shapes=scratch,
        input_output_aliases={leading + i: i for i in range(len(stash))},
        compiler_params=pltpu.CompilerParams(vmem_limit_bytes=56 * 1024 * 1024),
        cost_estimate=pl.CostEstimate(
            flops=2 * length * sum(w.size for w in weights),
            bytes_accessed=2 * sum(w.size for w in weights),
            transcendentals=0,
        ),
        name="forward_step",
    )(flags, tokens, arrived, allowed, *params, *stash)
    return outs[:-1], outs[-1]


def backward_kernel(
    branch_scale,
    flags,
    seeds,
    arrived,
    allowed_rows,
    wj,
    wo,
    we,
    wc,
    vecs,
    sh,
    sg,
    st,
    sd,
    *refs,
):
    names = ("gw", "gu", "gz", "gt", "small", "r")
    stash = dict(zip(names, refs[6:12]))
    sent = refs[12]
    (
        wj_v,
        wo_v,
        we_v,
        wc_v,
        vecs_v,
        allow_v,
        h_v,
        g_v,
        t_v,
        d_v,
        grad_v,
        gw_v,
        gu_v,
        gz_v,
        go_v,
        gt_v,
        small_v,
        w_sem,
        in_sem,
        s_sem,
        out_sem,
    ) = refs[13:]
    active, slot, first, last = flags[0], flags[1], flags[2], flags[3]
    feature = h_v.shape[-1]
    hidden = we_v.shape[-1]

    @pl.when(active == 1)
    def _():
        small = [
            pltpu.make_async_copy(allowed_rows.at[slot], allow_v, in_sem.at[1]),
            pltpu.make_async_copy(vecs, vecs_v, in_sem.at[2]),
        ]

        @pl.when(last == 1)
        def _():
            pltpu.make_async_copy(seeds.at[slot], grad_v, in_sem.at[0]).start()

        @pl.when(last == 0)
        def _():
            pltpu.make_async_copy(arrived, grad_v, in_sem.at[0]).start()

        for copy in small:
            copy.start()
        sources = ((wc, wc_v), (we, we_v), (wo, wo_v), (wj, wj_v))
        saved = ((sd, d_v), (sg, g_v), (st, t_v), (sh, h_v))

        def weight_copy(layer, index):
            source, target = sources[index]
            return pltpu.make_async_copy(
                source.at[layer], target.at[layer], w_sem.at[layer, index]
            )

        def saved_copy(layer, index):
            source, target = saved[index]
            return pltpu.make_async_copy(
                source.at[layer, slot], target.at[layer], s_sem.at[layer, index]
            )

        for layer in reversed(range(LAYERS)):
            for index in range(4):
                weight_copy(layer, index).start()
                saved_copy(layer, index).start()

        def put(layer, index, name, value_ref):
            return pltpu.make_async_copy(
                value_ref.at[layer], stash[name].at[layer, slot], out_sem.at[layer, index]
            )

        pltpu.make_async_copy(arrived, grad_v, in_sem.at[0]).wait()
        for copy in small:
            copy.wait()
        allowed = jnp.concatenate([allow_v[...], allow_v[...]], axis=0) > 0.5

        for layer in reversed(range(LAYERS)):
            gw = (branch_scale * grad_v[...]).astype(BF16)
            gw_v[layer] = gw
            put(layer, 0, "gw", gw_v).start()
            small_v[layer, 7:8, :] = column_sum(gw)
            weight_copy(layer, 0).wait()
            saved_copy(layer, 0).wait()
            for index, start in enumerate(range(0, hidden, CHUNK)):
                span = slice(start, start + CHUNK)
                gu = (
                    d_v[layer, :, span].astype(F32) * mm_nt(gw, wc_v[layer, span, :])
                ).astype(BF16)
                gu_v[layer, :, span] = gu
                small_v[layer, 8 + index : 9 + index, :] = column_sum(gu)
            put(layer, 1, "gu", gu_v).start()
            weight_copy(layer, 1).wait()
            gc = mm_nt(gu_v[layer], we_v[layer])
            saved_copy(layer, 1).wait()
            normed, scale = norm_parts(g_v[layer])
            small_v[layer, 4:5, :] = column_sum(gc * normed)
            small_v[layer, 5:6, :] = column_sum(gc)
            gg = grad_v[...] + norm_back(normed, scale, vecs_v[layer, 3:4, :], gc)
            grad_v[...] = gg
            gz = (branch_scale * gg).astype(BF16)
            gz_v[layer] = gz
            put(layer, 2, "gz", gz_v).start()
            small_v[layer, 6:7, :] = column_sum(gz)
            weight_copy(layer, 2).wait()
            go_v[...] = mm_nt(gz, wo_v[layer]).astype(BF16)
            saved_copy(layer, 2).wait()
            for start in range(0, feature, PAIR):
                queries = stack_halves(t_v[layer, :, start : start + PAIR])
                keys = t_v[layer, :, feature + start : feature + start + PAIR]
                values = t_v[layer, :, 2 * feature + start : 2 * feature + start + PAIR]
                go = stack_halves(go_v[:, start : start + PAIR])
                chances = pair_probabilities(queries, keys, allowed)
                g_values = mm_tn(chances.astype(BF16), go)
                g_chances = mm_nt(go, values)
                inner = jnp.sum(chances * g_chances, axis=-1, keepdims=True)
                g_scores = jnp.where(allowed, chances * (g_chances - inner), 0.0).astype(BF16)
                g_queries = join_halves(mm(g_scores, keys)) * HEAD_DIM ** (-0.5)
                g_keys = mm_tn(g_scores, queries) * HEAD_DIM ** (-0.5)
                for part, value in enumerate((g_queries, g_keys, g_values)):
                    low = part * feature + start
                    gt_v[layer, :, low : low + PAIR] = value.astype(BF16)
            put(layer, 3, "gt", gt_v).start()
            small_v[layer, 2:3, :] = column_sum(gt_v[layer, :, :feature])
            small_v[layer, 3:4, :] = column_sum(gt_v[layer, :, 2 * feature :])
            weight_copy(layer, 3).wait()
            ga = mm_nt(gt_v[layer], wj_v[layer])
            saved_copy(layer, 3).wait()
            normed, scale = norm_parts(h_v[layer])
            small_v[layer, 0:1, :] = column_sum(ga * normed)
            small_v[layer, 1:2, :] = column_sum(ga)
            grad_v[...] = grad_v[...] + norm_back(normed, scale, vecs_v[layer, 0:1, :], ga)
            put(layer, 4, "small", small_v).start()
        out = pltpu.make_async_copy(grad_v, sent, in_sem.at[0])
        out.start()

        @pl.when(first == 1)
        def _():
            final = pltpu.make_async_copy(grad_v, stash["r"].at[slot], in_sem.at[1])
            final.start()
            final.wait()

        for layer in range(LAYERS):
            for index, (name, value_ref) in enumerate(
                (
                    ("gw", gw_v),
                    ("gu", gu_v),
                    ("gz", gz_v),
                    ("gt", gt_v),
                    ("small", small_v),
                )
            ):
                put(layer, index, name, value_ref).wait()
        out.wait()


def backward_step(branch_scale, flags, seeds, arrived, allowed, weights, vecs, saved, stash):
    length, feature = arrived.shape
    wj, wo, we, wc = weights
    hidden = we.shape[-1]
    scratch = [
        pltpu.VMEM(wj.shape, BF16),
        pltpu.VMEM(wo.shape, BF16),
        pltpu.VMEM(we.shape, BF16),
        pltpu.VMEM(wc.shape, BF16),
        pltpu.VMEM(vecs.shape, F32),
        pltpu.VMEM((length, length), F32),
        pltpu.VMEM((LAYERS, length, feature), F32),
        pltpu.VMEM((LAYERS, length, feature), F32),
        pltpu.VMEM((LAYERS, length, 3 * feature), BF16),
        pltpu.VMEM((LAYERS, length, hidden), BF16),
        pltpu.VMEM((length, feature), F32),
        pltpu.VMEM((LAYERS, length, feature), BF16),
        pltpu.VMEM((LAYERS, length, hidden), BF16),
        pltpu.VMEM((LAYERS, length, feature), BF16),
        pltpu.VMEM((length, feature), BF16),
        pltpu.VMEM((LAYERS, length, 3 * feature), BF16),
        pltpu.VMEM((LAYERS, 16, feature), F32),
        pltpu.SemaphoreType.DMA((LAYERS, 4)),
        pltpu.SemaphoreType.DMA((3,)),
        pltpu.SemaphoreType.DMA((LAYERS, 4)),
        pltpu.SemaphoreType.DMA((LAYERS, 5)),
    ]
    leading = 4 + 5 + len(saved)
    outs = pl.pallas_call(
        partial(backward_kernel, branch_scale),
        out_shape=tuple(jax.ShapeDtypeStruct(s.shape, s.dtype) for s in stash)
        + (jax.ShapeDtypeStruct((length, feature), F32),),
        in_specs=[SMEM] + [ANY] * (leading - 1 + len(stash)),
        out_specs=tuple([ANY] * (len(stash) + 1)),
        scratch_shapes=scratch,
        input_output_aliases={leading + i: i for i in range(len(stash))},
        compiler_params=pltpu.CompilerParams(vmem_limit_bytes=56 * 1024 * 1024),
        cost_estimate=pl.CostEstimate(
            flops=2 * length * sum(w.size for w in weights),
            bytes_accessed=2 * sum(w.size for w in weights),
            transcendentals=0,
        ),
        name="backward_step",
    )(flags, seeds, arrived, allowed, wj, wo, we, wc, vecs, *saved, *stash)
    return outs[:-1], outs[-1]


def empty_arrays(shapes):
    return pl.pallas_call(
        lambda *refs: None,
        out_shape=tuple(shapes),
        out_specs=tuple([ANY] * len(shapes)),
        name="empty_arrays",
    )()


def body(
    tokens,
    cotangent,
    document_lengths,
    valid_counts,
    first_gain,
    first_shift,
    joint_weight,
    query_value_offsets,
    output_weight,
    output_bias,
    second_gain,
    second_shift,
    expand_weight,
    expand_bias,
    contract_weight,
    contract_bias,
):
    sections = lax.axis_size("section")
    replicas = lax.axis_size("dp")
    section = lax.axis_index("section")
    replica = lax.axis_index("dp")
    near = 2 if replicas % 2 == 0 else 1
    far = replicas // near
    group, member = replica // near, replica % near
    micro_count, row_count, length, feature = tokens.shape
    hidden = expand_weight.shape[-1]
    own = micro_count * row_count
    rows = own * far
    branch_scale = (LAYERS * sections) ** (-0.5)
    first, last = section == 0, section == sections - 1
    positions = jnp.arange(length, dtype=jnp.int32)

    lengths = document_lengths.reshape(own, -1)
    live = (positions[None] < valid_counts.reshape(own, 1)).astype(F32)
    edge_own = jnp.where(
        first,
        tokens.reshape(own, length, feature).astype(F32),
        cotangent.reshape(own, length, feature).astype(F32) * live[:, :, None],
    )
    edges, all_lengths = [edge_own], [lengths]
    for shift in range(1, far):
        pairs = [
            (((g + shift) % far) * near + m, g * near + m) for g in range(far) for m in range(near)
        ]
        ends = sorted({0, sections - 1})
        all_lengths.append(lax.ppermute(lengths, "dp", pairs))
        edges.append(
            lax.ppermute(
                edge_own,
                ("section", "dp"),
                [(e * replicas + a, e * replicas + b) for e in ends for a, b in pairs],
            )
        )
    edge = jnp.concatenate(edges, axis=0)
    document_ends = jnp.cumsum(jnp.concatenate(all_lengths, axis=0), axis=-1)
    segment = jnp.sum(
        (positions[None, :, None] >= document_ends[:, None, :]).astype(jnp.int32), axis=-1
    )
    causal = positions[:, None] >= positions[None, :]
    allowed = ((segment[:, :, None] == segment[:, None, :]) & causal[None]).astype(F32)

    wide = [
        v.astype(F32)
        for v in (first_gain, first_shift, output_bias, second_gain, second_shift, contract_bias)
    ]
    blank = jnp.zeros_like(wide[0])
    vecs = jnp.stack(wide + [blank, blank], axis=1)
    offsets = query_value_offsets.astype(F32)
    bj = jnp.concatenate([offsets[:, :feature], blank, offsets[:, feature:]], axis=1)[:, None]
    be = expand_bias.astype(F32)[:, None]
    weights = (joint_weight, output_weight, expand_weight, contract_weight)

    def saved(width, dtype):
        return jax.ShapeDtypeStruct((LAYERS, rows, length, width), dtype)

    edge_shape = jax.ShapeDtypeStruct((rows, length, feature), F32)
    row_shape = jax.ShapeDtypeStruct((length, feature), F32)
    forward_shapes = (
        saved(feature, F32),
        saved(feature, F32),
        saved(feature, BF16),
        saved(3 * feature, BF16),
        saved(feature, BF16),
        saved(feature, BF16),
        saved(hidden, BF16),
        saved(hidden, BF16),
        edge_shape,
    )
    backward_shapes = (
        saved(feature, BF16),
        saved(hidden, BF16),
        saved(feature, BF16),
        saved(3 * feature, BF16),
        jax.ShapeDtypeStruct((LAYERS, rows, 16, feature), F32),
        edge_shape,
    )
    made = empty_arrays(forward_shapes + backward_shapes + (row_shape, row_shape))
    forward_stash = made[: len(forward_shapes)]
    backward_stash = made[len(forward_shapes) : -2]
    ticks = rows + 2 * (sections - 1)
    onward = [(i, i + 1) for i in range(sections - 1)]
    back = [(i + 1, i) for i in range(sections - 1)]

    def flags_of(row):
        active = (row >= 0) & (row < rows)
        return jnp.stack(
            [
                active.astype(jnp.int32),
                jnp.clip(row, 0, rows - 1),
                first.astype(jnp.int32),
                last.astype(jnp.int32),
            ]
        )

    def forward_tick(tick, carry):
        stash, sent, arrived = carry
        arriving = lax.ppermute(sent, "section", onward)
        flags = flags_of(tick - 2 * section)
        stash, out = forward_step(
            branch_scale, flags, edge, arrived, allowed, weights, (vecs, bj, be), stash
        )
        return stash, out, arriving

    forward_stash, _, _ = lax.fori_loop(
        0, ticks, forward_tick, (forward_stash, made[-2], made[-1])
    )
    sh, sg, sa, st, so, sc, sm, sd, final_rows = forward_stash

    def backward_tick(tick, carry):
        stash, sent, arrived = carry
        arriving = lax.ppermute(sent, "section", back)
        flags = flags_of(tick - 2 * (sections - 1 - section))
        stash, out = backward_step(
            branch_scale, flags, edge, arrived, allowed, weights, vecs, (sh, sg, st, sd), stash
        )
        return stash, out, arriving

    backward_stash, _, _ = lax.fori_loop(
        0, ticks, backward_tick, (backward_stash, made[-2], made[-1])
    )
    gw, gu, gz, gt, small, first_rows = backward_stash

    def near_sum(parts):
        mine = parts[0]
        for shift in range(1, near):
            pairs = [
                (g * near + m, g * near + (m + shift) % near)
                for g in range(far)
                for m in range(near)
            ]
            mine = mine + lax.ppermute(parts[shift], "dp", pairs)
        return mine

    def weight_gradient(left, right):
        width = left.shape[-1]
        left = left.reshape(LAYERS, rows * length, width)
        right = right.reshape(LAYERS, rows * length, right.shape[-1])
        left = lax.dynamic_slice_in_dim(left, group * (width // far), width // far, axis=2)
        product = jnp.einsum("lrd,lre->lde", left, right, preferred_element_type=F32)
        share = width // replicas
        return near_sum(
            [
                lax.dynamic_slice_in_dim(
                    product, ((member + shift) % near) * share, share, axis=1
                )
                for shift in range(near)
            ]
        )

    contract_gradient = weight_gradient(sm, gw)
    expand_gradient = weight_gradient(sc, gu)
    joint_gradient = weight_gradient(sa, gt)
    output_gradient = weight_gradient(so, gz)

    sums = jnp.sum(small, axis=1)
    vectors = [
        sums[:, 0],
        sums[:, 1],
        sums[:, 2:4].reshape(LAYERS, 2 * feature),
        sums[:, 6],
        sums[:, 4],
        sums[:, 5],
        sums[:, 8 : 8 + hidden // feature].reshape(LAYERS, hidden),
        sums[:, 7],
    ]
    packed = jnp.concatenate([v.reshape(LAYERS, replicas, -1) for v in vectors], axis=2)
    shared = near_sum(
        [
            lax.dynamic_index_in_dim(
                packed, group * near + (member + shift) % near, axis=1, keepdims=False
            )
            for shift in range(near)
        ]
    )
    pieces, at = [], 0
    for v in vectors:
        share = v.shape[1] // replicas
        pieces.append(shared[:, at : at + share])
        at += share

    share = feature // sections
    from_first = first_rows[:own].reshape(own, length, feature)
    from_last = final_rows[:own].reshape(own, length, feature)

    def columns(block, index):
        return block[:, :, index * share : (index + 1) * share]

    received = []
    for step in range(1, sections):
        payload = jnp.where(first, columns(from_first, step), columns(from_last, step - 1))
        received.append(
            lax.ppermute(payload, "section", [(0, step), (sections - 1, step - 1)])
        )
    gradient_slices = jnp.stack([columns(from_first, 0)] + received)
    final_slices = jnp.stack(received + [columns(from_last, sections - 1)])
    out_shape = (micro_count, row_count, length, share)
    input_gradient = lax.dynamic_index_in_dim(gradient_slices, section, keepdims=False)
    final_hidden = lax.dynamic_index_in_dim(final_slices, section, keepdims=False)
    return (
        final_hidden.reshape(out_shape),
        input_gradient.reshape(out_shape),
        pieces[0],
        pieces[1],
        joint_gradient,
        pieces[2],
        output_gradient,
        pieces[3],
        pieces[4],
        pieces[5],
        expand_gradient,
        pieces[6],
        contract_gradient,
        pieces[7],
    )


def solution(mesh):
    return jax.shard_map(
        body,
        mesh=mesh,
        in_specs=(
            P(None, "dp", None, None),
            P(None, "dp", None, None),
            P(None, "dp", None),
            P(None, "dp"),
            P("section", None),
            P("section", None),
            P("section", None, None),
            P("section", None),
            P("section", None, None),
            P("section", None),
            P("section", None),
            P("section", None),
            P("section", None, None),
            P("section", None),
            P("section", None, None),
            P("section", None),
        ),
        out_specs=(
            P(None, "dp", None, "section"),
            P(None, "dp", None, "section"),
            P("section", "dp"),
            P("section", "dp"),
            P("section", "dp", None),
            P("section", "dp"),
            P("section", "dp", None),
            P("section", "dp"),
            P("section", "dp"),
            P("section", "dp"),
            P("section", "dp", None),
            P("section", "dp"),
            P("section", "dp", None),
            P("section", "dp"),
        ),
        check_vma=False,
    )
```

time: 3980 us -> 1370 us (0.34)
  waiting for transfers between devices: 1660 us -> 404 us
  starting transfers between devices: 1080 us -> 187 us
  matrix products: 573 us -> 23.2 us
  Pallas kernels: 0 us -> 440 us
  other arithmetic: 286 us -> 130 us
  local copies, waits for them, and re-layouts: 288 us -> 166 us
  loops' own time: 64.9 us -> 12.8 us
    ppermute x38 -> x58, starting transfers between devices: 1070 us -> 187 us  [the longest x22 136 us: forward_tick(): arriving = lax.ppermute(sent, 'section', onward)]
    reduce_scatter x6 -> x0, waiting for transfers between devices: 582 us -> none  [the longest x4 445 us: body(): lax.psum_scatter(carry_end[3], 'dp', scatter_dimension=1, tiled=True)]
    dot_general x168 -> x4, matrix products: 551 us -> 23.2 us  [weight_gradient(): jnp.einsum('lrd,lre->lde', left, right, preferred_element_type=F32)]
    ppermute x38 -> x58, waiting for transfers between devices: 913 us -> 404 us  [the longest x22 306 us: backward_tick(): arriving = lax.ppermute(sent, 'section', back)]
    pallas_call x0 -> x45, Pallas kernels: none -> 440 us  [the longest x22 271 us: backward_step(): pl.pallas_call(partial(backward_kernel, branch_scale), out_shape=tuple((j...]
    unnamed x22 -> x0, waiting for transfers between devices: 162 us -> none
    while x2 -> x88, local copies, waits for them, and re-layouts: 3.23 us -> 138 us  [body(): lax.scan(tick, carry_start, jnp.arange(tick_count, dtype=jnp.int32))]
    scatter-add x64 -> x0, local copies, waits for them, and re-layouts: 85.1 us -> none  [backward_work(): running.at[0].add(lower_term).at[1].add(upper_term)]
  transfers between devices with their start and end apart: 52 -> 58, of which waited for: 37 -> 44; matrix products, arithmetic and copies ran while one was open for 8% -> 11% of each run, Pallas kernels for 0% -> 32%
where the time goes in v1:
time: 1370 us; the launch traced here: 1360 us
  Pallas kernels  440 us (32%)
  waiting for transfers between devices  404 us (29%)
  starting transfers between devices  187 us (14%)
  local copies, waits for them, and re-layouts  166 us (12%)
  other arithmetic  130 us (9%)
  matrix products  23.2 us (2%)
    ppermute x22, waiting for transfers between devices, backward_tick(): arriving = lax.ppermute(sent, 'section', back)  306 us
    pallas_call x22, Pallas kernels, backward_step(): pl.pallas_call(partial(backward_kernel, branch_scale), out_shape=tuple((j...  271 us
    pallas_call x22, Pallas kernels, forward_step(): pl.pallas_call(partial(forward_kernel, branch_scale), out_shape=tuple((ja...  169 us
    while x88, local copies, waits for them, and re-layouts  138 us
    ppermute x22, starting transfers between devices, forward_tick(): arriving = lax.ppermute(sent, 'section', onward)  136 us
    convert_element_type x44, other arithmetic, body(): ((segment[:, :, None] == segment[:, None, :]) & causal[None]).astype(F32)  77.1 us
    ppermute x7, waiting for transfers between devices, body(): lax.ppermute(payload, 'section', [(0, step), (sections - 1, step - 1)])  36.8 us
    ppermute x1, waiting for transfers between devices, body(): all_lengths.append(lax.ppermute(lengths, 'dp', pairs))  30.6 us
  transfers between devices with their start and end apart: 58, of which 44 were waited for; matrix products, arithmetic and copies ran while one was open for 11% of the time, Pallas kernels for 32%

profile of v1, /device:TPU:0, one launch (start us, length us, event | category | flops | bytes accessed | tf_op | source)
XLA Modules:
  0.0 1364.8 jit_solution(7910351047681424746)
XLA Ops:
  11.9 30.6 %collective-permute-done.3 = s32[4,4]{1,0:T(4,128)S(1)} collective-permute-done((s32[4,4]{1,0:T(4,128)S(1)}, s32[4,4]{1,0:T(4,128)S(1)}, u32[]{:S(2)}, u32[]{:S(2)}) %collective-permute-start.3) | collective-permute-done | bytes 96 | tf_op jit(solution)/shard_map/ppermute | solution.py:555
  45.7 463.9 %while.66 = (s32[]{:T(128)}, f32[2,8,128,768]{3,2,1,0:T(8,128)}, f32[2,8,128,768]{3,2,1,0:T(8,128)}, bf16[2,8,128,768]{3,2,1,0:T(8,128)(2,1)}, bf16[2,8,128,2304...) while((s32[]{:T(128)}, f32[2,8,128,768]{3,2,1,0:T(8,128)}, ...), condition=%wide.region_3.4_spmd.clone, body=%wide.region_2.3_spmd.clone.sunk | while | flops 3624271872 | bytes 32002444 | solution.py:633
  51.8 19.5 %forward_step.7 = (f32[2,8,128,768]{3,2,1,0:T(8,128)}, f32[2,8,128,768]{3,2,1,0:T(8,128)}, bf16[2,8,128,768]{3,2,1,0:T(8,128)(2,1)}, bf16[2,8,128,2304]{3,2,1,0:...) custom-call(s32[4]{0:T(128)} %pad_add_fusion.5.flags, ...), custom_call_target="tpu_custom_call", output_to_operand_aliasing={{0}: (11, {}), {1}: (12, {}), {2}: (13, {}), {3}: (14, {}),... | custom-call | flops 3623878656 | bytes 28311552 | tf_op jit(solution)/shard_map/while/body/eval_jaxpr/forward_step/pallas_call | solution.py:261
  79.2 19.5 %forward_step.7 = (f32[2,8,128,768]{3,2,1,0:T(8,128)}, f32[2,8,128,768]{3,2,1,0:T(8,128)}, bf16[2,8,128,768]{3,2,1,0:T(8,128)(2,1)}, bf16[2,8,128,2304]{3,2,1,0:...) custom-call(s32[4]{0:T(128)} %pad_add_fusion.5.flags, ...), custom_call_target="tpu_custom_call", output_to_operand_aliasing={{0}: (11, {}), {1}: (12, {}), {2}: (13, {}), {3}: (14, {}),... | custom-call | flops 3623878656 | bytes 28311552 | tf_op jit(solution)/shard_map/while/body/eval_jaxpr/forward_step/pallas_call | solution.py:261
  106.6 19.5 %forward_step.7 = (f32[2,8,128,768]{3,2,1,0:T(8,128)}, f32[2,8,128,768]{3,2,1,0:T(8,128)}, bf16[2,8,128,768]{3,2,1,0:T(8,128)(2,1)}, bf16[2,8,128,2304]{3,2,1,0:...) custom-call(s32[4]{0:T(128)} %pad_add_fusion.5.flags, ...), custom_call_target="tpu_custom_call", output_to_operand_aliasing={{0}: (11, {}), {1}: (12, {}), {2}: (13, {}), {3}: (14, {}),... | custom-call | flops 3623878656 | bytes 28311552 | tf_op jit(solution)/shard_map/while/body/eval_jaxpr/forward_step/pallas_call | solution.py:261
  134.0 19.5 %forward_step.7 = (f32[2,8,128,768]{3,2,1,0:T(8,128)}, f32[2,8,128,768]{3,2,1,0:T(8,128)}, bf16[2,8,128,768]{3,2,1,0:T(8,128)(2,1)}, bf16[2,8,128,2304]{3,2,1,0:...) custom-call(s32[4]{0:T(128)} %pad_add_fusion.5.flags, ...), custom_call_target="tpu_custom_call", output_to_operand_aliasing={{0}: (11, {}), {1}: (12, {}), {2}: (13, {}), {3}: (14, {}),... | custom-call | flops 3623878656 | bytes 28311552 | tf_op jit(solution)/shard_map/while/body/eval_jaxpr/forward_step/pallas_call | solution.py:261
  161.4 19.5 %forward_step.7 = (f32[2,8,128,768]{3,2,1,0:T(8,128)}, f32[2,8,128,768]{3,2,1,0:T(8,128)}, bf16[2,8,128,768]{3,2,1,0:T(8,128)(2,1)}, bf16[2,8,128,2304]{3,2,1,0:...) custom-call(s32[4]{0:T(128)} %pad_add_fusion.5.flags, ...), custom_call_target="tpu_custom_call", output_to_operand_aliasing={{0}: (11, {}), {1}: (12, {}), {2}: (13, {}), {3}: (14, {}),... | custom-call | flops 3623878656 | bytes 28311552 | tf_op jit(solution)/shard_map/while/body/eval_jaxpr/forward_step/pallas_call | solution.py:261
  188.8 19.5 %forward_step.7 = (f32[2,8,128,768]{3,2,1,0:T(8,128)}, f32[2,8,128,768]{3,2,1,0:T(8,128)}, bf16[2,8,128,768]{3,2,1,0:T(8,128)(2,1)}, bf16[2,8,128,2304]{3,2,1,0:...) custom-call(s32[4]{0:T(128)} %pad_add_fusion.5.flags, ...), custom_call_target="tpu_custom_call", output_to_operand_aliasing={{0}: (11, {}), {1}: (12, {}), {2}: (13, {}), {3}: (14, {}),... | custom-call | flops 3623878656 | bytes 28311552 | tf_op jit(solution)/shard_map/while/body/eval_jaxpr/forward_step/pallas_call | solution.py:261
  216.2 19.5 %forward_step.7 = (f32[2,8,128,768]{3,2,1,0:T(8,128)}, f32[2,8,128,768]{3,2,1,0:T(8,128)}, bf16[2,8,128,768]{3,2,1,0:T(8,128)(2,1)}, bf16[2,8,128,2304]{3,2,1,0:...) custom-call(s32[4]{0:T(128)} %pad_add_fusion.5.flags, ...), custom_call_target="tpu_custom_call", output_to_operand_aliasing={{0}: (11, {}), {1}: (12, {}), {2}: (13, {}), {3}: (14, {}),... | custom-call | flops 3623878656 | bytes 28311552 | tf_op jit(solution)/shard_map/while/body/eval_jaxpr/forward_step/pallas_call | solution.py:261
  243.6 19.5 %forward_step.7 = (f32[2,8,128,768]{3,2,1,0:T(8,128)}, f32[2,8,128,768]{3,2,1,0:T(8,128)}, bf16[2,8,128,768]{3,2,1,0:T(8,128)(2,1)}, bf16[2,8,128,2304]{3,2,1,0:...) custom-call(s32[4]{0:T(128)} %pad_add_fusion.5.flags, ...), custom_call_target="tpu_custom_call", output_to_operand_aliasing={{0}: (11, {}), {1}: (12, {}), {2}: (13, {}), {3}: (14, {}),... | custom-call | flops 3623878656 | bytes 28311552 | tf_op jit(solution)/shard_map/while/body/eval_jaxpr/forward_step/pallas_call | solution.py:261
  295.2 16.9 %collective-permute-start = (f32[128,768]{1,0:T(8,128)}, f32[128,768]{1,0:T(8,128)}, u32[]{:S(2)}, u32[]{:S(2)}) collective-permute-start(f32[128,768]{1,0:T(8,128)} %copy.148), channel_id=1, source_target_pairs={{0,4},{4,8},{8,12},{12,16},{16,20},{20,24},{24,28},{1,5},{5,9},{9,... | collective-permute-start | bytes 1179656 | tf_op jit(solution)/shard_map/while/body/eval_jaxpr/ppermute | solution.py:626
  350.7 17.6 %collective-permute-start = (f32[128,768]{1,0:T(8,128)}, f32[128,768]{1,0:T(8,128)}, u32[]{:S(2)}, u32[]{:S(2)}) collective-permute-start(f32[128,768]{1,0:T(8,128)} %copy.148), channel_id=1, source_target_pairs={{0,4},{4,8},{8,12},{12,16},{16,20},{20,24},{24,28},{1,5},{5,9},{9,... | collective-permute-start | bytes 1179656 | tf_op jit(solution)/shard_map/while/body/eval_jaxpr/ppermute | solution.py:626
  405.9 15.1 %collective-permute-start = (f32[128,768]{1,0:T(8,128)}, f32[128,768]{1,0:T(8,128)}, u32[]{:S(2)}, u32[]{:S(2)}) collective-permute-start(f32[128,768]{1,0:T(8,128)} %copy.148), channel_id=1, source_target_pairs={{0,4},{4,8},{8,12},{12,16},{16,20},{20,24},{24,28},{1,5},{5,9},{9,... | collective-permute-start | bytes 1179656 | tf_op jit(solution)/shard_map/while/body/eval_jaxpr/ppermute | solution.py:626
  458.2 16.0 %collective-permute-start = (f32[128,768]{1,0:T(8,128)}, f32[128,768]{1,0:T(8,128)}, u32[]{:S(2)}, u32[]{:S(2)}) collective-permute-start(f32[128,768]{1,0:T(8,128)} %copy.148), channel_id=1, source_target_pairs={{0,4},{4,8},{8,12},{12,16},{16,20},{20,24},{24,28},{1,5},{5,9},{9,... | collective-permute-start | bytes 1179656 | tf_op jit(solution)/shard_map/while/body/eval_jaxpr/ppermute | solution.py:626
  509.6 729.4 %while.67 = (s32[]{:T(128)}, bf16[2,8,128,768]{3,2,1,0:T(8,128)(2,1)}, bf16[2,8,128,3072]{3,2,1,0:T(8,128)(2,1)}, bf16[2,8,128,768]{3,2,1,0:T(8,128)(2,1)}, bf16...) while((s32[]{:T(128)}, ...), condition=%wide.region_5.6_spmd.clone, body=%wide.region_4.5_spmd.clone.sunk | while | flops 3624271872 | bytes 32002436 | solution.py:647
  516.2 15.6 %collective-permute-done.1 = f32[128,768]{1,0:T(8,128)} collective-permute-done((f32[128,768]{1,0:T(8,128)}, f32[128,768]{1,0:T(8,128)}, u32[]{:S(2)}, u32[]{:S(2)}) %collective-permute-start.1) | collective-permute-done | bytes 393248 | tf_op jit(solution)/shard_map/while/body/eval_jaxpr/ppermute | solution.py:640
  567.3 17.0 %collective-permute-done.1 = f32[128,768]{1,0:T(8,128)} collective-permute-done((f32[128,768]{1,0:T(8,128)}, f32[128,768]{1,0:T(8,128)}, u32[]{:S(2)}, u32[]{:S(2)}) %collective-permute-start.1) | collective-permute-done | bytes 393248 | tf_op jit(solution)/shard_map/while/body/eval_jaxpr/ppermute | solution.py:640
  640.6 32.0 %collective-permute-done.1 = f32[128,768]{1,0:T(8,128)} collective-permute-done((f32[128,768]{1,0:T(8,128)}, f32[128,768]{1,0:T(8,128)}, u32[]{:S(2)}, u32[]{:S(2)}) %collective-permute-start.1) | collective-permute-done | bytes 393248 | tf_op jit(solution)/shard_map/while/body/eval_jaxpr/ppermute | solution.py:640
  679.9 31.9 %collective-permute-done.1 = f32[128,768]{1,0:T(8,128)} collective-permute-done((f32[128,768]{1,0:T(8,128)}, f32[128,768]{1,0:T(8,128)}, u32[]{:S(2)}, u32[]{:S(2)}) %collective-permute-start.1) | collective-permute-done | bytes 393248 | tf_op jit(solution)/shard_map/while/body/eval_jaxpr/ppermute | solution.py:640
  719.2 31.9 %collective-permute-done.1 = f32[128,768]{1,0:T(8,128)} collective-permute-done((f32[128,768]{1,0:T(8,128)}, f32[128,768]{1,0:T(8,128)}, u32[]{:S(2)}, u32[]{:S(2)}) %collective-permute-start.1) | collective-permute-done | bytes 393248 | tf_op jit(solution)/shard_map/while/body/eval_jaxpr/ppermute | solution.py:640
  758.4 31.9 %collective-permute-done.1 = f32[128,768]{1,0:T(8,128)} collective-permute-done((f32[128,768]{1,0:T(8,128)}, f32[128,768]{1,0:T(8,128)}, u32[]{:S(2)}, u32[]{:S(2)}) %collective-permute-start.1) | collective-permute-done | bytes 393248 | tf_op jit(solution)/shard_map/while/body/eval_jaxpr/ppermute | solution.py:640
  797.7 31.9 %collective-permute-done.1 = f32[128,768]{1,0:T(8,128)} collective-permute-done((f32[128,768]{1,0:T(8,128)}, f32[128,768]{1,0:T(8,128)}, u32[]{:S(2)}, u32[]{:S(2)}) %collective-permute-start.1) | collective-permute-done | bytes 393248 | tf_op jit(solution)/shard_map/while/body/eval_jaxpr/ppermute | solution.py:640
  836.9 31.9 %collective-permute-done.1 = f32[128,768]{1,0:T(8,128)} collective-permute-done((f32[128,768]{1,0:T(8,128)}, f32[128,768]{1,0:T(8,128)}, u32[]{:S(2)}, u32[]{:S(2)}) %collective-permute-start.1) | collective-permute-done | bytes 393248 | tf_op jit(solution)/shard_map/while/body/eval_jaxpr/ppermute | solution.py:640
  876.2 31.9 %collective-permute-done.1 = f32[128,768]{1,0:T(8,128)} collective-permute-done((f32[128,768]{1,0:T(8,128)}, f32[128,768]{1,0:T(8,128)}, u32[]{:S(2)}, u32[]{:S(2)}) %collective-permute-start.1) | collective-permute-done | bytes 393248 | tf_op jit(solution)/shard_map/while/body/eval_jaxpr/ppermute | solution.py:640
  914.5 32.4 %backward_step.7 = (bf16[2,8,128,768]{3,2,1,0:T(8,128)(2,1)}, bf16[2,8,128,3072]{3,2,1,0:T(8,128)(2,1)}, bf16[2,8,128,768]{3,2,1,0:T(8,128)(2,1)}, bf16[2,8,128,...) custom-call(s32[4]{0:T(128)} %pad_add_fusion.6.flags, ...), custom_call_target="tpu_custom_call", output_to_operand_aliasing={{0}: (13, {}), {1}: (14, {}), {2}: (15, {}), {3}: (16, {}),... | custom-call | flops 3623878656 | bytes 28311552 | tf_op jit(solution)/shard_map/while/body/eval_jaxpr/backward_step/pallas_call | solution.py:481
  953.7 32.3 %backward_step.7 = (bf16[2,8,128,768]{3,2,1,0:T(8,128)(2,1)}, bf16[2,8,128,3072]{3,2,1,0:T(8,128)(2,1)}, bf16[2,8,128,768]{3,2,1,0:T(8,128)(2,1)}, bf16[2,8,128,...) custom-call(s32[4]{0:T(128)} %pad_add_fusion.6.flags, ...), custom_call_target="tpu_custom_call", output_to_operand_aliasing={{0}: (13, {}), {1}: (14, {}), {2}: (15, {}), {3}: (16, {}),... | custom-call | flops 3623878656 | bytes 28311552 | tf_op jit(solution)/shard_map/while/body/eval_jaxpr/backward_step/pallas_call | solution.py:481
  992.9 32.2 %backward_step.7 = (bf16[2,8,128,768]{3,2,1,0:T(8,128)(2,1)}, bf16[2,8,128,3072]{3,2,1,0:T(8,128)(2,1)}, bf16[2,8,128,768]{3,2,1,0:T(8,128)(2,1)}, bf16[2,8,128,...) custom-call(s32[4]{0:T(128)} %pad_add_fusion.6.flags, ...), custom_call_target="tpu_custom_call", output_to_operand_aliasing={{0}: (13, {}), {1}: (14, {}), {2}: (15, {}), {3}: (16, {}),... | custom-call | flops 3623878656 | bytes 28311552 | tf_op jit(solution)/shard_map/while/body/eval_jaxpr/backward_step/pallas_call | solution.py:481
  1032.1 32.2 %backward_step.7 = (bf16[2,8,128,768]{3,2,1,0:T(8,128)(2,1)}, bf16[2,8,128,3072]{3,2,1,0:T(8,128)(2,1)}, bf16[2,8,128,768]{3,2,1,0:T(8,128)(2,1)}, bf16[2,8,128,...) custom-call(s32[4]{0:T(128)} %pad_add_fusion.6.flags, ...), custom_call_target="tpu_custom_call", output_to_operand_aliasing={{0}: (13, {}), {1}: (14, {}), {2}: (15, {}), {3}: (16, {}),... | custom-call | flops 3623878656 | bytes 28311552 | tf_op jit(solution)/shard_map/while/body/eval_jaxpr/backward_step/pallas_call | solution.py:481
  1071.4 32.3 %backward_step.7 = (bf16[2,8,128,768]{3,2,1,0:T(8,128)(2,1)}, bf16[2,8,128,3072]{3,2,1,0:T(8,128)(2,1)}, bf16[2,8,128,768]{3,2,1,0:T(8,128)(2,1)}, bf16[2,8,128,...) custom-call(s32[4]{0:T(128)} %pad_add_fusion.6.flags, ...), custom_call_target="tpu_custom_call", output_to_operand_aliasing={{0}: (13, {}), {1}: (14, {}), {2}: (15, {}), {3}: (16, {}),... | custom-call | flops 3623878656 | bytes 28311552 | tf_op jit(solution)/shard_map/while/body/eval_jaxpr/backward_step/pallas_call | solution.py:481
  1112.1 32.3 %backward_step.7 = (bf16[2,8,128,768]{3,2,1,0:T(8,128)(2,1)}, bf16[2,8,128,3072]{3,2,1,0:T(8,128)(2,1)}, bf16[2,8,128,768]{3,2,1,0:T(8,128)(2,1)}, bf16[2,8,128,...) custom-call(s32[4]{0:T(128)} %pad_add_fusion.6.flags, ...), custom_call_target="tpu_custom_call", output_to_operand_aliasing={{0}: (13, {}), {1}: (14, {}), {2}: (15, {}), {3}: (16, {}),... | custom-call | flops 3623878656 | bytes 28311552 | tf_op jit(solution)/shard_map/while/body/eval_jaxpr/backward_step/pallas_call | solution.py:481
  1155.0 32.2 %backward_step.7 = (bf16[2,8,128,768]{3,2,1,0:T(8,128)(2,1)}, bf16[2,8,128,3072]{3,2,1,0:T(8,128)(2,1)}, bf16[2,8,128,768]{3,2,1,0:T(8,128)(2,1)}, bf16[2,8,128,...) custom-call(s32[4]{0:T(128)} %pad_add_fusion.6.flags, ...), custom_call_target="tpu_custom_call", output_to_operand_aliasing={{0}: (13, {}), {1}: (14, {}), {2}: (15, {}), {3}: (16, {}),... | custom-call | flops 3623878656 | bytes 28311552 | tf_op jit(solution)/shard_map/while/body/eval_jaxpr/backward_step/pallas_call | solution.py:481
  1194.2 32.3 %backward_step.7 = (bf16[2,8,128,768]{3,2,1,0:T(8,128)(2,1)}, bf16[2,8,128,3072]{3,2,1,0:T(8,128)(2,1)}, bf16[2,8,128,768]{3,2,1,0:T(8,128)(2,1)}, bf16[2,8,128,...) custom-call(s32[4]{0:T(128)} %pad_add_fusion.6.flags, ...), custom_call_target="tpu_custom_call", output_to_operand_aliasing={{0}: (13, {}), {1}: (14, {}), {2}: (15, {}), {3}: (16, {}),... | custom-call | flops 3623878656 | bytes 28311552 | tf_op jit(solution)/shard_map/while/body/eval_jaxpr/backward_step/pallas_call | solution.py:481
  (435 shorter events, 584.0 us)
Async XLA Ops:
  3.2 40.3 %collective-permute-start.2 = (f32[4,128,768]{2,1,0:T(8,128)S(1)}, f32[4,128,768]{2,1,0:T(8,128)}, u32[]{:S(2)}, u32[]{:S(2)}) collective-permute-start(f32[4,128,768]{2,1,0:T(8,128)S(1)} %fusion.6), channel_id=1, source_target_pairs={{2,0},{3,1},{0,2},{1,3},{30,28},{31,29},{28,30},{29,31}} | collective-permute-start | bytes 4718600 | tf_op jit(solution)/shard_map/ppermute | solution.py:557
  8.1 34.5 %collective-permute-start.3 = (s32[4,4]{1,0:T(4,128)S(1)}, s32[4,4]{1,0:T(4,128)S(1)}, u32[]{:S(2)}, u32[]{:S(2)}) collective-permute-start(s32[4,4]{1,0:T(4,128)S(1)} %bitcast.97), channel_id=1, source_target_pairs={{2,0},{3,1},{0,2},{1,3},{6,4},{7,5},{4,6},{5,7},{10,8},{11,9},{8,1... | collective-permute-start | bytes 200 | tf_op jit(solution)/shard_map/ppermute | solution.py:555
  47.5 23.8 %collective-permute-start = (f32[128,768]{1,0:T(8,128)}, f32[128,768]{1,0:T(8,128)}, u32[]{:S(2)}, u32[]{:S(2)}) collective-permute-start(f32[128,768]{1,0:T(8,128)} %copy.148), channel_id=1, source_target_pairs={{0,4},{4,8},{8,12},{12,16},{16,20},{20,24},{24,28},{1,5},{5,9},{9,... | collective-permute-start | bytes 1179656 | tf_op jit(solution)/shard_map/while/body/eval_jaxpr/ppermute | solution.py:626
  74.8 23.9 %collective-permute-start = (f32[128,768]{1,0:T(8,128)}, f32[128,768]{1,0:T(8,128)}, u32[]{:S(2)}, u32[]{:S(2)}) collective-permute-start(f32[128,768]{1,0:T(8,128)} %copy.148), channel_id=1, source_target_pairs={{0,4},{4,8},{8,12},{12,16},{16,20},{20,24},{24,28},{1,5},{5,9},{9,... | collective-permute-start | bytes 1179656 | tf_op jit(solution)/shard_map/while/body/eval_jaxpr/ppermute | solution.py:626
  102.2 23.9 %collective-permute-start = (f32[128,768]{1,0:T(8,128)}, f32[128,768]{1,0:T(8,128)}, u32[]{:S(2)}, u32[]{:S(2)}) collective-permute-start(f32[128,768]{1,0:T(8,128)} %copy.148), channel_id=1, source_target_pairs={{0,4},{4,8},{8,12},{12,16},{16,20},{20,24},{24,28},{1,5},{5,9},{9,... | collective-permute-start | bytes 1179656 | tf_op jit(solution)/shard_map/while/body/eval_jaxpr/ppermute | solution.py:626
  129.6 23.9 %collective-permute-start = (f32[128,768]{1,0:T(8,128)}, f32[128,768]{1,0:T(8,128)}, u32[]{:S(2)}, u32[]{:S(2)}) collective-permute-start(f32[128,768]{1,0:T(8,128)} %copy.148), channel_id=1, source_target_pairs={{0,4},{4,8},{8,12},{12,16},{16,20},{20,24},{24,28},{1,5},{5,9},{9,... | collective-permute-start | bytes 1179656 | tf_op jit(solution)/shard_map/while/body/eval_jaxpr/ppermute | solution.py:626
  157.0 23.9 %collective-permute-start = (f32[128,768]{1,0:T(8,128)}, f32[128,768]{1,0:T(8,128)}, u32[]{:S(2)}, u32[]{:S(2)}) collective-permute-start(f32[128,768]{1,0:T(8,128)} %copy.148), channel_id=1, source_target_pairs={{0,4},{4,8},{8,12},{12,16},{16,20},{20,24},{24,28},{1,5},{5,9},{9,... | collective-permute-start | bytes 1179656 | tf_op jit(solution)/shard_map/while/body/eval_jaxpr/ppermute | solution.py:626
  184.4 23.9 %collective-permute-start = (f32[128,768]{1,0:T(8,128)}, f32[128,768]{1,0:T(8,128)}, u32[]{:S(2)}, u32[]{:S(2)}) collective-permute-start(f32[128,768]{1,0:T(8,128)} %copy.148), channel_id=1, source_target_pairs={{0,4},{4,8},{8,12},{12,16},{16,20},{20,24},{24,28},{1,5},{5,9},{9,... | collective-permute-start | bytes 1179656 | tf_op jit(solution)/shard_map/while/body/eval_jaxpr/ppermute | solution.py:626
  211.8 23.9 %collective-permute-start = (f32[128,768]{1,0:T(8,128)}, f32[128,768]{1,0:T(8,128)}, u32[]{:S(2)}, u32[]{:S(2)}) collective-permute-start(f32[128,768]{1,0:T(8,128)} %copy.148), channel_id=1, source_target_pairs={{0,4},{4,8},{8,12},{12,16},{16,20},{20,24},{24,28},{1,5},{5,9},{9,... | collective-permute-start | bytes 1179656 | tf_op jit(solution)/shard_map/while/body/eval_jaxpr/ppermute | solution.py:626
  239.2 23.9 %collective-permute-start = (f32[128,768]{1,0:T(8,128)}, f32[128,768]{1,0:T(8,128)}, u32[]{:S(2)}, u32[]{:S(2)}) collective-permute-start(f32[128,768]{1,0:T(8,128)} %copy.148), channel_id=1, source_target_pairs={{0,4},{4,8},{8,12},{12,16},{16,20},{20,24},{24,28},{1,5},{5,9},{9,... | collective-permute-start | bytes 1179656 | tf_op jit(solution)/shard_map/while/body/eval_jaxpr/ppermute | solution.py:626
  295.2 23.7 %collective-permute-start = (f32[128,768]{1,0:T(8,128)}, f32[128,768]{1,0:T(8,128)}, u32[]{:S(2)}, u32[]{:S(2)}) collective-permute-start(f32[128,768]{1,0:T(8,128)} %copy.148), channel_id=1, source_target_pairs={{0,4},{4,8},{8,12},{12,16},{16,20},{20,24},{24,28},{1,5},{5,9},{9,... | collective-permute-start | bytes 1179656 | tf_op jit(solution)/shard_map/while/body/eval_jaxpr/ppermute | solution.py:626
  350.7 22.9 %collective-permute-start = (f32[128,768]{1,0:T(8,128)}, f32[128,768]{1,0:T(8,128)}, u32[]{:S(2)}, u32[]{:S(2)}) collective-permute-start(f32[128,768]{1,0:T(8,128)} %copy.148), channel_id=1, source_target_pairs={{0,4},{4,8},{8,12},{12,16},{16,20},{20,24},{24,28},{1,5},{5,9},{9,... | collective-permute-start | bytes 1179656 | tf_op jit(solution)/shard_map/while/body/eval_jaxpr/ppermute | solution.py:626
  562.7 21.5 %collective-permute-start.1 = (f32[128,768]{1,0:T(8,128)}, f32[128,768]{1,0:T(8,128)}, u32[]{:S(2)}, u32[]{:S(2)}) collective-permute-start(f32[128,768]{1,0:T(8,128)} %copy.178), channel_id=1, source_target_pairs={{4,0},{8,4},{12,8},{16,12},{20,16},{24,20},{28,24},{5,1},{9,5},{13... | collective-permute-start | bytes 1179656 | tf_op jit(solution)/shard_map/while/body/eval_jaxpr/ppermute | solution.py:640
  636.0 36.6 %collective-permute-start.1 = (f32[128,768]{1,0:T(8,128)}, f32[128,768]{1,0:T(8,128)}, u32[]{:S(2)}, u32[]{:S(2)}) collective-permute-start(f32[128,768]{1,0:T(8,128)} %copy.178), channel_id=1, source_target_pairs={{4,0},{8,4},{12,8},{16,12},{20,16},{24,20},{28,24},{5,1},{9,5},{13... | collective-permute-start | bytes 1179656 | tf_op jit(solution)/shard_map/while/body/eval_jaxpr/ppermute | solution.py:640
  675.3 36.5 %collective-permute-start.1 = (f32[128,768]{1,0:T(8,128)}, f32[128,768]{1,0:T(8,128)}, u32[]{:S(2)}, u32[]{:S(2)}) collective-permute-start(f32[128,768]{1,0:T(8,128)} %copy.178), channel_id=1, source_target_pairs={{4,0},{8,4},{12,8},{16,12},{20,16},{24,20},{28,24},{5,1},{9,5},{13... | collective-permute-start | bytes 1179656 | tf_op jit(solution)/shard_map/while/body/eval_jaxpr/ppermute | solution.py:640
  714.6 36.5 %collective-permute-start.1 = (f32[128,768]{1,0:T(8,128)}, f32[128,768]{1,0:T(8,128)}, u32[]{:S(2)}, u32[]{:S(2)}) collective-permute-start(f32[128,768]{1,0:T(8,128)} %copy.178), channel_id=1, source_target_pairs={{4,0},{8,4},{12,8},{16,12},{20,16},{24,20},{28,24},{5,1},{9,5},{13... | collective-permute-start | bytes 1179656 | tf_op jit(solution)/shard_map/while/body/eval_jaxpr/ppermute | solution.py:640
  753.8 36.5 %collective-permute-start.1 = (f32[128,768]{1,0:T(8,128)}, f32[128,768]{1,0:T(8,128)}, u32[]{:S(2)}, u32[]{:S(2)}) collective-permute-start(f32[128,768]{1,0:T(8,128)} %copy.178), channel_id=1, source_target_pairs={{4,0},{8,4},{12,8},{16,12},{20,16},{24,20},{28,24},{5,1},{9,5},{13... | collective-permute-start | bytes 1179656 | tf_op jit(solution)/shard_map/while/body/eval_jaxpr/ppermute | solution.py:640
  793.1 36.5 %collective-permute-start.1 = (f32[128,768]{1,0:T(8,128)}, f32[128,768]{1,0:T(8,128)}, u32[]{:S(2)}, u32[]{:S(2)}) collective-permute-start(f32[128,768]{1,0:T(8,128)} %copy.178), channel_id=1, source_target_pairs={{4,0},{8,4},{12,8},{16,12},{20,16},{24,20},{28,24},{5,1},{9,5},{13... | collective-permute-start | bytes 1179656 | tf_op jit(solution)/shard_map/while/body/eval_jaxpr/ppermute | solution.py:640
  832.4 36.5 %collective-permute-start.1 = (f32[128,768]{1,0:T(8,128)}, f32[128,768]{1,0:T(8,128)}, u32[]{:S(2)}, u32[]{:S(2)}) collective-permute-start(f32[128,768]{1,0:T(8,128)} %copy.178), channel_id=1, source_target_pairs={{4,0},{8,4},{12,8},{16,12},{20,16},{24,20},{28,24},{5,1},{9,5},{13... | collective-permute-start | bytes 1179656 | tf_op jit(solution)/shard_map/while/body/eval_jaxpr/ppermute | solution.py:640
  871.6 36.5 %collective-permute-start.1 = (f32[128,768]{1,0:T(8,128)}, f32[128,768]{1,0:T(8,128)}, u32[]{:S(2)}, u32[]{:S(2)}) collective-permute-start(f32[128,768]{1,0:T(8,128)} %copy.178), channel_id=1, source_target_pairs={{4,0},{8,4},{12,8},{16,12},{20,16},{24,20},{28,24},{5,1},{9,5},{13... | collective-permute-start | bytes 1179656 | tf_op jit(solution)/shard_map/while/body/eval_jaxpr/ppermute | solution.py:640
  910.9 36.4 %collective-permute-start.1 = (f32[128,768]{1,0:T(8,128)}, f32[128,768]{1,0:T(8,128)}, u32[]{:S(2)}, u32[]{:S(2)}) collective-permute-start(f32[128,768]{1,0:T(8,128)} %copy.178), channel_id=1, source_target_pairs={{4,0},{8,4},{12,8},{16,12},{20,16},{24,20},{28,24},{5,1},{9,5},{13... | collective-permute-start | bytes 1179656 | tf_op jit(solution)/shard_map/while/body/eval_jaxpr/ppermute | solution.py:640
  950.1 36.4 %collective-permute-start.1 = (f32[128,768]{1,0:T(8,128)}, f32[128,768]{1,0:T(8,128)}, u32[]{:S(2)}, u32[]{:S(2)}) collective-permute-start(f32[128,768]{1,0:T(8,128)} %copy.178), channel_id=1, source_target_pairs={{4,0},{8,4},{12,8},{16,12},{20,16},{24,20},{28,24},{5,1},{9,5},{13... | collective-permute-start | bytes 1179656 | tf_op jit(solution)/shard_map/while/body/eval_jaxpr/ppermute | solution.py:640
  989.2 36.5 %collective-permute-start.1 = (f32[128,768]{1,0:T(8,128)}, f32[128,768]{1,0:T(8,128)}, u32[]{:S(2)}, u32[]{:S(2)}) collective-permute-start(f32[128,768]{1,0:T(8,128)} %copy.178), channel_id=1, source_target_pairs={{4,0},{8,4},{12,8},{16,12},{20,16},{24,20},{28,24},{5,1},{9,5},{13... | collective-permute-start | bytes 1179656 | tf_op jit(solution)/shard_map/while/body/eval_jaxpr/ppermute | solution.py:640
  1028.4 36.6 %collective-permute-start.1 = (f32[128,768]{1,0:T(8,128)}, f32[128,768]{1,0:T(8,128)}, u32[]{:S(2)}, u32[]{:S(2)}) collective-permute-start(f32[128,768]{1,0:T(8,128)} %copy.178), channel_id=1, source_target_pairs={{4,0},{8,4},{12,8},{16,12},{20,16},{24,20},{28,24},{5,1},{9,5},{13... | collective-permute-start | bytes 1179656 | tf_op jit(solution)/shard_map/while/body/eval_jaxpr/ppermute | solution.py:640
  1067.8 37.9 %collective-permute-start.1 = (f32[128,768]{1,0:T(8,128)}, f32[128,768]{1,0:T(8,128)}, u32[]{:S(2)}, u32[]{:S(2)}) collective-permute-start(f32[128,768]{1,0:T(8,128)} %copy.178), channel_id=1, source_target_pairs={{4,0},{8,4},{12,8},{16,12},{20,16},{24,20},{28,24},{5,1},{9,5},{13... | collective-permute-start | bytes 1179656 | tf_op jit(solution)/shard_map/while/body/eval_jaxpr/ppermute | solution.py:640
  1108.4 40.1 %collective-permute-start.1 = (f32[128,768]{1,0:T(8,128)}, f32[128,768]{1,0:T(8,128)}, u32[]{:S(2)}, u32[]{:S(2)}) collective-permute-start(f32[128,768]{1,0:T(8,128)} %copy.178), channel_id=1, source_target_pairs={{4,0},{8,4},{12,8},{16,12},{20,16},{24,20},{28,24},{5,1},{9,5},{13... | collective-permute-start | bytes 1179656 | tf_op jit(solution)/shard_map/while/body/eval_jaxpr/ppermute | solution.py:640
  1151.3 36.5 %collective-permute-start.1 = (f32[128,768]{1,0:T(8,128)}, f32[128,768]{1,0:T(8,128)}, u32[]{:S(2)}, u32[]{:S(2)}) collective-permute-start(f32[128,768]{1,0:T(8,128)} %copy.178), channel_id=1, source_target_pairs={{4,0},{8,4},{12,8},{16,12},{20,16},{24,20},{28,24},{5,1},{9,5},{13... | collective-permute-start | bytes 1179656 | tf_op jit(solution)/shard_map/while/body/eval_jaxpr/ppermute | solution.py:640
  1190.6 35.9 %collective-permute-start.1 = (f32[128,768]{1,0:T(8,128)}, f32[128,768]{1,0:T(8,128)}, u32[]{:S(2)}, u32[]{:S(2)}) collective-permute-start(f32[128,768]{1,0:T(8,128)} %copy.178), channel_id=1, source_target_pairs={{4,0},{8,4},{12,8},{16,12},{20,16},{24,20},{28,24},{5,1},{9,5},{13... | collective-permute-start | bytes 1179656 | tf_op jit(solution)/shard_map/while/body/eval_jaxpr/ppermute | solution.py:640
  1254.5 104.9 %collective-permute-start.15 = (f32[2,768,768]{2,1,0:T(8,128)}, f32[2,768,768]{2,1,0:T(8,128)}, u32[]{:S(2)}, u32[]{:S(2)}) collective-permute-start(f32[2,768,768]{2,1,0:T(8,128)} %constant_dynamic-slice_fusion), channel_id=1, source_target_pairs={{0,1},{1,0},{2,3},{3,2},{4,5},{5,4},{6,7},{7,6},{8,9},{9,8},{10,11... | collective-permute-start | bytes 14155784 | tf_op jit(solution)/shard_map/ppermute | solution.py:660
  1267.3 84.8 %collective-permute-start.14 = (f32[2,192,3072]{2,1,0:T(8,128)}, f32[2,192,3072]{2,1,0:T(8,128)}, u32[]{:S(2)}, u32[]{:S(2)}) collective-permute-start(f32[2,192,3072]{2,1,0:T(8,128)} %constant_dynamic-slice_fusion.1), channel_id=1, source_target_pairs={{0,1},{1,0},{2,3},{3,2},{4,5},{5,4},{6,7},{7,6},{8,9},{9,8},{10,11... | collective-permute-start | bytes 14155784 | tf_op jit(solution)/shard_map/ppermute | solution.py:660
  1276.7 70.0 %collective-permute-start.12 = (f32[2,192,2304]{2,1,0:T(8,128)}, f32[2,192,2304]{2,1,0:T(8,128)}, u32[]{:S(2)}, u32[]{:S(2)}) collective-permute-start(f32[2,192,2304]{2,1,0:T(8,128)} %constant_dynamic-slice_fusion.3), channel_id=1, source_target_pairs={{0,1},{1,0},{2,3},{3,2},{4,5},{5,4},{6,7},{7,6},{8,9},{9,8},{10,11... | collective-permute-start | bytes 10616840 | tf_op jit(solution)/shard_map/ppermute | solution.py:660
  1282.4 61.8 %collective-permute-start.13 = (f32[2,192,768]{2,1,0:T(8,128)S(1)}, f32[2,192,768]{2,1,0:T(8,128)}, u32[]{:S(2)}, u32[]{:S(2)}) collective-permute-start(f32[2,192,768]{2,1,0:T(8,128)S(1)} %constant_dynamic-slice_fusion.2), channel_id=1, source_target_pairs={{0,1},{1,0},{2,3},{3,2},{4,5},{5,4},{6,7},{7,6},{8,9},{9,8},{10,11... | collective-permute-start | bytes 3538952 | tf_op jit(solution)/shard_map/ppermute | solution.py:660
  (55 other events, 639.7 us)

commit v2 on v1

--- a/solution.py
+++ b/solution.py
@@ -10,11 +10,14 @@
 HEAD_DIM = 64
 LAYERS = 2
 PAIR = 2 * HEAD_DIM
-CHUNK = 768
+SCOPED = 10368 * 1024
 EPS = 1e-05
 BF16 = jnp.bfloat16
 F32 = jnp.float32
 ANY = pl.BlockSpec(memory_space=pl.ANY)
+VMEM = pl.BlockSpec(memory_space=pltpu.VMEM)
+HBM = pl.BlockSpec(memory_space=pltpu.HBM)
+UNROLL = 22
 SMEM = pl.BlockSpec(memory_space=pltpu.SMEM)
 TANH_SCALE = 0.7978845608028654
 
@@ -70,106 +73,104 @@
     return jnp.sum(values.astype(F32), axis=0, keepdims=True)
 
 
-def forward_kernel(
-    branch_scale,
-    flags,
-    tokens,
-    arrived,
-    allowed_rows,
-    wj,
-    wo,
-    we,
-    wc,
-    vecs,
-    bj,
-    be,
-    *refs,
-):
+def weight_blocks(weights):
+    width = weights[1].shape[-1]
+    return [
+        (index, row, column)
+        for index, weight in enumerate(weights)
+        for row in range(0, weight.shape[1], width)
+        for column in range(0, weight.shape[2], width)
+    ]
+
+
+def load_kernel(blocks, width, *refs):
+    weights, targets, sems = refs[:4], refs[4:-1], refs[-1]
+    copies = [
+        pltpu.make_async_copy(
+            weights[index].at[:, row : row + width, column : column + width],
+            target,
+            sems.at[at],
+        )
+        for at, ((index, row, column), target) in enumerate(zip(blocks, targets))
+    ]
+    for copy in copies:
+        copy.start()
+    for copy in copies:
+        copy.wait()
+
+
+def load_weights(weights):
+    width = weights[1].shape[-1]
+    blocks = weight_blocks(weights)
+    return pl.pallas_call(
+        partial(load_kernel, blocks, width),
+        out_shape=tuple(pltpu.VMEM((LAYERS, width, width), BF16) for _ in blocks),
+        in_specs=[ANY] * 4,
+        out_specs=tuple([VMEM] * len(blocks)),
+        scratch_shapes=[pltpu.SemaphoreType.DMA((len(blocks),))],
+        compiler_params=pltpu.CompilerParams(vmem_limit_bytes=SCOPED),
+        name="load_weights",
+    )(*map(in_hbm, weights))
+
+
+def in_hbm(value):
+    return pltpu.with_memory_space_constraint(value, pltpu.HBM)
+
+
+def layer_loop(body):
+    lax.fori_loop(0, LAYERS, lambda index, carry: (body(index), carry)[1], 0)
+
+
+def forward_kernel(branch_scale, joint_count, hidden_count, tick, tokens, arrived, allowed_rows, *refs):
+    weight_count = joint_count + 1 + 2 * hidden_count
+    wj = refs[:joint_count]
+    wo = refs[joint_count]
+    we = refs[joint_count + 1 : joint_count + 1 + hidden_count]
+    wc = refs[joint_count + 1 + hidden_count : weight_count]
+    vecs, bj, be = refs[weight_count : weight_count + 3]
+    refs = refs[weight_count + 3 :]
     names = ("h", "g", "a", "t", "o", "c", "m", "d", "f")
     stash = dict(zip(names, refs[9:18]))
-    sent = refs[18]
-    (
-        wj_v,
-        wo_v,
-        we_v,
-        wc_v,
-        vecs_v,
-        bj_v,
-        be_v,
-        allow_v,
-        h_v,
-        g_v,
-        a_v,
-        t_v,
-        o_v,
-        c_v,
-        m_v,
-        d_v,
-        w_sem,
-        in_sem,
-        out_sem,
-    ) = refs[19:]
-    active, slot, first, last = flags[0], flags[1], flags[2], flags[3]
-    feature = h_v.shape[-1]
-    hidden = we_v.shape[-1]
-
-    @pl.when(active == 1)
+    sent, next_tick = refs[18:20]
+    h_v, g_v, a_v, t_v, o_v, c_v, m_v, d_v, in_sem, out_sem = refs[20:]
+    next_tick[0] = tick[0] + 1
+    section = lax.axis_index("section")
+    last = section == lax.axis_size("section") - 1
+    feature = tokens.shape[-1]
+    rows = allowed_rows.shape[0]
+    row_index = tick[0] - 2 * section
+
+    @pl.when((row_index >= 0) & (row_index < rows))
     def _():
-        small = [
-            pltpu.make_async_copy(allowed_rows.at[slot], allow_v, in_sem.at[1]),
-            pltpu.make_async_copy(vecs, vecs_v, in_sem.at[2]),
-            pltpu.make_async_copy(bj, bj_v, in_sem.at[3]),
-            pltpu.make_async_copy(be, be_v, in_sem.at[4]),
-        ]
-
-        @pl.when(first == 1)
+        slot = jnp.clip(row_index, 0, rows - 1)
+
+        @pl.when(section == 0)
         def _():
-            pltpu.make_async_copy(tokens.at[slot], h_v.at[0], in_sem.at[0]).start()
-
-        @pl.when(first == 0)
+            pltpu.make_async_copy(tokens.at[lax.rem(slot, tokens.shape[0])], h_v.at[0], in_sem.at[0]).start()
+
+        @pl.when(section > 0)
         def _():
             pltpu.make_async_copy(arrived, h_v.at[0], in_sem.at[0]).start()
-
-        for copy in small:
-            copy.start()
-        sources = ((wj, wj_v), (wo, wo_v), (we, we_v), (wc, wc_v))
-        for layer in range(LAYERS):
-            for index, (source, target) in enumerate(sources):
-                pltpu.make_async_copy(
-                    source.at[layer], target.at[layer], w_sem.at[layer, index]
-                ).start()
-
-        def weight_wait(layer, index):
-            source, target = sources[index]
-            pltpu.make_async_copy(
-                source.at[layer], target.at[layer], w_sem.at[layer, index]
-            ).wait()
 
         def put(layer, index, name, value_ref):
             return pltpu.make_async_copy(
                 value_ref.at[layer], stash[name].at[layer, slot], out_sem.at[layer, index]
             )
 
+        allowed = jnp.concatenate([allowed_rows[slot], allowed_rows[slot]], axis=0) > 0.5
         pltpu.make_async_copy(arrived, h_v.at[0], in_sem.at[0]).wait()
-        for copy in small:
-            copy.wait()
-        allowed = allow_v[...] > 0.5
-        allowed = jnp.concatenate([allow_v[...], allow_v[...]], axis=0) > 0.5
-
-        for layer in range(LAYERS):
+
+        def one_layer(layer):
             put(layer, 0, "h", h_v).start()
             row = h_v[layer]
             normed, _ = norm_parts(row)
-            a_low = (
-                normed * vecs_v[layer, 0:1, :] + vecs_v[layer, 1:2, :]
-            ).astype(BF16)
+            a_low = (normed * vecs[layer, 0:1, :] + vecs[layer, 1:2, :]).astype(BF16)
             a_v[layer] = a_low
             put(layer, 2, "a", a_v).start()
-            weight_wait(layer, 0)
-            for start in range(0, 3 * feature, CHUNK):
-                span = slice(start, start + CHUNK)
+            for index in range(joint_count):
+                span = slice(index * feature, (index + 1) * feature)
                 t_v[layer, :, span] = (
-                    mm(a_low, wj_v[layer, :, span]) + bj_v[layer, :, span]
+                    mm(a_low, wj[index][layer]) + bj[layer, :, span]
                 ).astype(BF16)
             put(layer, 3, "t", t_v).start()
             for start in range(0, feature, PAIR):
@@ -179,18 +180,16 @@
                 chances = pair_probabilities(queries, keys, allowed).astype(BF16)
                 o_v[layer, :, start : start + PAIR] = join_halves(mm(chances, values)).astype(BF16)
             put(layer, 4, "o", o_v).start()
-            weight_wait(layer, 1)
-            mixed = row + branch_scale * (mm(o_v[layer], wo_v[layer]) + vecs_v[layer, 2:3, :])
+            mixed = row + branch_scale * (mm(o_v[layer], wo[layer]) + vecs[layer, 2:3, :])
             g_v[layer] = mixed
             put(layer, 1, "g", g_v).start()
             normed, _ = norm_parts(mixed)
-            c_low = (normed * vecs_v[layer, 3:4, :] + vecs_v[layer, 4:5, :]).astype(BF16)
+            c_low = (normed * vecs[layer, 3:4, :] + vecs[layer, 4:5, :]).astype(BF16)
             c_v[layer] = c_low
             put(layer, 5, "c", c_v).start()
-            weight_wait(layer, 2)
-            for start in range(0, hidden, CHUNK):
-                span = slice(start, start + CHUNK)
-                u = mm(c_low, we_v[layer, :, span]) + be_v[layer, :, span]
+            for index in range(hidden_count):
+                span = slice(index * feature, (index + 1) * feature)
+                u = mm(c_low, we[index][layer]) + be[layer, :, span]
                 square = u * u
                 th = jnp.tanh(TANH_SCALE * (u + 0.044715 * (square * u)))
                 half = 0.5 * (1.0 + th)
@@ -201,13 +200,16 @@
                 d_v[layer, :, span] = slope.astype(BF16)
             put(layer, 6, "m", m_v).start()
             put(layer, 7, "d", d_v).start()
-            weight_wait(layer, 3)
-            output = mixed + branch_scale * (mm(m_v[layer], wc_v[layer]) + vecs_v[layer, 5:6, :])
-            h_v[layer + 1] = output
-        out = pltpu.make_async_copy(h_v.at[LAYERS], sent, in_sem.at[0])
-        out.start()
-
-        @pl.when(last == 1)
+            z = vecs[layer, 5:6, :]
+            for index in range(hidden_count):
+                span = slice(index * feature, (index + 1) * feature)
+                z = z + mm(m_v[layer, :, span], wc[index][layer])
+            h_v[layer + 1] = mixed + branch_scale * z
+
+        layer_loop(one_layer)
+        sent[...] = h_v[LAYERS]
+
+        @pl.when(last)
         def _():
             final = pltpu.make_async_copy(h_v.at[LAYERS], stash["f"].at[slot], in_sem.at[1])
             final.start()
@@ -227,24 +229,27 @@
                 )
             ):
                 put(layer, index, name, value_ref).wait()
-        out.wait()
-
-
-def forward_step(branch_scale, flags, tokens, arrived, allowed, weights, vectors, stash):
+
+
+def counts_of(weights, feature):
+    hidden_count = (len(weights) - 4) // 2
+    return 3, hidden_count
+
+
+def cost_of(length, weights):
+    return pl.CostEstimate(
+        flops=2 * length * sum(w.size for w in weights),
+        bytes_accessed=2 * sum(w.size for w in weights),
+        transcendentals=0,
+    )
+
+
+def forward_step(branch_scale, tick, tokens, arrived, allowed, weights, vectors, stash):
     length, feature = arrived.shape
-    wj, wo, we, wc = weights
-    vecs, bj, be = vectors
-    hidden = we.shape[-1]
-    params = (wj, wo, we, wc, vecs, bj, be)
+    joint_count, hidden_count = counts_of(weights, feature)
+    hidden = hidden_count * feature
+    weights = tuple(pltpu.with_memory_space_constraint(w, pltpu.VMEM) for w in weights)
     scratch = [
-        pltpu.VMEM(wj.shape, BF16),
-        pltpu.VMEM(wo.shape, BF16),
-        pltpu.VMEM(we.shape, BF16),
-        pltpu.VMEM(wc.shape, BF16),
-        pltpu.VMEM(vecs.shape, F32),
-        pltpu.VMEM(bj.shape, F32),
-        pltpu.VMEM(be.shape, F32),
-        pltpu.VMEM((length, length), F32),
         pltpu.VMEM((LAYERS + 1, length, feature), F32),
         pltpu.VMEM((LAYERS, length, feature), F32),
         pltpu.VMEM((LAYERS, length, feature), BF16),
@@ -253,57 +258,39 @@
         pltpu.VMEM((LAYERS, length, feature), BF16),
         pltpu.VMEM((LAYERS, length, hidden), BF16),
         pltpu.VMEM((LAYERS, length, hidden), BF16),
-        pltpu.SemaphoreType.DMA((LAYERS, 4)),
-        pltpu.SemaphoreType.DMA((5,)),
+        pltpu.SemaphoreType.DMA((2,)),
         pltpu.SemaphoreType.DMA((LAYERS, 8)),
     ]
-    leading = 4 + len(params)
+    leading = 4 + len(weights) + len(vectors)
     outs = pl.pallas_call(
-        partial(forward_kernel, branch_scale),
-        out_shape=tuple(jax.ShapeDtypeStruct(s.shape, s.dtype) for s in stash)
-        + (jax.ShapeDtypeStruct((length, feature), F32),),
-        in_specs=[SMEM] + [ANY] * (leading - 1 + len(stash)),
-        out_specs=tuple([ANY] * (len(stash) + 1)),
+        partial(forward_kernel, branch_scale, joint_count, hidden_count),
+        out_shape=tuple(pltpu.HBM(s.shape, s.dtype) for s in stash)
+        + (pltpu.VMEM((length, feature), F32), jax.ShapeDtypeStruct((1,), jnp.int32)),
+        in_specs=[SMEM, ANY, ANY]
+        + [VMEM] * (1 + len(weights) + len(vectors))
+        + [HBM] * len(stash),
+        out_specs=tuple([HBM] * len(stash) + [VMEM, SMEM]),
         scratch_shapes=scratch,
         input_output_aliases={leading + i: i for i in range(len(stash))},
-        compiler_params=pltpu.CompilerParams(vmem_limit_bytes=56 * 1024 * 1024),
-        cost_estimate=pl.CostEstimate(
-            flops=2 * length * sum(w.size for w in weights),
-            bytes_accessed=2 * sum(w.size for w in weights),
-            transcendentals=0,
-        ),
+        compiler_params=pltpu.CompilerParams(vmem_limit_bytes=SCOPED),
+        cost_estimate=cost_of(length, weights),
         name="forward_step",
-    )(flags, tokens, arrived, allowed, *params, *stash)
-    return outs[:-1], outs[-1]
-
-
-def backward_kernel(
-    branch_scale,
-    flags,
-    seeds,
-    arrived,
-    allowed_rows,
-    wj,
-    wo,
-    we,
-    wc,
-    vecs,
-    sh,
-    sg,
-    st,
-    sd,
-    *refs,
-):
+    )(tick, in_hbm(tokens), arrived, allowed, *weights, *vectors, *stash)
+    return outs[:-2], outs[-2], outs[-1]
+
+
+def backward_kernel(branch_scale, joint_count, hidden_count, tick, seeds, arrived, allowed_rows, *refs):
+    weight_count = joint_count + 1 + 2 * hidden_count
+    wj = refs[:joint_count]
+    wo = refs[joint_count]
+    we = refs[joint_count + 1 : joint_count + 1 + hidden_count]
+    wc = refs[joint_count + 1 + hidden_count : weight_count]
+    vecs, sh, sg, st, sd = refs[weight_count : weight_count + 5]
+    refs = refs[weight_count + 5 :]
     names = ("gw", "gu", "gz", "gt", "small", "r")
     stash = dict(zip(names, refs[6:12]))
-    sent = refs[12]
+    sent, next_tick = refs[12:14]
     (
-        wj_v,
-        wo_v,
-        we_v,
-        wc_v,
-        vecs_v,
-        allow_v,
         h_v,
         g_v,
         t_v,
@@ -315,40 +302,30 @@
         go_v,
         gt_v,
         small_v,
-        w_sem,
         in_sem,
         s_sem,
         out_sem,
-    ) = refs[13:]
-    active, slot, first, last = flags[0], flags[1], flags[2], flags[3]
-    feature = h_v.shape[-1]
-    hidden = we_v.shape[-1]
-
-    @pl.when(active == 1)
+    ) = refs[14:]
+    next_tick[0] = tick[0] + 1
+    section = lax.axis_index("section")
+    sections = lax.axis_size("section")
+    _, length, feature = seeds.shape
+    rows = allowed_rows.shape[0]
+    row_index = tick[0] - 2 * (sections - 1 - section)
+
+    @pl.when((row_index >= 0) & (row_index < rows))
     def _():
-        small = [
-            pltpu.make_async_copy(allowed_rows.at[slot], allow_v, in_sem.at[1]),
-            pltpu.make_async_copy(vecs, vecs_v, in_sem.at[2]),
-        ]
-
-        @pl.when(last == 1)
+        slot = jnp.clip(row_index, 0, rows - 1)
+
+        @pl.when(section == sections - 1)
         def _():
-            pltpu.make_async_copy(seeds.at[slot], grad_v, in_sem.at[0]).start()
-
-        @pl.when(last == 0)
+            pltpu.make_async_copy(seeds.at[lax.rem(slot, seeds.shape[0])], grad_v, in_sem.at[0]).start()
+
+        @pl.when(section < sections - 1)
         def _():
             pltpu.make_async_copy(arrived, grad_v, in_sem.at[0]).start()
 
-        for copy in small:
-            copy.start()
-        sources = ((wc, wc_v), (we, we_v), (wo, wo_v), (wj, wj_v))
         saved = ((sd, d_v), (sg, g_v), (st, t_v), (sh, h_v))
-
-        def weight_copy(layer, index):
-            source, target = sources[index]
-            return pltpu.make_async_copy(
-                source.at[layer], target.at[layer], w_sem.at[layer, index]
-            )
 
         def saved_copy(layer, index):
             source, target = saved[index]
@@ -358,7 +335,6 @@
 
         for layer in reversed(range(LAYERS)):
             for index in range(4):
-                weight_copy(layer, index).start()
                 saved_copy(layer, index).start()
 
         def put(layer, index, name, value_ref):
@@ -366,40 +342,37 @@
                 value_ref.at[layer], stash[name].at[layer, slot], out_sem.at[layer, index]
             )
 
+        allowed = jnp.concatenate([allowed_rows[slot], allowed_rows[slot]], axis=0) > 0.5
         pltpu.make_async_copy(arrived, grad_v, in_sem.at[0]).wait()
-        for copy in small:
-            copy.wait()
-        allowed = jnp.concatenate([allow_v[...], allow_v[...]], axis=0) > 0.5
-
-        for layer in reversed(range(LAYERS)):
+
+        def one_layer(turn):
+            layer = LAYERS - 1 - turn
             gw = (branch_scale * grad_v[...]).astype(BF16)
             gw_v[layer] = gw
             put(layer, 0, "gw", gw_v).start()
             small_v[layer, 7:8, :] = column_sum(gw)
-            weight_copy(layer, 0).wait()
             saved_copy(layer, 0).wait()
-            for index, start in enumerate(range(0, hidden, CHUNK)):
-                span = slice(start, start + CHUNK)
-                gu = (
-                    d_v[layer, :, span].astype(F32) * mm_nt(gw, wc_v[layer, span, :])
-                ).astype(BF16)
+            gc = jnp.zeros((length, feature), F32)
+            for index in range(hidden_count):
+                span = slice(index * feature, (index + 1) * feature)
+                gu = (d_v[layer, :, span].astype(F32) * mm_nt(gw, wc[index][layer])).astype(BF16)
                 gu_v[layer, :, span] = gu
                 small_v[layer, 8 + index : 9 + index, :] = column_sum(gu)
             put(layer, 1, "gu", gu_v).start()
-            weight_copy(layer, 1).wait()
-            gc = mm_nt(gu_v[layer], we_v[layer])
+            for index in range(hidden_count):
+                span = slice(index * feature, (index + 1) * feature)
+                gc = gc + mm_nt(gu_v[layer, :, span], we[index][layer])
             saved_copy(layer, 1).wait()
             normed, scale = norm_parts(g_v[layer])
             small_v[layer, 4:5, :] = column_sum(gc * normed)
             small_v[layer, 5:6, :] = column_sum(gc)
-            gg = grad_v[...] + norm_back(normed, scale, vecs_v[layer, 3:4, :], gc)
+            gg = grad_v[...] + norm_back(normed, scale, vecs[layer, 3:4, :], gc)
             grad_v[...] = gg
             gz = (branch_scale * gg).astype(BF16)
             gz_v[layer] = gz
             put(layer, 2, "gz", gz_v).start()
             small_v[layer, 6:7, :] = column_sum(gz)
-            weight_copy(layer, 2).wait()
-            go_v[...] = mm_nt(gz, wo_v[layer]).astype(BF16)
+            go_v[...] = mm_nt(gz, wo[layer]).astype(BF16)
             saved_copy(layer, 2).wait()
             for start in range(0, feature, PAIR):
                 queries = stack_halves(t_v[layer, :, start : start + PAIR])
@@ -419,18 +392,21 @@
             put(layer, 3, "gt", gt_v).start()
             small_v[layer, 2:3, :] = column_sum(gt_v[layer, :, :feature])
             small_v[layer, 3:4, :] = column_sum(gt_v[layer, :, 2 * feature :])
-            weight_copy(layer, 3).wait()
-            ga = mm_nt(gt_v[layer], wj_v[layer])
+            ga = jnp.zeros((length, feature), F32)
+            for index in range(joint_count):
+                span = slice(index * feature, (index + 1) * feature)
+                ga = ga + mm_nt(gt_v[layer, :, span], wj[index][layer])
             saved_copy(layer, 3).wait()
             normed, scale = norm_parts(h_v[layer])
             small_v[layer, 0:1, :] = column_sum(ga * normed)
             small_v[layer, 1:2, :] = column_sum(ga)
-            grad_v[...] = grad_v[...] + norm_back(normed, scale, vecs_v[layer, 0:1, :], ga)
+            grad_v[...] = grad_v[...] + norm_back(normed, scale, vecs[layer, 0:1, :], ga)
             put(layer, 4, "small", small_v).start()
-        out = pltpu.make_async_copy(grad_v, sent, in_sem.at[0])
-        out.start()
-
-        @pl.when(first == 1)
+
+        layer_loop(one_layer)
+        sent[...] = grad_v[...]
+
+        @pl.when(section == 0)
         def _():
             final = pltpu.make_async_copy(grad_v, stash["r"].at[slot], in_sem.at[1])
             final.start()
@@ -447,20 +423,14 @@
                 )
             ):
                 put(layer, index, name, value_ref).wait()
-        out.wait()
-
-
-def backward_step(branch_scale, flags, seeds, arrived, allowed, weights, vecs, saved, stash):
+
+
+def backward_step(branch_scale, tick, seeds, arrived, allowed, weights, vecs, saved, stash):
     length, feature = arrived.shape
-    wj, wo, we, wc = weights
-    hidden = we.shape[-1]
+    joint_count, hidden_count = counts_of(weights, feature)
+    hidden = hidden_count * feature
+    weights = tuple(pltpu.with_memory_space_constraint(w, pltpu.VMEM) for w in weights)
     scratch = [
-        pltpu.VMEM(wj.shape, BF16),
-        pltpu.VMEM(wo.shape, BF16),
-        pltpu.VMEM(we.shape, BF16),
-        pltpu.VMEM(wc.shape, BF16),
-        pltpu.VMEM(vecs.shape, F32),
-        pltpu.VMEM((length, length), F32),
         pltpu.VMEM((LAYERS, length, feature), F32),
         pltpu.VMEM((LAYERS, length, feature), F32),
         pltpu.VMEM((LAYERS, length, 3 * feature), BF16),
@@ -472,36 +442,33 @@
         pltpu.VMEM((length, feature), BF16),
         pltpu.VMEM((LAYERS, length, 3 * feature), BF16),
         pltpu.VMEM((LAYERS, 16, feature), F32),
-        pltpu.SemaphoreType.DMA((LAYERS, 4)),
-        pltpu.SemaphoreType.DMA((3,)),
+        pltpu.SemaphoreType.DMA((2,)),
         pltpu.SemaphoreType.DMA((LAYERS, 4)),
         pltpu.SemaphoreType.DMA((LAYERS, 5)),
     ]
-    leading = 4 + 5 + len(saved)
+    leading = 5 + len(weights) + len(saved)
     outs = pl.pallas_call(
-        partial(backward_kernel, branch_scale),
-        out_shape=tuple(jax.ShapeDtypeStruct(s.shape, s.dtype) for s in stash)
-        + (jax.ShapeDtypeStruct((length, feature), F32),),
-        in_specs=[SMEM] + [ANY] * (leading - 1 + len(stash)),
-        out_specs=tuple([ANY] * (len(stash) + 1)),
+        partial(backward_kernel, branch_scale, joint_count, hidden_count),
+        out_shape=tuple(pltpu.HBM(s.shape, s.dtype) for s in stash)
+        + (pltpu.VMEM((length, feature), F32), jax.ShapeDtypeStruct((1,), jnp.int32)),
+        in_specs=[SMEM, ANY, ANY]
+        + [VMEM] * (2 + len(weights))
+        + [HBM] * (len(saved) + len(stash)),
+        out_specs=tuple([HBM] * len(stash) + [VMEM, SMEM]),
         scratch_shapes=scratch,
         input_output_aliases={leading + i: i for i in range(len(stash))},
-        compiler_params=pltpu.CompilerParams(vmem_limit_bytes=56 * 1024 * 1024),
-        cost_estimate=pl.CostEstimate(
-            flops=2 * length * sum(w.size for w in weights),
-            bytes_accessed=2 * sum(w.size for w in weights),
-            transcendentals=0,
-        ),
+        compiler_params=pltpu.CompilerParams(vmem_limit_bytes=SCOPED),
+        cost_estimate=cost_of(length, weights),
         name="backward_step",
-    )(flags, seeds, arrived, allowed, wj, wo, we, wc, vecs, *saved, *stash)
-    return outs[:-1], outs[-1]
+    )(tick, in_hbm(seeds), arrived, allowed, *weights, vecs, *map(in_hbm, saved), *stash)
+    return outs[:-2], outs[-2], outs[-1]
 
 
 def empty_arrays(shapes):
     return pl.pallas_call(
         lambda *refs: None,
-        out_shape=tuple(shapes),
-        out_specs=tuple([ANY] * len(shapes)),
+        out_shape=tuple(pltpu.HBM(s.shape, s.dtype) for s in shapes),
+        out_specs=tuple([HBM] * len(shapes)),
         name="empty_arrays",
     )()
 
@@ -560,7 +527,6 @@
                 [(e * replicas + a, e * replicas + b) for e in ends for a, b in pairs],
             )
         )
-    edge = jnp.concatenate(edges, axis=0)
     document_ends = jnp.cumsum(jnp.concatenate(all_lengths, axis=0), axis=-1)
     segment = jnp.sum(
         (positions[None, :, None] >= document_ends[:, None, :]).astype(jnp.int32), axis=-1
@@ -610,42 +576,42 @@
     onward = [(i, i + 1) for i in range(sections - 1)]
     back = [(i + 1, i) for i in range(sections - 1)]
 
-    def flags_of(row):
-        active = (row >= 0) & (row < rows)
-        return jnp.stack(
-            [
-                active.astype(jnp.int32),
-                jnp.clip(row, 0, rows - 1),
-                first.astype(jnp.int32),
-                last.astype(jnp.int32),
-            ]
-        )
-
-    def forward_tick(tick, carry):
-        stash, sent, arrived = carry
-        arriving = lax.ppermute(sent, "section", onward)
-        flags = flags_of(tick - 2 * section)
-        stash, out = forward_step(
-            branch_scale, flags, edge, arrived, allowed, weights, (vecs, bj, be), stash
-        )
-        return stash, out, arriving
-
-    forward_stash, _, _ = lax.fori_loop(
-        0, ticks, forward_tick, (forward_stash, made[-2], made[-1])
+    vectors = lax.optimization_barrier((vecs, bj, be))
+    allowed = lax.optimization_barrier(allowed)
+    loaded = load_weights(weights)
+    chunk = min(ticks, UNROLL)
+    rounds = -(-ticks // chunk)
+    edge = jnp.concatenate(edges, axis=0) if rounds > 1 else None
+
+    def run(step, pairs, stash):
+        def turn(carry, source_of):
+            stash, sent, arrived, tick = carry
+            for index in range(chunk):
+                arriving = lax.ppermute(sent, "section", pairs)
+                stash, sent, tick = step(tick, source_of(index), arrived, stash)
+                arrived = arriving
+            return stash, sent, arrived, tick
+
+        start = (stash, made[-2], made[-1], jnp.zeros((1,), jnp.int32))
+        if rounds == 1:
+            return turn(start, lambda index: edges[min(index, rows - 1) // own])[::3]
+        return lax.fori_loop(0, rounds, lambda _, carry: turn(carry, lambda index: edge), start)[::3]
+
+    forward_stash, walked = run(
+        lambda tick, source, arrived, stash: forward_step(
+            branch_scale, tick, source, arrived, allowed, loaded, vectors, stash
+        ),
+        onward,
+        forward_stash,
     )
     sh, sg, sa, st, so, sc, sm, sd, final_rows = forward_stash
 
-    def backward_tick(tick, carry):
-        stash, sent, arrived = carry
-        arriving = lax.ppermute(sent, "section", back)
-        flags = flags_of(tick - 2 * (sections - 1 - section))
-        stash, out = backward_step(
-            branch_scale, flags, edge, arrived, allowed, weights, vecs, (sh, sg, st, sd), stash
-        )
-        return stash, out, arriving
-
-    backward_stash, _, _ = lax.fori_loop(
-        0, ticks, backward_tick, (backward_stash, made[-2], made[-1])
+    backward_stash, _ = run(
+        lambda tick, source, arrived, stash: backward_step(
+            branch_scale, tick, source, arrived, allowed, loaded, vectors[0], (sh, sg, st, sd), stash
+        ),
+        back,
+        backward_stash,
     )
     gw, gu, gz, gt, small, first_rows = backward_stash
 

time: 1370 us -> 914 us (0.67)
  waiting for transfers between devices: 404 us -> 215 us
  other arithmetic: 130 us -> 26.3 us
  local copies, waits for them, and re-layouts: 166 us -> 86 us
  starting transfers between devices: 187 us -> 144 us
  Pallas kernels: 440 us -> 405 us
    ppermute x44 -> x42, waiting for transfers between devices: 336 us -> 177 us  [turn(): arriving = lax.ppermute(sent, 'section', pairs)]
    while x88 -> x0, local copies, waits for them, and re-layouts: 138 us -> none
    convert_element_type x44 -> x1, other arithmetic: 77.1 us -> 0.21 us  [body(): ((segment[:, :, None] == segment[:, None, :]) & causal[None]).astype(F32)]
    unnamed x68 -> x254, local copies, waits for them, and re-layouts: 7.99 us -> 70 us
    ppermute x44 -> x42, starting transfers between devices: 164 us -> 120 us  [turn(): arriving = lax.ppermute(sent, 'section', pairs)]
    pallas_call x45 -> x46, Pallas kernels: 440 us -> 405 us  [the longest x22 248 us: backward_step(): pl.pallas_call(partial(backward_kernel, branch_scale, joint_count, hidden...]
    ppermute x1, waiting for transfers between devices: 30.6 us -> 0.01 us  [body(): all_lengths.append(lax.ppermute(lengths, 'dp', pairs))]
    another operation x44 -> x0, other arithmetic: 25.5 us -> none  [flags_of(): jnp.stack([active.astype(jnp.int32), jnp.clip(row, 0, rows - 1), first.as...]
  transfers between devices with their start and end apart: 58 -> 56, of which waited for: 44 -> 29; matrix products, arithmetic and copies ran while one was open for 11% -> 6% of each run, Pallas kernels for 32% -> 42%
where the time goes in v2:
time: 914 us; the launch traced here: 905 us
  Pallas kernels  405 us (44%)
  waiting for transfers between devices  215 us (24%)
  starting transfers between devices  144 us (16%)
  local copies, waits for them, and re-layouts  86 us (9%)
  other arithmetic  26.3 us (3%)
  matrix products  26.1 us (3%)
    pallas_call x22, Pallas kernels, backward_step(): pl.pallas_call(partial(backward_kernel, branch_scale, joint_count, hidden...  248 us
    ppermute x42, waiting for transfers between devices, turn(): arriving = lax.ppermute(sent, 'section', pairs)  177 us
    pallas_call x22, Pallas kernels, forward_step(): pl.pallas_call(partial(forward_kernel, branch_scale, joint_count, hidden_...  147 us
    ppermute x42, starting transfers between devices, turn(): arriving = lax.ppermute(sent, 'section', pairs)  120 us
    unnamed x254, local copies, waits for them, and re-layouts  70 us
    ppermute x7, waiting for transfers between devices, body(): lax.ppermute(payload, 'section', [(0, step), (sections - 1, step - 1)])  37.3 us
    dot_general x4, matrix products, weight_gradient(): jnp.einsum('lrd,lre->lde', left, right, preferred_element_type=F32)  26.1 us
    add x5, other arithmetic, near_sum(): mine = mine + lax.ppermute(parts[shift], 'dp', pairs)  20.3 us
  transfers between devices with their start and end apart: 56, of which 29 were waited for; matrix products, arithmetic and copies ran while one was open for 6% of the time, Pallas kernels for 42%

profile of v2, /device:TPU:0, one launch (start us, length us, event | category | flops | bytes accessed | tf_op | source)
XLA Modules:
  0.0 905.2 jit_solution(17503561884693602820)
XLA Ops:
  14.3 9.6 %load_weights.1 = (bf16[2,768,768]{2,1,0:T(8,128)(2,1)S(1)}, bf16[2,768,768]{2,1,0:T(8,128)(2,1)S(1)}, bf16[2,768,768]{2,1,0:T(8,128)(2,1)S(1)}, bf16[2,768,768]...) custom-call(bf16[2,768,2304]{2,1,0:T(8,128)(2,1)} %refs_0_.1, ...), custom_call_target="tpu_custom_call" | custom-call | tf_op jit(solution)/shard_map/load_weights/pallas_call | solution.py:105
  58.4 12.0 %forward_step.22 = (f32[2,8,128,768]{3,2,1,0:T(8,128)}, f32[2,8,128,768]{3,2,1,0:T(8,128)}, bf16[2,8,128,768]{3,2,1,0:T(8,128)(2,1)}, bf16[2,8,128,2304]{3,2,1,0...) custom-call(s32[1]{0:T(128)} %constant.79.clone.1.tick, ...), custom_call_target="tpu_custom_call", output_to_operand_aliasing={{0}: (19, {}), {1}: (20, {}), {2}: (21, {}), {3}: (22, {}),... | custom-call | flops 3623878656 | bytes 28311552 | tf_op jit(solution)/shard_map/forward_step/pallas_call | solution.py:265
  71.7 12.7 %forward_step.23 = (f32[2,8,128,768]{3,2,1,0:T(8,128)}, f32[2,8,128,768]{3,2,1,0:T(8,128)}, bf16[2,8,128,768]{3,2,1,0:T(8,128)(2,1)}, bf16[2,8,128,2304]{3,2,1,0...) custom-call(s32[1]{0:T(128)} %get-tuple-element.483.tick, ...), custom_call_target="tpu_custom_call", output_to_operand_aliasing={{0}: (19, {}), {1}: (20, {}), {2}: (21, {}), {3}: (22, {}),... | custom-call | flops 3623878656 | bytes 28311552 | tf_op jit(solution)/shard_map/forward_step/pallas_call | solution.py:265
  85.7 12.9 %forward_step.24 = (f32[2,8,128,768]{3,2,1,0:T(8,128)}, f32[2,8,128,768]{3,2,1,0:T(8,128)}, bf16[2,8,128,768]{3,2,1,0:T(8,128)(2,1)}, bf16[2,8,128,2304]{3,2,1,0...) custom-call(s32[1]{0:T(128)} %get-tuple-element.494.tick, ...), custom_call_target="tpu_custom_call", output_to_operand_aliasing={{0}: (19, {}), {1}: (20, {}), {2}: (21, {}), {3}: (22, {}),... | custom-call | flops 3623878656 | bytes 28311552 | tf_op jit(solution)/shard_map/forward_step/pallas_call | solution.py:265
  99.9 12.7 %forward_step.25 = (f32[2,8,128,768]{3,2,1,0:T(8,128)}, f32[2,8,128,768]{3,2,1,0:T(8,128)}, bf16[2,8,128,768]{3,2,1,0:T(8,128)(2,1)}, bf16[2,8,128,2304]{3,2,1,0...) custom-call(s32[1]{0:T(128)} %get-tuple-element.505.tick, ...), custom_call_target="tpu_custom_call", output_to_operand_aliasing={{0}: (19, {}), {1}: (20, {}), {2}: (21, {}), {3}: (22, {}),... | custom-call | flops 3623878656 | bytes 28311552 | tf_op jit(solution)/shard_map/forward_step/pallas_call | solution.py:265
  114.0 12.7 %forward_step.26 = (f32[2,8,128,768]{3,2,1,0:T(8,128)}, f32[2,8,128,768]{3,2,1,0:T(8,128)}, bf16[2,8,128,768]{3,2,1,0:T(8,128)(2,1)}, bf16[2,8,128,2304]{3,2,1,0...) custom-call(s32[1]{0:T(128)} %get-tuple-element.516.tick, ...), custom_call_target="tpu_custom_call", output_to_operand_aliasing={{0}: (19, {}), {1}: (20, {}), {2}: (21, {}), {3}: (22, {}),... | custom-call | flops 3623878656 | bytes 28311552 | tf_op jit(solution)/shard_map/forward_step/pallas_call | solution.py:265
  128.0 12.6 %forward_step.27 = (f32[2,8,128,768]{3,2,1,0:T(8,128)}, f32[2,8,128,768]{3,2,1,0:T(8,128)}, bf16[2,8,128,768]{3,2,1,0:T(8,128)(2,1)}, bf16[2,8,128,2304]{3,2,1,0...) custom-call(s32[1]{0:T(128)} %get-tuple-element.527.tick, ...), custom_call_target="tpu_custom_call", output_to_operand_aliasing={{0}: (19, {}), {1}: (20, {}), {2}: (21, {}), {3}: (22, {}),... | custom-call | flops 3623878656 | bytes 28311552 | tf_op jit(solution)/shard_map/forward_step/pallas_call | solution.py:265
  142.0 12.8 %forward_step.28 = (f32[2,8,128,768]{3,2,1,0:T(8,128)}, f32[2,8,128,768]{3,2,1,0:T(8,128)}, bf16[2,8,128,768]{3,2,1,0:T(8,128)(2,1)}, bf16[2,8,128,2304]{3,2,1,0...) custom-call(s32[1]{0:T(128)} %get-tuple-element.538.tick, ...), custom_call_target="tpu_custom_call", output_to_operand_aliasing={{0}: (19, {}), {1}: (20, {}), {2}: (21, {}), {3}: (22, {}),... | custom-call | flops 3623878656 | bytes 28311552 | tf_op jit(solution)/shard_map/forward_step/pallas_call | solution.py:265
  156.1 12.6 %forward_step.29 = (f32[2,8,128,768]{3,2,1,0:T(8,128)}, f32[2,8,128,768]{3,2,1,0:T(8,128)}, bf16[2,8,128,768]{3,2,1,0:T(8,128)(2,1)}, bf16[2,8,128,2304]{3,2,1,0...) custom-call(s32[1]{0:T(128)} %get-tuple-element.549.tick, ...), custom_call_target="tpu_custom_call", output_to_operand_aliasing={{0}: (19, {}), {1}: (20, {}), {2}: (21, {}), {3}: (22, {}),... | custom-call | flops 3623878656 | bytes 28311552 | tf_op jit(solution)/shard_map/forward_step/pallas_call | solution.py:265
  171.5 8.8 collective-permute-start.11
  181.7 12.5 %collective-permute-start.12 = (f32[128,768]{1,0:T(8,128)S(1)}, f32[128,768]{1,0:T(8,128)S(1)}, u32[]{:S(2)}, u32[]{:S(2)}) collective-permute-start(f32[128,768]{1,0:T(8,128)S(1)} %get-tuple-element.594), channel_id=1, source_target_pairs={{0,4},{4,8},{8,12},{12,16},{16,20},{20,24},{24,28},{1,5},{5,9},{9,... | collective-permute-start | bytes 1179656 | tf_op jit(solution)/shard_map/ppermute | solution.py:590
  194.2 10.0 %forward_step.32 = (f32[2,8,128,768]{3,2,1,0:T(8,128)}, f32[2,8,128,768]{3,2,1,0:T(8,128)}, bf16[2,8,128,768]{3,2,1,0:T(8,128)(2,1)}, bf16[2,8,128,2304]{3,2,1,0...) custom-call(s32[1]{0:T(128)} %get-tuple-element.582.tick, ...), custom_call_target="tpu_custom_call", output_to_operand_aliasing={{0}: (19, {}), {1}: (20, {}), {2}: (21, {}), {3}: (22, {}),... | custom-call | flops 3623878656 | bytes 28311552 | tf_op jit(solution)/shard_map/forward_step/pallas_call | solution.py:265
  231.7 10.2 %forward_step.36 = (f32[2,8,128,768]{3,2,1,0:T(8,128)}, f32[2,8,128,768]{3,2,1,0:T(8,128)}, bf16[2,8,128,768]{3,2,1,0:T(8,128)(2,1)}, bf16[2,8,128,2304]{3,2,1,0...) custom-call(s32[1]{0:T(128)} %get-tuple-element.626.tick, ...), custom_call_target="tpu_custom_call", output_to_operand_aliasing={{0}: (19, {}), {1}: (20, {}), {2}: (21, {}), {3}: (22, {}),... | custom-call | flops 3623878656 | bytes 28311552 | tf_op jit(solution)/shard_map/forward_step/pallas_call | solution.py:265
  275.7 9.9 %forward_step.40 = (f32[2,8,128,768]{3,2,1,0:T(8,128)}, f32[2,8,128,768]{3,2,1,0:T(8,128)}, bf16[2,8,128,768]{3,2,1,0:T(8,128)(2,1)}, bf16[2,8,128,2304]{3,2,1,0...) custom-call(s32[1]{0:T(128)} %get-tuple-element.670.tick, ...), custom_call_target="tpu_custom_call", output_to_operand_aliasing={{0}: (19, {}), {1}: (20, {}), {2}: (21, {}), {3}: (22, {}),... | custom-call | flops 3623878656 | bytes 28311552 | tf_op jit(solution)/shard_map/forward_step/pallas_call | solution.py:265
  313.4 9.2 %backward_step.22 = (bf16[2,8,128,768]{3,2,1,0:T(8,128)(2,1)}, bf16[2,8,128,3072]{3,2,1,0:T(8,128)(2,1)}, bf16[2,8,128,768]{3,2,1,0:T(8,128)(2,1)}, bf16[2,8,128...) custom-call(s32[1]{0:T(128)} %constant.79.clone.1.tick, ...), custom_call_target="tpu_custom_call", output_to_operand_aliasing={{0}: (21, {}), {1}: (22, {}), {2}: (23, {}), {3}: (24, {}),... | custom-call | flops 3623878656 | bytes 28311552 | tf_op jit(solution)/shard_map/backward_step/pallas_call | solution.py:450
  337.0 9.8 %backward_step.25 = (bf16[2,8,128,768]{3,2,1,0:T(8,128)(2,1)}, bf16[2,8,128,3072]{3,2,1,0:T(8,128)(2,1)}, bf16[2,8,128,768]{3,2,1,0:T(8,128)(2,1)}, bf16[2,8,128...) custom-call(s32[1]{0:T(128)} %get-tuple-element.739.tick, ...), custom_call_target="tpu_custom_call", output_to_operand_aliasing={{0}: (21, {}), {1}: (22, {}), {2}: (23, {}), {3}: (24, {}),... | custom-call | flops 3623878656 | bytes 28311552 | tf_op jit(solution)/shard_map/backward_step/pallas_call | solution.py:450
  353.1 16.6 %collective-permute-done.27.arrived = f32[128,768]{1,0:T(8,128)S(1)} collective-permute-done((f32[128,768]{1,0:T(8,128)}, f32[128,768]{1,0:T(8,128)S(1)}, u32[]{:S(2)}, u32[]{:S(2)}) %collective-permute-start.27) | collective-permute-done | bytes 393248 | tf_op jit(solution)/shard_map/ppermute | solution.py:590
  377.5 10.0 %backward_step.28 = (bf16[2,8,128,768]{3,2,1,0:T(8,128)(2,1)}, bf16[2,8,128,3072]{3,2,1,0:T(8,128)(2,1)}, bf16[2,8,128,768]{3,2,1,0:T(8,128)(2,1)}, bf16[2,8,128...) custom-call(s32[1]{0:T(128)} %get-tuple-element.763.tick, ...), custom_call_target="tpu_custom_call", output_to_operand_aliasing={{0}: (21, {}), {1}: (22, {}), {2}: (23, {}), {3}: (24, {}),... | custom-call | flops 3623878656 | bytes 28311552 | tf_op jit(solution)/shard_map/backward_step/pallas_call | solution.py:450
  393.3 9.4 %collective-permute-done.30.arrived = f32[128,768]{1,0:T(8,128)S(1)} collective-permute-done((f32[128,768]{1,0:T(8,128)}, f32[128,768]{1,0:T(8,128)S(1)}, u32[]{:S(2)}, u32[]{:S(2)}) %collective-permute-start.30) | collective-permute-done | bytes 393248 | tf_op jit(solution)/shard_map/ppermute | solution.py:590
  407.3 9.8 %backward_step.31 = (bf16[2,8,128,768]{3,2,1,0:T(8,128)(2,1)}, bf16[2,8,128,3072]{3,2,1,0:T(8,128)(2,1)}, bf16[2,8,128,768]{3,2,1,0:T(8,128)(2,1)}, bf16[2,8,128...) custom-call(s32[1]{0:T(128)} %get-tuple-element.787.tick, ...), custom_call_target="tpu_custom_call", output_to_operand_aliasing={{0}: (21, {}), {1}: (22, {}), {2}: (23, {}), {3}: (24, {}),... | custom-call | flops 3623878656 | bytes 28311552 | tf_op jit(solution)/shard_map/backward_step/pallas_call | solution.py:450
  433.0 10.0 %backward_step.34 = (bf16[2,8,128,768]{3,2,1,0:T(8,128)(2,1)}, bf16[2,8,128,3072]{3,2,1,0:T(8,128)(2,1)}, bf16[2,8,128,768]{3,2,1,0:T(8,128)(2,1)}, bf16[2,8,128...) custom-call(s32[1]{0:T(128)} %get-tuple-element.811.tick, ...), custom_call_target="tpu_custom_call", output_to_operand_aliasing={{0}: (21, {}), {1}: (22, {}), {2}: (23, {}), {3}: (24, {}),... | custom-call | flops 3623878656 | bytes 28311552 | tf_op jit(solution)/shard_map/backward_step/pallas_call | solution.py:450
  448.8 109.4 %collective-permute-done.36.arrived = f32[128,768]{1,0:T(8,128)S(1)} collective-permute-done((f32[128,768]{1,0:T(8,128)}, f32[128,768]{1,0:T(8,128)S(1)}, u32[]{:S(2)}, u32[]{:S(2)}) %collective-permute-start.36) | collective-permute-done | bytes 393248 | tf_op jit(solution)/shard_map/ppermute | solution.py:590
  558.2 23.1 %backward_step.36 = (bf16[2,8,128,768]{3,2,1,0:T(8,128)(2,1)}, bf16[2,8,128,3072]{3,2,1,0:T(8,128)(2,1)}, bf16[2,8,128,768]{3,2,1,0:T(8,128)(2,1)}, bf16[2,8,128...) custom-call(s32[1]{0:T(128)} %get-tuple-element.827.tick, ...), custom_call_target="tpu_custom_call", output_to_operand_aliasing={{0}: (21, {}), {1}: (22, {}), {2}: (23, {}), {3}: (24, {}),... | custom-call | flops 3623878656 | bytes 28311552 | tf_op jit(solution)/shard_map/backward_step/pallas_call | solution.py:450
  584.0 23.7 %backward_step.37 = (bf16[2,8,128,768]{3,2,1,0:T(8,128)(2,1)}, bf16[2,8,128,3072]{3,2,1,0:T(8,128)(2,1)}, bf16[2,8,128,768]{3,2,1,0:T(8,128)(2,1)}, bf16[2,8,128...) custom-call(s32[1]{0:T(128)} %get-tuple-element.835.tick, ...), custom_call_target="tpu_custom_call", output_to_operand_aliasing={{0}: (21, {}), {1}: (22, {}), {2}: (23, {}), {3}: (24, {}),... | custom-call | flops 3623878656 | bytes 28311552 | tf_op jit(solution)/shard_map/backward_step/pallas_call | solution.py:450
  610.4 23.1 %backward_step.38 = (bf16[2,8,128,768]{3,2,1,0:T(8,128)(2,1)}, bf16[2,8,128,3072]{3,2,1,0:T(8,128)(2,1)}, bf16[2,8,128,768]{3,2,1,0:T(8,128)(2,1)}, bf16[2,8,128...) custom-call(s32[1]{0:T(128)} %get-tuple-element.843.tick, ...), custom_call_target="tpu_custom_call", output_to_operand_aliasing={{0}: (21, {}), {1}: (22, {}), {2}: (23, {}), {3}: (24, {}),... | custom-call | flops 3623878656 | bytes 28311552 | tf_op jit(solution)/shard_map/backward_step/pallas_call | solution.py:450
  636.7 23.1 %backward_step.39 = (bf16[2,8,128,768]{3,2,1,0:T(8,128)(2,1)}, bf16[2,8,128,3072]{3,2,1,0:T(8,128)(2,1)}, bf16[2,8,128,768]{3,2,1,0:T(8,128)(2,1)}, bf16[2,8,128...) custom-call(s32[1]{0:T(128)} %get-tuple-element.851.tick, ...), custom_call_target="tpu_custom_call", output_to_operand_aliasing={{0}: (21, {}), {1}: (22, {}), {2}: (23, {}), {3}: (24, {}),... | custom-call | flops 3623878656 | bytes 28311552 | tf_op jit(solution)/shard_map/backward_step/pallas_call | solution.py:450
  662.4 23.8 %backward_step.40 = (bf16[2,8,128,768]{3,2,1,0:T(8,128)(2,1)}, bf16[2,8,128,3072]{3,2,1,0:T(8,128)(2,1)}, bf16[2,8,128,768]{3,2,1,0:T(8,128)(2,1)}, bf16[2,8,128...) custom-call(s32[1]{0:T(128)} %get-tuple-element.859.tick, ...), custom_call_target="tpu_custom_call", output_to_operand_aliasing={{0}: (21, {}), {1}: (22, {}), {2}: (23, {}), {3}: (24, {}),... | custom-call | flops 3623878656 | bytes 28311552 | tf_op jit(solution)/shard_map/backward_step/pallas_call | solution.py:450
  688.8 22.5 %backward_step.41 = (bf16[2,8,128,768]{3,2,1,0:T(8,128)(2,1)}, bf16[2,8,128,3072]{3,2,1,0:T(8,128)(2,1)}, bf16[2,8,128,768]{3,2,1,0:T(8,128)(2,1)}, bf16[2,8,128...) custom-call(s32[1]{0:T(128)} %get-tuple-element.867.tick, ...), custom_call_target="tpu_custom_call", output_to_operand_aliasing={{0}: (21, {}), {1}: (22, {}), {2}: (23, {}), {3}: (24, {}),... | custom-call | flops 3623878656 | bytes 28311552 | tf_op jit(solution)/shard_map/backward_step/pallas_call | solution.py:450
  733.5 23.5 %backward_step.42 = (bf16[2,8,128,768]{3,2,1,0:T(8,128)(2,1)}, bf16[2,8,128,3072]{3,2,1,0:T(8,128)(2,1)}, bf16[2,8,128,768]{3,2,1,0:T(8,128)(2,1)}, bf16[2,8,128...) custom-call(s32[1]{0:T(128)} %get-tuple-element.875.tick, ...), custom_call_target="tpu_custom_call", output_to_operand_aliasing={{0}: (21, {}), {1}: (22, {}), {2}: (23, {}), {3}: (24, {}),... | custom-call | flops 3623878656 | bytes 28311552 | tf_op jit(solution)/shard_map/backward_step/pallas_call | solution.py:450
  757.1 23.2 %backward_step.43 = (bf16[2,8,128,768]{3,2,1,0:T(8,128)(2,1)}, bf16[2,8,128,3072]{3,2,1,0:T(8,128)(2,1)}, bf16[2,8,128,768]{3,2,1,0:T(8,128)(2,1)}, bf16[2,8,128...) custom-call(s32[1]{0:T(128)} %get-tuple-element.883.tick, ...), custom_call_target="tpu_custom_call", output_to_operand_aliasing={{0}: (21, {}), {1}: (22, {}), {2}: (23, {}), {3}: (24, {}),... | custom-call | flops 3623878656 | bytes 28311552 | tf_op jit(solution)/shard_map/backward_step/pallas_call | solution.py:450
  795.2 9.4 %fusion.3 = f32[2,384,3072]{2,1,0:T(8,128)} fusion(bf16[2,1024,3072]{2,1,0:T(8,128)(2,1)S(1)} %bitcast.58, bf16[2,1024,768]{2,1,0:T(8,128)(2,1)} %bitcast.63, s32[]{:T(128)S(6)} %select_n.128), kind=kOutput, calls=%fused_computation.7 | convolution fusion | flops 4831838208 | bytes 23592964 | tf_op jit(solution)/shard_map/lrd,lre->lde/dot_general | solution.py:634
  830.0 9.4 %collective-permute-done.44 = f32[4,128,96]{2,1,0:T(8,128)S(1)} collective-permute-done((f32[4,128,96]{2,1,0:T(8,128)S(1)}, f32[4,128,96]{2,1,0:T(8,128)S(1)}, u32[]{:S(2)}, u32[]{:S(2)}) %collective-permute-start.44) | collective-permute-done | bytes 196640 | tf_op jit(solution)/shard_map/ppermute | solution.py:687
  (440 shorter events, 350.7 us)
Async XLA Ops:
  0.7 38.7 %collective-permute-start = (s32[4,4]{1,0:T(4,128)}, s32[4,4]{1,0:T(4,128)S(1)}, u32[]{:S(2)}, u32[]{:S(2)}) collective-permute-start(s32[4,4]{1,0:T(4,128)} %bitcast.73), channel_id=1, source_target_pairs={{2,0},{3,1},{0,2},{1,3},{6,4},{7,5},{4,6},{5,7},{10,8},{11,9},{8,1... | collective-permute-start | bytes 200 | tf_op jit(solution)/shard_map/ppermute | solution.py:522
  3.8 67.9 %collective-permute-start.1 = (f32[128,768]{1,0:T(8,128)}, f32[128,768]{1,0:T(8,128)}, u32[]{:S(2)}, u32[]{:S(2)}) collective-permute-start(f32[128,768]{1,0:T(8,128)} %get-tuple-element.484), channel_id=1, source_target_pairs={{0,4},{4,8},{8,12},{12,16},{16,20},{20,24},{24,28},{1,5},{5,9},{9,... | collective-permute-start | bytes 1179656 | tf_op jit(solution)/shard_map/ppermute | solution.py:590
  11.5 102.5 %collective-permute-start.4 = (f32[4,128,768]{2,1,0:T(8,128)}, f32[4,128,768]{2,1,0:T(8,128)}, u32[]{:S(2)}, u32[]{:S(2)}) collective-permute-start(f32[4,128,768]{2,1,0:T(8,128)} %fusion.2.tokens.seeds), channel_id=1, source_target_pairs={{2,0},{3,1},{0,2},{1,3},{30,28},{31,29},{28,30},{29,31}} | collective-permute-start | bytes 4718600 | tf_op jit(solution)/shard_map/ppermute | solution.py:524
  84.4 15.6 %collective-permute-start.3 = (f32[128,768]{1,0:T(8,128)S(1)}, f32[128,768]{1,0:T(8,128)S(1)}, u32[]{:S(2)}, u32[]{:S(2)}) collective-permute-start(f32[128,768]{1,0:T(8,128)S(1)} %get-tuple-element.506), channel_id=1, source_target_pairs={{0,4},{4,8},{8,12},{12,16},{16,20},{20,24},{24,28},{1,5},{5,9},{9,... | collective-permute-start | bytes 1179656 | tf_op jit(solution)/shard_map/ppermute | solution.py:590
  112.6 15.4 %collective-permute-start.6 = (f32[128,768]{1,0:T(8,128)S(1)}, f32[128,768]{1,0:T(8,128)S(1)}, u32[]{:S(2)}, u32[]{:S(2)}) collective-permute-start(f32[128,768]{1,0:T(8,128)S(1)} %get-tuple-element.528), channel_id=1, source_target_pairs={{0,4},{4,8},{8,12},{12,16},{16,20},{20,24},{24,28},{1,5},{5,9},{9,... | collective-permute-start | bytes 1179656 | tf_op jit(solution)/shard_map/ppermute | solution.py:590
  140.6 15.5 %collective-permute-start.8 = (f32[128,768]{1,0:T(8,128)S(1)}, f32[128,768]{1,0:T(8,128)S(1)}, u32[]{:S(2)}, u32[]{:S(2)}) collective-permute-start(f32[128,768]{1,0:T(8,128)S(1)} %get-tuple-element.550), channel_id=1, source_target_pairs={{0,4},{4,8},{8,12},{12,16},{16,20},{20,24},{24,28},{1,5},{5,9},{9,... | collective-permute-start | bytes 1179656 | tf_op jit(solution)/shard_map/ppermute | solution.py:590
  171.5 22.6 %collective-permute-start.11 = (f32[128,768]{1,0:T(8,128)S(1)}, f32[128,768]{1,0:T(8,128)S(1)}, u32[]{:S(2)}, u32[]{:S(2)}) collective-permute-start(f32[128,768]{1,0:T(8,128)S(1)} %get-tuple-element.583), channel_id=1, source_target_pairs={{0,4},{4,8},{8,12},{12,16},{16,20},{20,24},{24,28},{1,5},{5,9},{9,... | collective-permute-start | bytes 1179656 | tf_op jit(solution)/shard_map/ppermute | solution.py:590
  181.7 24.4 %collective-permute-start.12 = (f32[128,768]{1,0:T(8,128)S(1)}, f32[128,768]{1,0:T(8,128)S(1)}, u32[]{:S(2)}, u32[]{:S(2)}) collective-permute-start(f32[128,768]{1,0:T(8,128)S(1)} %get-tuple-element.594), channel_id=1, source_target_pairs={{0,4},{4,8},{8,12},{12,16},{16,20},{20,24},{24,28},{1,5},{5,9},{9,... | collective-permute-start | bytes 1179656 | tf_op jit(solution)/shard_map/ppermute | solution.py:590
  207.5 15.5 %collective-permute-start.14 = (f32[128,768]{1,0:T(8,128)S(1)}, f32[128,768]{1,0:T(8,128)S(1)}, u32[]{:S(2)}, u32[]{:S(2)}) collective-permute-start(f32[128,768]{1,0:T(8,128)S(1)} %get-tuple-element.616), channel_id=1, source_target_pairs={{0,4},{4,8},{8,12},{12,16},{16,20},{20,24},{24,28},{1,5},{5,9},{9,... | collective-permute-start | bytes 1179656 | tf_op jit(solution)/shard_map/ppermute | solution.py:590
  224.4 24.6 %collective-permute-start.16 = (f32[128,768]{1,0:T(8,128)S(1)}, f32[128,768]{1,0:T(8,128)S(1)}, u32[]{:S(2)}, u32[]{:S(2)}) collective-permute-start(f32[128,768]{1,0:T(8,128)S(1)} %get-tuple-element.638), channel_id=1, source_target_pairs={{0,4},{4,8},{8,12},{12,16},{16,20},{20,24},{24,28},{1,5},{5,9},{9,... | collective-permute-start | bytes 1179656 | tf_op jit(solution)/shard_map/ppermute | solution.py:590
  241.9 15.5 %collective-permute-start.17 = (f32[128,768]{1,0:T(8,128)S(1)}, f32[128,768]{1,0:T(8,128)S(1)}, u32[]{:S(2)}, u32[]{:S(2)}) collective-permute-start(f32[128,768]{1,0:T(8,128)S(1)} %get-tuple-element.649), channel_id=1, source_target_pairs={{0,4},{4,8},{8,12},{12,16},{16,20},{20,24},{24,28},{1,5},{5,9},{9,... | collective-permute-start | bytes 1179656 | tf_op jit(solution)/shard_map/ppermute | solution.py:590
  250.3 16.5 %collective-permute-start.18 = (f32[128,768]{1,0:T(8,128)S(1)}, f32[128,768]{1,0:T(8,128)S(1)}, u32[]{:S(2)}, u32[]{:S(2)}) collective-permute-start(f32[128,768]{1,0:T(8,128)S(1)} %get-tuple-element.660), channel_id=1, source_target_pairs={{0,4},{4,8},{8,12},{12,16},{16,20},{20,24},{24,28},{1,5},{5,9},{9,... | collective-permute-start | bytes 1179656 | tf_op jit(solution)/shard_map/ppermute | solution.py:590
  258.8 16.9 %collective-permute-start.19 = (f32[128,768]{1,0:T(8,128)S(1)}, f32[128,768]{1,0:T(8,128)S(1)}, u32[]{:S(2)}, u32[]{:S(2)}) collective-permute-start(f32[128,768]{1,0:T(8,128)S(1)} %get-tuple-element.671), channel_id=1, source_target_pairs={{0,4},{4,8},{8,12},{12,16},{16,20},{20,24},{24,28},{1,5},{5,9},{9,... | collective-permute-start | bytes 1179656 | tf_op jit(solution)/shard_map/ppermute | solution.py:590
  268.2 24.0 %collective-permute-start.20 = (f32[128,768]{1,0:T(8,128)S(1)}, f32[128,768]{1,0:T(8,128)S(1)}, u32[]{:S(2)}, u32[]{:S(2)}) collective-permute-start(f32[128,768]{1,0:T(8,128)S(1)} %get-tuple-element.682), channel_id=1, source_target_pairs={{0,4},{4,8},{8,12},{12,16},{16,20},{20,24},{24,28},{1,5},{5,9},{9,... | collective-permute-start | bytes 1179656 | tf_op jit(solution)/shard_map/ppermute | solution.py:590
  285.6 17.7 %collective-permute-start.21 = (f32[128,768]{1,0:T(8,128)S(1)}, f32[128,768]{1,0:T(8,128)S(1)}, u32[]{:S(2)}, u32[]{:S(2)}) collective-permute-start(f32[128,768]{1,0:T(8,128)S(1)} %get-tuple-element.693), channel_id=1, source_target_pairs={{0,4},{4,8},{8,12},{12,16},{16,20},{20,24},{24,28},{1,5},{5,9},{9,... | collective-permute-start | bytes 1179656 | tf_op jit(solution)/shard_map/ppermute | solution.py:590
  293.7 18.1 %collective-permute-start.22 = (f32[128,768]{1,0:T(8,128)S(1)}, f32[128,768]{1,0:T(8,128)S(1)}, u32[]{:S(2)}, u32[]{:S(2)}) collective-permute-start(f32[128,768]{1,0:T(8,128)S(1)} %get-tuple-element.704), channel_id=1, source_target_pairs={{0,4},{4,8},{8,12},{12,16},{16,20},{20,24},{24,28},{1,5},{5,9},{9,... | collective-permute-start | bytes 1179656 | tf_op jit(solution)/shard_map/ppermute | solution.py:590
  299.0 25.0 %collective-permute-start.23 = (f32[128,768]{1,0:T(8,128)S(1)}, f32[128,768]{1,0:T(8,128)S(1)}, u32[]{:S(2)}, u32[]{:S(2)}) collective-permute-start(f32[128,768]{1,0:T(8,128)S(1)} %copy-done.113), channel_id=1, source_target_pairs={{4,0},{8,4},{12,8},{16,12},{20,16},{24,20},{28,24},{5,1},{9,5},{13... | collective-permute-start | bytes 1179656 | tf_op jit(solution)/shard_map/ppermute | solution.py:590
  347.6 22.1 %collective-permute-start.27 = (f32[128,768]{1,0:T(8,128)}, f32[128,768]{1,0:T(8,128)S(1)}, u32[]{:S(2)}, u32[]{:S(2)}) collective-permute-start(f32[128,768]{1,0:T(8,128)} %copy-done.84), channel_id=1, source_target_pairs={{4,0},{8,4},{12,8},{16,12},{20,16},{24,20},{28,24},{5,1},{9,5},{13... | collective-permute-start | bytes 1179656 | tf_op jit(solution)/shard_map/ppermute | solution.py:590
  351.9 25.6 %collective-permute-start.28 = (f32[128,768]{1,0:T(8,128)}, f32[128,768]{1,0:T(8,128)S(1)}, u32[]{:S(2)}, u32[]{:S(2)}) collective-permute-start(f32[128,768]{1,0:T(8,128)} %copy-done.85), channel_id=1, source_target_pairs={{4,0},{8,4},{12,8},{16,12},{20,16},{24,20},{28,24},{5,1},{9,5},{13... | collective-permute-start | bytes 1179656 | tf_op jit(solution)/shard_map/ppermute | solution.py:590
  372.2 17.4 %collective-permute-start.29 = (f32[128,768]{1,0:T(8,128)}, f32[128,768]{1,0:T(8,128)S(1)}, u32[]{:S(2)}, u32[]{:S(2)}) collective-permute-start(f32[128,768]{1,0:T(8,128)} %copy-done.86), channel_id=1, source_target_pairs={{4,0},{8,4},{12,8},{16,12},{20,16},{24,20},{28,24},{5,1},{9,5},{13... | collective-permute-start | bytes 1179656 | tf_op jit(solution)/shard_map/ppermute | solution.py:590
  443.8 114.4 %collective-permute-start.36 = (f32[128,768]{1,0:T(8,128)}, f32[128,768]{1,0:T(8,128)S(1)}, u32[]{:S(2)}, u32[]{:S(2)}) collective-permute-start(f32[128,768]{1,0:T(8,128)} %copy-done.93), channel_id=1, source_target_pairs={{4,0},{8,4},{12,8},{16,12},{20,16},{24,20},{28,24},{5,1},{9,5},{13... | collective-permute-start | bytes 1179656 | tf_op jit(solution)/shard_map/ppermute | solution.py:590
  447.5 136.5 %collective-permute-start.37 = (f32[128,768]{1,0:T(8,128)}, f32[128,768]{1,0:T(8,128)S(1)}, u32[]{:S(2)}, u32[]{:S(2)}) collective-permute-start(f32[128,768]{1,0:T(8,128)} %copy-done.94), channel_id=1, source_target_pairs={{4,0},{8,4},{12,8},{16,12},{20,16},{24,20},{28,24},{5,1},{9,5},{13... | collective-permute-start | bytes 1179656 | tf_op jit(solution)/shard_map/ppermute | solution.py:590
  582.1 28.3 %collective-permute-start.38 = (f32[128,768]{1,0:T(8,128)}, f32[128,768]{1,0:T(8,128)S(1)}, u32[]{:S(2)}, u32[]{:S(2)}) collective-permute-start(f32[128,768]{1,0:T(8,128)} %copy-done.95), channel_id=1, source_target_pairs={{4,0},{8,4},{12,8},{16,12},{20,16},{24,20},{28,24},{5,1},{9,5},{13... | collective-permute-start | bytes 1179656 | tf_op jit(solution)/shard_map/ppermute | solution.py:590
  608.5 28.2 %collective-permute-start.39 = (f32[128,768]{1,0:T(8,128)}, f32[128,768]{1,0:T(8,128)S(1)}, u32[]{:S(2)}, u32[]{:S(2)}) collective-permute-start(f32[128,768]{1,0:T(8,128)} %copy-done.96), channel_id=1, source_target_pairs={{4,0},{8,4},{12,8},{16,12},{20,16},{24,20},{28,24},{5,1},{9,5},{13... | collective-permute-start | bytes 1179656 | tf_op jit(solution)/shard_map/ppermute | solution.py:590
  634.3 28.1 %collective-permute-start.40 = (f32[128,768]{1,0:T(8,128)}, f32[128,768]{1,0:T(8,128)S(1)}, u32[]{:S(2)}, u32[]{:S(2)}) collective-permute-start(f32[128,768]{1,0:T(8,128)} %copy-done.97), channel_id=1, source_target_pairs={{4,0},{8,4},{12,8},{16,12},{20,16},{24,20},{28,24},{5,1},{9,5},{13... | collective-permute-start | bytes 1179656 | tf_op jit(solution)/shard_map/ppermute | solution.py:590
  660.6 28.1 %collective-permute-start.41 = (f32[128,768]{1,0:T(8,128)}, f32[128,768]{1,0:T(8,128)S(1)}, u32[]{:S(2)}, u32[]{:S(2)}) collective-permute-start(f32[128,768]{1,0:T(8,128)} %copy-done.98), channel_id=1, source_target_pairs={{4,0},{8,4},{12,8},{16,12},{20,16},{24,20},{28,24},{5,1},{9,5},{13... | collective-permute-start | bytes 1179656 | tf_op jit(solution)/shard_map/ppermute | solution.py:590
  687.0 28.2 %collective-permute-start.42 = (f32[128,768]{1,0:T(8,128)}, f32[128,768]{1,0:T(8,128)}, u32[]{:S(2)}, u32[]{:S(2)}) collective-permute-start(f32[128,768]{1,0:T(8,128)} %copy-done.82), channel_id=1, source_target_pairs={{4,0},{8,4},{12,8},{16,12},{20,16},{24,20},{28,24},{5,1},{9,5},{13... | collective-permute-start | bytes 1179656 | tf_op jit(solution)/shard_map/ppermute | solution.py:590
  712.0 45.1 %collective-permute-start.43 = (f32[128,768]{1,0:T(8,128)}, f32[128,768]{1,0:T(8,128)S(1)}, u32[]{:S(2)}, u32[]{:S(2)}) collective-permute-start(f32[128,768]{1,0:T(8,128)} %copy-done.83), channel_id=1, source_target_pairs={{4,0},{8,4},{12,8},{16,12},{20,16},{24,20},{28,24},{5,1},{9,5},{13... | collective-permute-start | bytes 1179656 | tf_op jit(solution)/shard_map/ppermute | solution.py:590
  795.1 104.4 %collective-permute-start.55 = (f32[2,768,768]{2,1,0:T(8,128)}, f32[2,768,768]{2,1,0:T(8,128)}, u32[]{:S(2)}, u32[]{:S(2)}) collective-permute-start(f32[2,768,768]{2,1,0:T(8,128)} %constant_dynamic-slice_fusion), channel_id=1, source_target_pairs={{0,1},{1,0},{2,3},{3,2},{4,5},{5,4},{6,7},{7,6},{8,9},{9,8},{10,11... | collective-permute-start | bytes 14155784 | tf_op jit(solution)/shard_map/ppermute | solution.py:626
  809.8 82.5 %collective-permute-start.54 = (f32[2,192,3072]{2,1,0:T(8,128)}, f32[2,192,3072]{2,1,0:T(8,128)}, u32[]{:S(2)}, u32[]{:S(2)}) collective-permute-start(f32[2,192,3072]{2,1,0:T(8,128)} %constant_dynamic-slice_fusion.1), channel_id=1, source_target_pairs={{0,1},{1,0},{2,3},{3,2},{4,5},{5,4},{6,7},{7,6},{8,9},{9,8},{10,11... | collective-permute-start | bytes 14155784 | tf_op jit(solution)/shard_map/ppermute | solution.py:626
  818.6 68.2 %collective-permute-start.52 = (f32[2,192,2304]{2,1,0:T(8,128)}, f32[2,192,2304]{2,1,0:T(8,128)}, u32[]{:S(2)}, u32[]{:S(2)}) collective-permute-start(f32[2,192,2304]{2,1,0:T(8,128)} %constant_dynamic-slice_fusion.3), channel_id=1, source_target_pairs={{0,1},{1,0},{2,3},{3,2},{4,5},{5,4},{6,7},{7,6},{8,9},{9,8},{10,11... | collective-permute-start | bytes 10616840 | tf_op jit(solution)/shard_map/ppermute | solution.py:626
  826.1 58.3 %collective-permute-start.53 = (f32[2,192,768]{2,1,0:T(8,128)}, f32[2,192,768]{2,1,0:T(8,128)}, u32[]{:S(2)}, u32[]{:S(2)}) collective-permute-start(f32[2,192,768]{2,1,0:T(8,128)} %constant_dynamic-slice_fusion.2), channel_id=1, source_target_pairs={{0,1},{1,0},{2,3},{3,2},{4,5},{5,4},{6,7},{7,6},{8,9},{9,8},{10,11... | collective-permute-start | bytes 3538952 | tf_op jit(solution)/shard_map/ppermute | solution.py:626
  (147 other events, 1705.8 us)

commit v3 on v2

--- a/solution.py
+++ b/solution.py
@@ -576,12 +576,32 @@
     onward = [(i, i + 1) for i in range(sections - 1)]
     back = [(i + 1, i) for i in range(sections - 1)]
 
-    vectors = lax.optimization_barrier((vecs, bj, be))
-    allowed = lax.optimization_barrier(allowed)
+    steps = []
+    while not steps or steps[-1] > 1:
+        steps.append(steps[-1] // 2 if steps else sections // 2)
+    mirrored = sections - 1 - section
+    even = section % 2 == 0
+    arrives = [jnp.where(even, section, mirrored) % (2 * step) == step for step in steps]
+    vectors, allowed, even, arrives, first, where, weights = lax.optimization_barrier(
+        ((vecs, bj, be), allowed, even, arrives, first, (section, group, member), weights)
+    )
     loaded = load_weights(weights)
     chunk = min(ticks, UNROLL)
     rounds = -(-ticks // chunk)
     edge = jnp.concatenate(edges, axis=0) if rounds > 1 else None
+
+    def halve(block, step):
+        low, high = jnp.split(block, 2, axis=-1)
+        pairs = [(a, a + step) for a in range(0, sections, 2 * step)]
+        pairs += [(sections - 1 - a, sections - 1 - b) for a, b in pairs]
+        got = lax.ppermute(jnp.where(even, high, low), "section", pairs)
+        return jnp.where(even, low, high), got
+
+    def spread(block, level):
+        kept, got = halve(block, steps[level])
+        if steps[level] == 1:
+            return kept, got
+        return jnp.where(arrives[level], got, kept)
 
     def run(step, pairs, stash):
         def turn(carry, source_of):
@@ -595,7 +615,11 @@
         start = (stash, made[-2], made[-1], jnp.zeros((1,), jnp.int32))
         if rounds == 1:
             return turn(start, lambda index: edges[min(index, rows - 1) // own])[::3]
-        return lax.fori_loop(0, rounds, lambda _, carry: turn(carry, lambda index: edge), start)[::3]
+
+        def again(_, carry):
+            return turn(carry, lambda index: edge)
+
+        return lax.fori_loop(0, rounds, again, start)[::3]
 
     forward_stash, walked = run(
         lambda tick, source, arrived, stash: forward_step(
@@ -605,47 +629,59 @@
         forward_stash,
     )
     sh, sg, sa, st, so, sc, sm, sd, final_rows = forward_stash
-
-    backward_stash, _ = run(
+    backward_stash, walked = run(
         lambda tick, source, arrived, stash: backward_step(
             branch_scale, tick, source, arrived, allowed, loaded, vectors[0], (sh, sg, st, sd), stash
         ),
         back,
         backward_stash,
     )
+    backward_stash, (section, group, member), _ = lax.optimization_barrier(
+        (backward_stash, where, walked)
+    )
     gw, gu, gz, gt, small, first_rows = backward_stash
 
-    def near_sum(parts):
-        mine = parts[0]
-        for shift in range(1, near):
+    def exchange(sends):
+        got = []
+        for shift, payload in enumerate(sends, 1):
             pairs = [
                 (g * near + m, g * near + (m + shift) % near)
                 for g in range(far)
                 for m in range(near)
             ]
-            mine = mine + lax.ppermute(parts[shift], "dp", pairs)
-        return mine
+            got.append(lax.ppermute(payload, "dp", pairs))
+        return got
+
+    def near_sum(part):
+        sends = [part((member + shift) % near) for shift in range(1, near)]
+        return sends, lambda got: sum(got, part(member))
 
     def weight_gradient(left, right):
         width = left.shape[-1]
+        share = width // replicas
         left = left.reshape(LAYERS, rows * length, width)
         right = right.reshape(LAYERS, rows * length, right.shape[-1])
-        left = lax.dynamic_slice_in_dim(left, group * (width // far), width // far, axis=2)
-        product = jnp.einsum("lrd,lre->lde", left, right, preferred_element_type=F32)
-        share = width // replicas
-        return near_sum(
-            [
-                lax.dynamic_slice_in_dim(
-                    product, ((member + shift) % near) * share, share, axis=1
-                )
-                for shift in range(near)
-            ]
-        )
-
-    contract_gradient = weight_gradient(sm, gw)
-    expand_gradient = weight_gradient(sc, gu)
-    joint_gradient = weight_gradient(sa, gt)
-    output_gradient = weight_gradient(so, gz)
+
+        def part(index):
+            mine = lax.dynamic_slice_in_dim(left, (group * near + index) * share, share, axis=2)
+            return jnp.einsum("lrd,lre->lde", mine, right, preferred_element_type=F32)
+
+        return near_sum(part)
+
+    block = jnp.where(first, first_rows[:own], final_rows[:own])
+    pending = []
+    for level, (left, right) in enumerate(((sm, gw), (sc, gu), (sa, gt), (so, gz))):
+        if level < len(steps):
+            block = spread(block, level)
+        sends, finish = weight_gradient(left, right)
+        if level < len(steps):
+            block, sends = lax.optimization_barrier((block, sends))
+        pending.append((sends, finish))
+    for level in range(len(pending), len(steps)):
+        block = spread(block, level)
+    kept, got = block
+    pending = [finish(exchange(sends)) for sends, finish in pending]
+    contract_gradient, expand_gradient, joint_gradient, output_gradient = pending
 
     sums = jnp.sum(small, axis=1)
     vectors = [
@@ -659,14 +695,12 @@
         sums[:, 7],
     ]
     packed = jnp.concatenate([v.reshape(LAYERS, replicas, -1) for v in vectors], axis=2)
-    shared = near_sum(
-        [
-            lax.dynamic_index_in_dim(
-                packed, group * near + (member + shift) % near, axis=1, keepdims=False
-            )
-            for shift in range(near)
-        ]
-    )
+    sends, finish = near_sum(
+        lambda index: lax.dynamic_index_in_dim(
+            packed, group * near + index, axis=1, keepdims=False
+        )
+    )
+    shared = finish(exchange(sends))
     pieces, at = [], 0
     for v in vectors:
         share = v.shape[1] // replicas
@@ -674,23 +708,9 @@
         at += share
 
     share = feature // sections
-    from_first = first_rows[:own].reshape(own, length, feature)
-    from_last = final_rows[:own].reshape(own, length, feature)
-
-    def columns(block, index):
-        return block[:, :, index * share : (index + 1) * share]
-
-    received = []
-    for step in range(1, sections):
-        payload = jnp.where(first, columns(from_first, step), columns(from_last, step - 1))
-        received.append(
-            lax.ppermute(payload, "section", [(0, step), (sections - 1, step - 1)])
-        )
-    gradient_slices = jnp.stack([columns(from_first, 0)] + received)
-    final_slices = jnp.stack(received + [columns(from_last, sections - 1)])
     out_shape = (micro_count, row_count, length, share)
-    input_gradient = lax.dynamic_index_in_dim(gradient_slices, section, keepdims=False)
-    final_hidden = lax.dynamic_index_in_dim(final_slices, section, keepdims=False)
+    input_gradient = jnp.where(even, kept, got)
+    final_hidden = jnp.where(even, got, kept)
     return (
         final_hidden.reshape(out_shape),
         input_gradient.reshape(out_shape),

time: 914 us -> 836 us (0.915)
  local copies, waits for them, and re-layouts: 86 us -> 30.9 us
  matrix products: 26.1 us -> 55.5 us
  waiting for transfers between devices: 215 us -> 193 us
  other arithmetic: 26.3 us -> 9.6 us
  starting transfers between devices: 144 us -> 129 us
    unnamed x254 -> x193, local copies, waits for them, and re-layouts: 70 us -> 21.9 us
    ppermute x12 -> x8, waiting for transfers between devices: 37.4 us -> 7.38 us  [the longest x3 5.15 us: halve(): got = lax.ppermute(jnp.where(even, high, low), 'section', pairs)]
    dot_general x4 -> x8, matrix products: 26.1 us -> 55.5 us  [part(): return jnp.einsum('lrd,lre->lde', mine, right, preferred_element_type=F32)]
    add x5 -> x1, other arithmetic: 20.3 us -> 0.02 us  [near_sum(): return (sends, lambda got: sum(got, part(member)))]
    ppermute x12 -> x8, starting transfers between devices: 17.9 us -> 4.93 us  [the longest x3 3.85 us: halve(): got = lax.ppermute(jnp.where(even, high, low), 'section', pairs)]
    dynamic_slice x8 -> x1, local copies, waits for them, and re-layouts: 12.9 us -> 0.03 us  [body(): lax.dynamic_index_in_dim(packed, group * near + index, axis=1, keepdims=F...]
  transfers between devices with their start and end apart: 56 -> 52, of which waited for: 29 -> 24; matrix products, arithmetic and copies ran while one was open for 6% -> 8% of each run, Pallas kernels for 42% -> 46%
where the time goes in v3:
time: 836 us; the launch traced here: 827 us
  Pallas kernels  405 us (48%)
  waiting for transfers between devices  193 us (23%)
  starting transfers between devices  129 us (15%)
  matrix products  55.5 us (7%)
  local copies, waits for them, and re-layouts  30.9 us (4%)
  other arithmetic  9.6 us (1%)
    pallas_call x22, Pallas kernels, backward_step(): pl.pallas_call(partial(backward_kernel, branch_scale, joint_count, hidden...  248 us
    ppermute x42, waiting for transfers between devices, turn(): arriving = lax.ppermute(sent, 'section', pairs)  186 us
    pallas_call x22, Pallas kernels, forward_step(): pl.pallas_call(partial(forward_kernel, branch_scale, joint_count, hidden_...  147 us
    ppermute x42, starting transfers between devices, turn(): arriving = lax.ppermute(sent, 'section', pairs)  120 us
    dot_general x8, matrix products, part(): return jnp.einsum('lrd,lre->lde', mine, right, preferred_element_type=F32)  55.5 us
    unnamed x193, local copies, waits for them, and re-layouts  21.9 us
  transfers between devices with their start and end apart: 52, of which 24 were waited for; matrix products, arithmetic and copies ran while one was open for 8% of the time, Pallas kernels for 46%

profile of v3, /device:TPU:0, one launch (start us, length us, event | category | flops | bytes accessed | tf_op | source)
XLA Modules:
  0.0 827.1 jit_solution(11433973957352047978)
XLA Ops:
  12.6 9.6 %load_weights.1 = (bf16[2,768,768]{2,1,0:T(8,128)(2,1)S(1)}, bf16[2,768,768]{2,1,0:T(8,128)(2,1)S(1)}, bf16[2,768,768]{2,1,0:T(8,128)(2,1)S(1)}, bf16[2,768,768]...) custom-call(bf16[2,768,2304]{2,1,0:T(8,128)(2,1)} %refs_0_, ...), custom_call_target="tpu_custom_call" | custom-call | tf_op jit(solution)/shard_map/load_weights/pallas_call | solution.py:105
  22.2 12.4 %forward_step.22 = (f32[2,8,128,768]{3,2,1,0:T(8,128)}, f32[2,8,128,768]{3,2,1,0:T(8,128)}, bf16[2,8,128,768]{3,2,1,0:T(8,128)(2,1)}, bf16[2,8,128,2304]{3,2,1,0...) custom-call(s32[1]{0:T(128)} %constant.91.clone.1.tick, ...), custom_call_target="tpu_custom_call", output_to_operand_aliasing={{0}: (19, {}), {1}: (20, {}), {2}: (21, {}), {3}: (22, {}),... | custom-call | flops 3623878656 | bytes 28311552 | tf_op jit(solution)/shard_map/forward_step/pallas_call | solution.py:265
  36.0 12.8 %forward_step.23 = (f32[2,8,128,768]{3,2,1,0:T(8,128)}, f32[2,8,128,768]{3,2,1,0:T(8,128)}, bf16[2,8,128,768]{3,2,1,0:T(8,128)(2,1)}, bf16[2,8,128,2304]{3,2,1,0...) custom-call(s32[1]{0:T(128)} %get-tuple-element.518.tick, ...), custom_call_target="tpu_custom_call", output_to_operand_aliasing={{0}: (19, {}), {1}: (20, {}), {2}: (21, {}), {3}: (22, {}),... | custom-call | flops 3623878656 | bytes 28311552 | tf_op jit(solution)/shard_map/forward_step/pallas_call | solution.py:265
  50.1 12.9 %forward_step.24 = (f32[2,8,128,768]{3,2,1,0:T(8,128)}, f32[2,8,128,768]{3,2,1,0:T(8,128)}, bf16[2,8,128,768]{3,2,1,0:T(8,128)(2,1)}, bf16[2,8,128,2304]{3,2,1,0...) custom-call(s32[1]{0:T(128)} %get-tuple-element.529.tick, ...), custom_call_target="tpu_custom_call", output_to_operand_aliasing={{0}: (19, {}), {1}: (20, {}), {2}: (21, {}), {3}: (22, {}),... | custom-call | flops 3623878656 | bytes 28311552 | tf_op jit(solution)/shard_map/forward_step/pallas_call | solution.py:265
  64.3 12.7 %forward_step.25 = (f32[2,8,128,768]{3,2,1,0:T(8,128)}, f32[2,8,128,768]{3,2,1,0:T(8,128)}, bf16[2,8,128,768]{3,2,1,0:T(8,128)(2,1)}, bf16[2,8,128,2304]{3,2,1,0...) custom-call(s32[1]{0:T(128)} %get-tuple-element.540.tick, ...), custom_call_target="tpu_custom_call", output_to_operand_aliasing={{0}: (19, {}), {1}: (20, {}), {2}: (21, {}), {3}: (22, {}),... | custom-call | flops 3623878656 | bytes 28311552 | tf_op jit(solution)/shard_map/forward_step/pallas_call | solution.py:265
  79.6 12.8 %forward_step.26 = (f32[2,8,128,768]{3,2,1,0:T(8,128)}, f32[2,8,128,768]{3,2,1,0:T(8,128)}, bf16[2,8,128,768]{3,2,1,0:T(8,128)(2,1)}, bf16[2,8,128,2304]{3,2,1,0...) custom-call(s32[1]{0:T(128)} %get-tuple-element.551.tick, ...), custom_call_target="tpu_custom_call", output_to_operand_aliasing={{0}: (19, {}), {1}: (20, {}), {2}: (21, {}), {3}: (22, {}),... | custom-call | flops 3623878656 | bytes 28311552 | tf_op jit(solution)/shard_map/forward_step/pallas_call | solution.py:265
  93.7 12.7 %forward_step.27 = (f32[2,8,128,768]{3,2,1,0:T(8,128)}, f32[2,8,128,768]{3,2,1,0:T(8,128)}, bf16[2,8,128,768]{3,2,1,0:T(8,128)(2,1)}, bf16[2,8,128,2304]{3,2,1,0...) custom-call(s32[1]{0:T(128)} %get-tuple-element.562.tick, ...), custom_call_target="tpu_custom_call", output_to_operand_aliasing={{0}: (19, {}), {1}: (20, {}), {2}: (21, {}), {3}: (22, {}),... | custom-call | flops 3623878656 | bytes 28311552 | tf_op jit(solution)/shard_map/forward_step/pallas_call | solution.py:265
  107.7 12.8 %forward_step.28 = (f32[2,8,128,768]{3,2,1,0:T(8,128)}, f32[2,8,128,768]{3,2,1,0:T(8,128)}, bf16[2,8,128,768]{3,2,1,0:T(8,128)(2,1)}, bf16[2,8,128,2304]{3,2,1,0...) custom-call(s32[1]{0:T(128)} %get-tuple-element.573.tick, ...), custom_call_target="tpu_custom_call", output_to_operand_aliasing={{0}: (19, {}), {1}: (20, {}), {2}: (21, {}), {3}: (22, {}),... | custom-call | flops 3623878656 | bytes 28311552 | tf_op jit(solution)/shard_map/forward_step/pallas_call | solution.py:265
  121.9 12.6 %forward_step.29 = (f32[2,8,128,768]{3,2,1,0:T(8,128)}, f32[2,8,128,768]{3,2,1,0:T(8,128)}, bf16[2,8,128,768]{3,2,1,0:T(8,128)(2,1)}, bf16[2,8,128,2304]{3,2,1,0...) custom-call(s32[1]{0:T(128)} %get-tuple-element.584.tick, ...), custom_call_target="tpu_custom_call", output_to_operand_aliasing={{0}: (19, {}), {1}: (20, {}), {2}: (21, {}), {3}: (22, {}),... | custom-call | flops 3623878656 | bytes 28311552 | tf_op jit(solution)/shard_map/forward_step/pallas_call | solution.py:265
  147.8 12.4 %collective-permute-start.12 = (f32[128,768]{1,0:T(8,128)S(1)}, f32[128,768]{1,0:T(8,128)S(1)}, u32[]{:S(2)}, u32[]{:S(2)}) collective-permute-start(f32[128,768]{1,0:T(8,128)S(1)} %get-tuple-element.629), channel_id=1, source_target_pairs={{0,4},{4,8},{8,12},{12,16},{16,20},{20,24},{24,28},{1,5},{5,9},{9,... | collective-permute-start | bytes 1179656 | tf_op jit(solution)/shard_map/ppermute | solution.py:610
  160.2 10.0 %forward_step.32 = (f32[2,8,128,768]{3,2,1,0:T(8,128)}, f32[2,8,128,768]{3,2,1,0:T(8,128)}, bf16[2,8,128,768]{3,2,1,0:T(8,128)(2,1)}, bf16[2,8,128,2304]{3,2,1,0...) custom-call(s32[1]{0:T(128)} %get-tuple-element.617.tick, ...), custom_call_target="tpu_custom_call", output_to_operand_aliasing={{0}: (19, {}), {1}: (20, {}), {2}: (21, {}), {3}: (22, {}),... | custom-call | flops 3623878656 | bytes 28311552 | tf_op jit(solution)/shard_map/forward_step/pallas_call | solution.py:265
  198.2 10.2 %forward_step.36 = (f32[2,8,128,768]{3,2,1,0:T(8,128)}, f32[2,8,128,768]{3,2,1,0:T(8,128)}, bf16[2,8,128,768]{3,2,1,0:T(8,128)(2,1)}, bf16[2,8,128,2304]{3,2,1,0...) custom-call(s32[1]{0:T(128)} %get-tuple-element.661.tick, ...), custom_call_target="tpu_custom_call", output_to_operand_aliasing={{0}: (19, {}), {1}: (20, {}), {2}: (21, {}), {3}: (22, {}),... | custom-call | flops 3623878656 | bytes 28311552 | tf_op jit(solution)/shard_map/forward_step/pallas_call | solution.py:265
  242.8 9.9 %forward_step.40 = (f32[2,8,128,768]{3,2,1,0:T(8,128)}, f32[2,8,128,768]{3,2,1,0:T(8,128)}, bf16[2,8,128,768]{3,2,1,0:T(8,128)(2,1)}, bf16[2,8,128,2304]{3,2,1,0...) custom-call(s32[1]{0:T(128)} %get-tuple-element.705.tick, ...), custom_call_target="tpu_custom_call", output_to_operand_aliasing={{0}: (19, {}), {1}: (20, {}), {2}: (21, {}), {3}: (22, {}),... | custom-call | flops 3623878656 | bytes 28311552 | tf_op jit(solution)/shard_map/forward_step/pallas_call | solution.py:265
  280.9 9.2 %backward_step.22 = (bf16[2,8,128,768]{3,2,1,0:T(8,128)(2,1)}, bf16[2,8,128,3072]{3,2,1,0:T(8,128)(2,1)}, bf16[2,8,128,768]{3,2,1,0:T(8,128)(2,1)}, bf16[2,8,128...) custom-call(s32[1]{0:T(128)} %constant.91.clone.1.tick, ...), custom_call_target="tpu_custom_call", output_to_operand_aliasing={{0}: (21, {}), {1}: (22, {}), {2}: (23, {}), {3}: (24, {}),... | custom-call | flops 3623878656 | bytes 28311552 | tf_op jit(solution)/shard_map/backward_step/pallas_call | solution.py:450
  304.5 9.7 %backward_step.25 = (bf16[2,8,128,768]{3,2,1,0:T(8,128)(2,1)}, bf16[2,8,128,3072]{3,2,1,0:T(8,128)(2,1)}, bf16[2,8,128,768]{3,2,1,0:T(8,128)(2,1)}, bf16[2,8,128...) custom-call(s32[1]{0:T(128)} %get-tuple-element.774.tick, ...), custom_call_target="tpu_custom_call", output_to_operand_aliasing={{0}: (21, {}), {1}: (22, {}), {2}: (23, {}), {3}: (24, {}),... | custom-call | flops 3623878656 | bytes 28311552 | tf_op jit(solution)/shard_map/backward_step/pallas_call | solution.py:450
  325.1 9.3 %collective-permute-done.27.arrived = f32[128,768]{1,0:T(8,128)S(1)} collective-permute-done((f32[128,768]{1,0:T(8,128)}, f32[128,768]{1,0:T(8,128)S(1)}, u32[]{:S(2)}, u32[]{:S(2)}) %collective-permute-start.27) | collective-permute-done | bytes 393248 | tf_op jit(solution)/shard_map/ppermute | solution.py:610
  346.9 10.0 %backward_step.28 = (bf16[2,8,128,768]{3,2,1,0:T(8,128)(2,1)}, bf16[2,8,128,3072]{3,2,1,0:T(8,128)(2,1)}, bf16[2,8,128,768]{3,2,1,0:T(8,128)(2,1)}, bf16[2,8,128...) custom-call(s32[1]{0:T(128)} %get-tuple-element.798.tick, ...), custom_call_target="tpu_custom_call", output_to_operand_aliasing={{0}: (21, {}), {1}: (22, {}), {2}: (23, {}), {3}: (24, {}),... | custom-call | flops 3623878656 | bytes 28311552 | tf_op jit(solution)/shard_map/backward_step/pallas_call | solution.py:450
  376.9 9.8 %backward_step.31 = (bf16[2,8,128,768]{3,2,1,0:T(8,128)(2,1)}, bf16[2,8,128,3072]{3,2,1,0:T(8,128)(2,1)}, bf16[2,8,128,768]{3,2,1,0:T(8,128)(2,1)}, bf16[2,8,128...) custom-call(s32[1]{0:T(128)} %get-tuple-element.822.tick, ...), custom_call_target="tpu_custom_call", output_to_operand_aliasing={{0}: (21, {}), {1}: (22, {}), {2}: (23, {}), {3}: (24, {}),... | custom-call | flops 3623878656 | bytes 28311552 | tf_op jit(solution)/shard_map/backward_step/pallas_call | solution.py:450
  406.8 10.0 %backward_step.34 = (bf16[2,8,128,768]{3,2,1,0:T(8,128)(2,1)}, bf16[2,8,128,3072]{3,2,1,0:T(8,128)(2,1)}, bf16[2,8,128,768]{3,2,1,0:T(8,128)(2,1)}, bf16[2,8,128...) custom-call(s32[1]{0:T(128)} %get-tuple-element.846.tick, ...), custom_call_target="tpu_custom_call", output_to_operand_aliasing={{0}: (21, {}), {1}: (22, {}), {2}: (23, {}), {3}: (24, {}),... | custom-call | flops 3623878656 | bytes 28311552 | tf_op jit(solution)/shard_map/backward_step/pallas_call | solution.py:450
  422.5 107.8 %collective-permute-done.36.arrived = f32[128,768]{1,0:T(8,128)S(1)} collective-permute-done((f32[128,768]{1,0:T(8,128)}, f32[128,768]{1,0:T(8,128)S(1)}, u32[]{:S(2)}, u32[]{:S(2)}) %collective-permute-start.36) | collective-permute-done | bytes 393248 | tf_op jit(solution)/shard_map/ppermute | solution.py:610
  530.3 23.1 %backward_step.36 = (bf16[2,8,128,768]{3,2,1,0:T(8,128)(2,1)}, bf16[2,8,128,3072]{3,2,1,0:T(8,128)(2,1)}, bf16[2,8,128,768]{3,2,1,0:T(8,128)(2,1)}, bf16[2,8,128...) custom-call(s32[1]{0:T(128)} %get-tuple-element.862.tick, ...), custom_call_target="tpu_custom_call", output_to_operand_aliasing={{0}: (21, {}), {1}: (22, {}), {2}: (23, {}), {3}: (24, {}),... | custom-call | flops 3623878656 | bytes 28311552 | tf_op jit(solution)/shard_map/backward_step/pallas_call | solution.py:450
  556.0 23.7 %backward_step.37 = (bf16[2,8,128,768]{3,2,1,0:T(8,128)(2,1)}, bf16[2,8,128,3072]{3,2,1,0:T(8,128)(2,1)}, bf16[2,8,128,768]{3,2,1,0:T(8,128)(2,1)}, bf16[2,8,128...) custom-call(s32[1]{0:T(128)} %get-tuple-element.870.tick, ...), custom_call_target="tpu_custom_call", output_to_operand_aliasing={{0}: (21, {}), {1}: (22, {}), {2}: (23, {}), {3}: (24, {}),... | custom-call | flops 3623878656 | bytes 28311552 | tf_op jit(solution)/shard_map/backward_step/pallas_call | solution.py:450
  582.3 23.1 %backward_step.38 = (bf16[2,8,128,768]{3,2,1,0:T(8,128)(2,1)}, bf16[2,8,128,3072]{3,2,1,0:T(8,128)(2,1)}, bf16[2,8,128,768]{3,2,1,0:T(8,128)(2,1)}, bf16[2,8,128...) custom-call(s32[1]{0:T(128)} %get-tuple-element.878.tick, ...), custom_call_target="tpu_custom_call", output_to_operand_aliasing={{0}: (21, {}), {1}: (22, {}), {2}: (23, {}), {3}: (24, {}),... | custom-call | flops 3623878656 | bytes 28311552 | tf_op jit(solution)/shard_map/backward_step/pallas_call | solution.py:450
  608.5 23.1 %backward_step.39 = (bf16[2,8,128,768]{3,2,1,0:T(8,128)(2,1)}, bf16[2,8,128,3072]{3,2,1,0:T(8,128)(2,1)}, bf16[2,8,128,768]{3,2,1,0:T(8,128)(2,1)}, bf16[2,8,128...) custom-call(s32[1]{0:T(128)} %get-tuple-element.886.tick, ...), custom_call_target="tpu_custom_call", output_to_operand_aliasing={{0}: (21, {}), {1}: (22, {}), {2}: (23, {}), {3}: (24, {}),... | custom-call | flops 3623878656 | bytes 28311552 | tf_op jit(solution)/shard_map/backward_step/pallas_call | solution.py:450
  634.2 23.8 %backward_step.40 = (bf16[2,8,128,768]{3,2,1,0:T(8,128)(2,1)}, bf16[2,8,128,3072]{3,2,1,0:T(8,128)(2,1)}, bf16[2,8,128,768]{3,2,1,0:T(8,128)(2,1)}, bf16[2,8,128...) custom-call(s32[1]{0:T(128)} %get-tuple-element.894.tick, ...), custom_call_target="tpu_custom_call", output_to_operand_aliasing={{0}: (21, {}), {1}: (22, {}), {2}: (23, {}), {3}: (24, {}),... | custom-call | flops 3623878656 | bytes 28311552 | tf_op jit(solution)/shard_map/backward_step/pallas_call | solution.py:450
  660.1 23.1 %backward_step.41 = (bf16[2,8,128,768]{3,2,1,0:T(8,128)(2,1)}, bf16[2,8,128,3072]{3,2,1,0:T(8,128)(2,1)}, bf16[2,8,128,768]{3,2,1,0:T(8,128)(2,1)}, bf16[2,8,128...) custom-call(s32[1]{0:T(128)} %get-tuple-element.902.tick, ...), custom_call_target="tpu_custom_call", output_to_operand_aliasing={{0}: (21, {}), {1}: (22, {}), {2}: (23, {}), {3}: (24, {}),... | custom-call | flops 3623878656 | bytes 28311552 | tf_op jit(solution)/shard_map/backward_step/pallas_call | solution.py:450
  686.3 22.7 %backward_step.42 = (bf16[2,8,128,768]{3,2,1,0:T(8,128)(2,1)}, bf16[2,8,128,3072]{3,2,1,0:T(8,128)(2,1)}, bf16[2,8,128,768]{3,2,1,0:T(8,128)(2,1)}, bf16[2,8,128...) custom-call(s32[1]{0:T(128)} %get-tuple-element.910.tick, ...), custom_call_target="tpu_custom_call", output_to_operand_aliasing={{0}: (21, {}), {1}: (22, {}), {2}: (23, {}), {3}: (24, {}),... | custom-call | flops 3623878656 | bytes 28311552 | tf_op jit(solution)/shard_map/backward_step/pallas_call | solution.py:450
  709.0 9.2 %collective-permute-done.43.arrived = f32[128,768]{1,0:T(8,128)S(1)} collective-permute-done((f32[128,768]{1,0:T(8,128)}, f32[128,768]{1,0:T(8,128)S(1)}, u32[]{:S(2)}, u32[]{:S(2)}) %collective-permute-start.43) | collective-permute-done | bytes 393248 | tf_op jit(solution)/shard_map/ppermute | solution.py:610
  718.1 23.3 %backward_step.43 = (bf16[2,8,128,768]{3,2,1,0:T(8,128)(2,1)}, bf16[2,8,128,3072]{3,2,1,0:T(8,128)(2,1)}, bf16[2,8,128,768]{3,2,1,0:T(8,128)(2,1)}, bf16[2,8,128...) custom-call(s32[1]{0:T(128)} %get-tuple-element.918.tick, ...), custom_call_target="tpu_custom_call", output_to_operand_aliasing={{0}: (21, {}), {1}: (22, {}), {2}: (23, {}), {3}: (24, {}),... | custom-call | flops 3623878656 | bytes 28311552 | tf_op jit(solution)/shard_map/backward_step/pallas_call | solution.py:450
  758.4 10.1 %fusion.15 = f32[2,192,3072]{2,1,0:T(8,128)} fusion(bf16[2,1024,3072]{2,1,0:T(8,128)(2,1)} %bitcast.37, bf16[2,1024,768]{2,1,0:T(8,128)(2,1)} %bitcast.53, s32[]{:T(128)S(6)} %select_n.158), kind=kOutput, calls=%fused_computation.18 | convolution fusion | flops 2415919104 | bytes 18350084 | tf_op jit(solution)/shard_map/lrd,lre->lde/dot_general | solution.py:667
  801.4 9.2 %convolution_add_fusion = f32[2,192,2304]{2,1,0:T(8,128)} fusion(f32[2,192,2304]{2,1,0:T(8,128)} %collective-permute-done.48, bf16[2,1024,2304]{2,1,0:T(8,128)(2,1)} %bitcast.43, bf16[2,1024,768]{2,1,0:T(8,128)(2,1)} %bitcast.50, s32[]{:T(128)S(6)} %select_n.165), kind=kOutput, calls=%fused_computation | convolution fusion | flops 1812824064 | bytes 17563652 | tf_op jit(solution)/shard_map/lrd,lre->lde/dot_general | solution.py:667
  810.6 9.1 %fusion.4 = f32[2,768,768]{2,1,0:T(8,128)} fusion(f32[2,768,768]{2,1,0:T(8,128)} %collective-permute-done.51, bf16[2,1024,768]{2,1,0:T(8,128)(2,1)S(1)} %bitcast.56, bf16[2,1024,3072]{2,1,0:T(8,128)(2,1)} %bitcast.42, s32[]{:T(128)S(6)} %select_n.166), kind=kOutput, calls=%fused_computation.6 | convolution fusion | flops 2417098752 | bytes 15728644 | tf_op jit(solution)/shard_map/lrd,lre->lde/dot_general | solution.py:667
  (367 shorter events, 280.6 us)
Async XLA Ops:
  7.3 71.1 %collective-permute-start.4 = (f32[4,128,768]{2,1,0:T(8,128)}, f32[4,128,768]{2,1,0:T(8,128)S(1)}, u32[]{:S(2)}, u32[]{:S(2)}) collective-permute-start(f32[4,128,768]{2,1,0:T(8,128)} %fusion.7.tokens.seeds), channel_id=1, source_target_pairs={{2,0},{3,1},{0,2},{1,3},{30,28},{31,29},{28,30},{29,31}} | collective-permute-start | bytes 4718600 | tf_op jit(solution)/shard_map/ppermute | solution.py:524
  9.2 26.7 %collective-permute-start.1 = (f32[128,768]{1,0:T(8,128)}, f32[128,768]{1,0:T(8,128)S(1)}, u32[]{:S(2)}, u32[]{:S(2)}) collective-permute-start(f32[128,768]{1,0:T(8,128)} %get-tuple-element.519), channel_id=1, source_target_pairs={{0,4},{4,8},{8,12},{12,16},{16,20},{20,24},{24,28},{1,5},{5,9},{9,... | collective-permute-start | bytes 1179656 | tf_op jit(solution)/shard_map/ppermute | solution.py:610
  48.7 15.6 %collective-permute-start.3 = (f32[128,768]{1,0:T(8,128)S(1)}, f32[128,768]{1,0:T(8,128)S(1)}, u32[]{:S(2)}, u32[]{:S(2)}) collective-permute-start(f32[128,768]{1,0:T(8,128)S(1)} %get-tuple-element.541), channel_id=1, source_target_pairs={{0,4},{4,8},{8,12},{12,16},{16,20},{20,24},{24,28},{1,5},{5,9},{9,... | collective-permute-start | bytes 1179656 | tf_op jit(solution)/shard_map/ppermute | solution.py:610
  77.0 16.6 %collective-permute-start.6 = (f32[128,768]{1,0:T(8,128)S(1)}, f32[128,768]{1,0:T(8,128)S(1)}, u32[]{:S(2)}, u32[]{:S(2)}) collective-permute-start(f32[128,768]{1,0:T(8,128)S(1)} %get-tuple-element.563), channel_id=1, source_target_pairs={{0,4},{4,8},{8,12},{12,16},{16,20},{20,24},{24,28},{1,5},{5,9},{9,... | collective-permute-start | bytes 1179656 | tf_op jit(solution)/shard_map/ppermute | solution.py:610
  106.4 15.5 %collective-permute-start.8 = (f32[128,768]{1,0:T(8,128)S(1)}, f32[128,768]{1,0:T(8,128)S(1)}, u32[]{:S(2)}, u32[]{:S(2)}) collective-permute-start(f32[128,768]{1,0:T(8,128)S(1)} %get-tuple-element.585), channel_id=1, source_target_pairs={{0,4},{4,8},{8,12},{12,16},{16,20},{20,24},{24,28},{1,5},{5,9},{9,... | collective-permute-start | bytes 1179656 | tf_op jit(solution)/shard_map/ppermute | solution.py:610
  137.2 22.9 %collective-permute-start.11 = (f32[128,768]{1,0:T(8,128)S(1)}, f32[128,768]{1,0:T(8,128)S(1)}, u32[]{:S(2)}, u32[]{:S(2)}) collective-permute-start(f32[128,768]{1,0:T(8,128)S(1)} %get-tuple-element.618), channel_id=1, source_target_pairs={{0,4},{4,8},{8,12},{12,16},{16,20},{20,24},{24,28},{1,5},{5,9},{9,... | collective-permute-start | bytes 1179656 | tf_op jit(solution)/shard_map/ppermute | solution.py:610
  147.8 24.3 %collective-permute-start.12 = (f32[128,768]{1,0:T(8,128)S(1)}, f32[128,768]{1,0:T(8,128)S(1)}, u32[]{:S(2)}, u32[]{:S(2)}) collective-permute-start(f32[128,768]{1,0:T(8,128)S(1)} %get-tuple-element.629), channel_id=1, source_target_pairs={{0,4},{4,8},{8,12},{12,16},{16,20},{20,24},{24,28},{1,5},{5,9},{9,... | collective-permute-start | bytes 1179656 | tf_op jit(solution)/shard_map/ppermute | solution.py:610
  190.2 25.1 %collective-permute-start.16 = (f32[128,768]{1,0:T(8,128)S(1)}, f32[128,768]{1,0:T(8,128)S(1)}, u32[]{:S(2)}, u32[]{:S(2)}) collective-permute-start(f32[128,768]{1,0:T(8,128)S(1)} %get-tuple-element.673), channel_id=1, source_target_pairs={{0,4},{4,8},{8,12},{12,16},{16,20},{20,24},{24,28},{1,5},{5,9},{9,... | collective-permute-start | bytes 1179656 | tf_op jit(solution)/shard_map/ppermute | solution.py:610
  208.3 15.7 %collective-permute-start.17 = (f32[128,768]{1,0:T(8,128)S(1)}, f32[128,768]{1,0:T(8,128)S(1)}, u32[]{:S(2)}, u32[]{:S(2)}) collective-permute-start(f32[128,768]{1,0:T(8,128)S(1)} %get-tuple-element.684), channel_id=1, source_target_pairs={{0,4},{4,8},{8,12},{12,16},{16,20},{20,24},{24,28},{1,5},{5,9},{9,... | collective-permute-start | bytes 1179656 | tf_op jit(solution)/shard_map/ppermute | solution.py:610
  216.8 16.8 %collective-permute-start.18 = (f32[128,768]{1,0:T(8,128)S(1)}, f32[128,768]{1,0:T(8,128)S(1)}, u32[]{:S(2)}, u32[]{:S(2)}) collective-permute-start(f32[128,768]{1,0:T(8,128)S(1)} %get-tuple-element.695), channel_id=1, source_target_pairs={{0,4},{4,8},{8,12},{12,16},{16,20},{20,24},{24,28},{1,5},{5,9},{9,... | collective-permute-start | bytes 1179656 | tf_op jit(solution)/shard_map/ppermute | solution.py:610
  225.5 17.4 %collective-permute-start.19 = (f32[128,768]{1,0:T(8,128)S(1)}, f32[128,768]{1,0:T(8,128)S(1)}, u32[]{:S(2)}, u32[]{:S(2)}) collective-permute-start(f32[128,768]{1,0:T(8,128)S(1)} %get-tuple-element.706), channel_id=1, source_target_pairs={{0,4},{4,8},{8,12},{12,16},{16,20},{20,24},{24,28},{1,5},{5,9},{9,... | collective-permute-start | bytes 1179656 | tf_op jit(solution)/shard_map/ppermute | solution.py:610
  234.9 24.0 %collective-permute-start.20 = (f32[128,768]{1,0:T(8,128)S(1)}, f32[128,768]{1,0:T(8,128)S(1)}, u32[]{:S(2)}, u32[]{:S(2)}) collective-permute-start(f32[128,768]{1,0:T(8,128)S(1)} %get-tuple-element.717), channel_id=1, source_target_pairs={{0,4},{4,8},{8,12},{12,16},{16,20},{20,24},{24,28},{1,5},{5,9},{9,... | collective-permute-start | bytes 1179656 | tf_op jit(solution)/shard_map/ppermute | solution.py:610
  252.8 18.1 %collective-permute-start.21 = (f32[128,768]{1,0:T(8,128)S(1)}, f32[128,768]{1,0:T(8,128)S(1)}, u32[]{:S(2)}, u32[]{:S(2)}) collective-permute-start(f32[128,768]{1,0:T(8,128)S(1)} %get-tuple-element.728), channel_id=1, source_target_pairs={{0,4},{4,8},{8,12},{12,16},{16,20},{20,24},{24,28},{1,5},{5,9},{9,... | collective-permute-start | bytes 1179656 | tf_op jit(solution)/shard_map/ppermute | solution.py:610
  260.4 18.9 %collective-permute-start.22 = (f32[128,768]{1,0:T(8,128)S(1)}, f32[128,768]{1,0:T(8,128)S(1)}, u32[]{:S(2)}, u32[]{:S(2)}) collective-permute-start(f32[128,768]{1,0:T(8,128)S(1)} %get-tuple-element.739), channel_id=1, source_target_pairs={{0,4},{4,8},{8,12},{12,16},{16,20},{20,24},{24,28},{1,5},{5,9},{9,... | collective-permute-start | bytes 1179656 | tf_op jit(solution)/shard_map/ppermute | solution.py:610
  265.7 25.7 %collective-permute-start.23 = (f32[128,768]{1,0:T(8,128)S(1)}, f32[128,768]{1,0:T(8,128)S(1)}, u32[]{:S(2)}, u32[]{:S(2)}) collective-permute-start(f32[128,768]{1,0:T(8,128)S(1)} %copy-done.88), channel_id=1, source_target_pairs={{4,0},{8,4},{12,8},{16,12},{20,16},{24,20},{28,24},{5,1},{9,5},{13... | collective-permute-start | bytes 1179656 | tf_op jit(solution)/shard_map/ppermute | solution.py:610
  314.9 19.5 %collective-permute-start.27 = (f32[128,768]{1,0:T(8,128)}, f32[128,768]{1,0:T(8,128)S(1)}, u32[]{:S(2)}, u32[]{:S(2)}) collective-permute-start(f32[128,768]{1,0:T(8,128)} %copy-done.55), channel_id=1, source_target_pairs={{4,0},{8,4},{12,8},{16,12},{20,16},{24,20},{28,24},{5,1},{9,5},{13... | collective-permute-start | bytes 1179656 | tf_op jit(solution)/shard_map/ppermute | solution.py:610
  323.8 23.0 %collective-permute-start.28 = (f32[128,768]{1,0:T(8,128)}, f32[128,768]{1,0:T(8,128)S(1)}, u32[]{:S(2)}, u32[]{:S(2)}) collective-permute-start(f32[128,768]{1,0:T(8,128)} %copy-done.56), channel_id=1, source_target_pairs={{4,0},{8,4},{12,8},{16,12},{20,16},{24,20},{28,24},{5,1},{9,5},{13... | collective-permute-start | bytes 1179656 | tf_op jit(solution)/shard_map/ppermute | solution.py:610
  336.8 22.2 %collective-permute-start.29 = (f32[128,768]{1,0:T(8,128)}, f32[128,768]{1,0:T(8,128)S(1)}, u32[]{:S(2)}, u32[]{:S(2)}) collective-permute-start(f32[128,768]{1,0:T(8,128)} %copy-done.57), channel_id=1, source_target_pairs={{4,0},{8,4},{12,8},{16,12},{20,16},{24,20},{28,24},{5,1},{9,5},{13... | collective-permute-start | bytes 1179656 | tf_op jit(solution)/shard_map/ppermute | solution.py:610
  361.4 15.5 %collective-permute-start.31 = (f32[128,768]{1,0:T(8,128)}, f32[128,768]{1,0:T(8,128)S(1)}, u32[]{:S(2)}, u32[]{:S(2)}) collective-permute-start(f32[128,768]{1,0:T(8,128)} %copy-done.59), channel_id=1, source_target_pairs={{4,0},{8,4},{12,8},{16,12},{20,16},{24,20},{28,24},{5,1},{9,5},{13... | collective-permute-start | bytes 1179656 | tf_op jit(solution)/shard_map/ppermute | solution.py:610
  372.3 16.5 %collective-permute-start.32 = (f32[128,768]{1,0:T(8,128)}, f32[128,768]{1,0:T(8,128)S(1)}, u32[]{:S(2)}, u32[]{:S(2)}) collective-permute-start(f32[128,768]{1,0:T(8,128)} %copy-done.60), channel_id=1, source_target_pairs={{4,0},{8,4},{12,8},{16,12},{20,16},{24,20},{28,24},{5,1},{9,5},{13... | collective-permute-start | bytes 1179656 | tf_op jit(solution)/shard_map/ppermute | solution.py:610
  391.2 15.5 %collective-permute-start.34 = (f32[128,768]{1,0:T(8,128)}, f32[128,768]{1,0:T(8,128)S(1)}, u32[]{:S(2)}, u32[]{:S(2)}) collective-permute-start(f32[128,768]{1,0:T(8,128)} %copy-done.62), channel_id=1, source_target_pairs={{4,0},{8,4},{12,8},{16,12},{20,16},{24,20},{28,24},{5,1},{9,5},{13... | collective-permute-start | bytes 1179656 | tf_op jit(solution)/shard_map/ppermute | solution.py:610
  417.5 112.7 %collective-permute-start.36 = (f32[128,768]{1,0:T(8,128)}, f32[128,768]{1,0:T(8,128)S(1)}, u32[]{:S(2)}, u32[]{:S(2)}) collective-permute-start(f32[128,768]{1,0:T(8,128)} %copy-done.64), channel_id=1, source_target_pairs={{4,0},{8,4},{12,8},{16,12},{20,16},{24,20},{28,24},{5,1},{9,5},{13... | collective-permute-start | bytes 1179656 | tf_op jit(solution)/shard_map/ppermute | solution.py:610
  421.2 134.8 %collective-permute-start.37 = (f32[128,768]{1,0:T(8,128)}, f32[128,768]{1,0:T(8,128)S(1)}, u32[]{:S(2)}, u32[]{:S(2)}) collective-permute-start(f32[128,768]{1,0:T(8,128)} %copy-done.65), channel_id=1, source_target_pairs={{4,0},{8,4},{12,8},{16,12},{20,16},{24,20},{28,24},{5,1},{9,5},{13... | collective-permute-start | bytes 1179656 | tf_op jit(solution)/shard_map/ppermute | solution.py:610
  554.2 28.1 %collective-permute-start.38 = (f32[128,768]{1,0:T(8,128)}, f32[128,768]{1,0:T(8,128)S(1)}, u32[]{:S(2)}, u32[]{:S(2)}) collective-permute-start(f32[128,768]{1,0:T(8,128)} %copy-done.66), channel_id=1, source_target_pairs={{4,0},{8,4},{12,8},{16,12},{20,16},{24,20},{28,24},{5,1},{9,5},{13... | collective-permute-start | bytes 1179656 | tf_op jit(solution)/shard_map/ppermute | solution.py:610
  580.4 28.0 %collective-permute-start.39 = (f32[128,768]{1,0:T(8,128)}, f32[128,768]{1,0:T(8,128)S(1)}, u32[]{:S(2)}, u32[]{:S(2)}) collective-permute-start(f32[128,768]{1,0:T(8,128)} %copy-done.67), channel_id=1, source_target_pairs={{4,0},{8,4},{12,8},{16,12},{20,16},{24,20},{28,24},{5,1},{9,5},{13... | collective-permute-start | bytes 1179656 | tf_op jit(solution)/shard_map/ppermute | solution.py:610
  606.1 28.0 %collective-permute-start.40 = (f32[128,768]{1,0:T(8,128)}, f32[128,768]{1,0:T(8,128)S(1)}, u32[]{:S(2)}, u32[]{:S(2)}) collective-permute-start(f32[128,768]{1,0:T(8,128)} %copy-done.68), channel_id=1, source_target_pairs={{4,0},{8,4},{12,8},{16,12},{20,16},{24,20},{28,24},{5,1},{9,5},{13... | collective-permute-start | bytes 1179656 | tf_op jit(solution)/shard_map/ppermute | solution.py:610
  632.4 27.7 %collective-permute-start.41 = (f32[128,768]{1,0:T(8,128)}, f32[128,768]{1,0:T(8,128)S(1)}, u32[]{:S(2)}, u32[]{:S(2)}) collective-permute-start(f32[128,768]{1,0:T(8,128)} %copy-done.69), channel_id=1, source_target_pairs={{4,0},{8,4},{12,8},{16,12},{20,16},{24,20},{28,24},{5,1},{9,5},{13... | collective-permute-start | bytes 1179656 | tf_op jit(solution)/shard_map/ppermute | solution.py:610
  658.8 27.5 %collective-permute-start.42 = (f32[128,768]{1,0:T(8,128)}, f32[128,768]{1,0:T(8,128)S(1)}, u32[]{:S(2)}, u32[]{:S(2)}) collective-permute-start(f32[128,768]{1,0:T(8,128)} %copy-done.70), channel_id=1, source_target_pairs={{4,0},{8,4},{12,8},{16,12},{20,16},{24,20},{28,24},{5,1},{9,5},{13... | collective-permute-start | bytes 1179656 | tf_op jit(solution)/shard_map/ppermute | solution.py:610
  684.0 34.1 %collective-permute-start.43 = (f32[128,768]{1,0:T(8,128)}, f32[128,768]{1,0:T(8,128)S(1)}, u32[]{:S(2)}, u32[]{:S(2)}) collective-permute-start(f32[128,768]{1,0:T(8,128)} %copy-done.71), channel_id=1, source_target_pairs={{4,0},{8,4},{12,8},{16,12},{20,16},{24,20},{28,24},{5,1},{9,5},{13... | collective-permute-start | bytes 1179656 | tf_op jit(solution)/shard_map/ppermute | solution.py:610
  768.6 42.0 %collective-permute-start.51 = (f32[2,768,768]{2,1,0:T(8,128)}, f32[2,768,768]{2,1,0:T(8,128)}, u32[]{:S(2)}, u32[]{:S(2)}) collective-permute-start(f32[2,768,768]{2,1,0:T(8,128)} %fusion.2), channel_id=1, source_target_pairs={{0,1},{1,0},{2,3},{3,2},{4,5},{5,4},{6,7},{7,6},{8,9},{9,8},{10,11... | collective-permute-start | bytes 14155784 | tf_op jit(solution)/shard_map/ppermute | solution.py:652
  777.8 23.5 %collective-permute-start.48 = (f32[2,192,2304]{2,1,0:T(8,128)}, f32[2,192,2304]{2,1,0:T(8,128)}, u32[]{:S(2)}, u32[]{:S(2)}) collective-permute-start(f32[2,192,2304]{2,1,0:T(8,128)} %fusion.13), channel_id=1, source_target_pairs={{0,1},{1,0},{2,3},{3,2},{4,5},{5,4},{6,7},{7,6},{8,9},{9,8},{10,11... | collective-permute-start | bytes 10616840 | tf_op jit(solution)/shard_map/ppermute | solution.py:652
  777.8 41.9 %collective-permute-start.50 = (f32[2,192,3072]{2,1,0:T(8,128)}, f32[2,192,3072]{2,1,0:T(8,128)}, u32[]{:S(2)}, u32[]{:S(2)}) collective-permute-start(f32[2,192,3072]{2,1,0:T(8,128)} %fusion.15), channel_id=1, source_target_pairs={{0,1},{1,0},{2,3},{3,2},{4,5},{5,4},{6,7},{7,6},{8,9},{9,8},{10,11... | collective-permute-start | bytes 14155784 | tf_op jit(solution)/shard_map/ppermute | solution.py:652
  (115 other events, 2462.5 us)

commit v4 on v3

--- a/solution.py
+++ b/solution.py
@@ -111,6 +111,88 @@
         compiler_params=pltpu.CompilerParams(vmem_limit_bytes=SCOPED),
         name="load_weights",
     )(*map(in_hbm, weights))
+
+
+def load_turned_kernel(source, *refs):
+    targets, sems = refs[:-1], refs[-1]
+    copies = [
+        pltpu.make_async_copy(source.at[at], target, sems.at[at])
+        for at, target in enumerate(targets)
+    ]
+    for copy in copies:
+        copy.start()
+    for copy in copies:
+        copy.wait()
+
+
+def load_turned(turned):
+    count, _, width, _ = turned.shape
+    return pl.pallas_call(
+        load_turned_kernel,
+        out_shape=tuple(pltpu.VMEM((LAYERS, width, width), BF16) for _ in range(count)),
+        in_specs=[ANY],
+        out_specs=tuple([VMEM] * count),
+        scratch_shapes=[pltpu.SemaphoreType.DMA((count,))],
+        compiler_params=pltpu.CompilerParams(vmem_limit_bytes=SCOPED),
+        name="load_turned",
+    )(in_hbm(turned))
+
+
+def turn_kernel(blocks, width, late, *refs):
+    weights, turned, before_v, after_v, in_sem, out_sem = refs[:4], *refs[5:]
+    section = lax.axis_index("section")
+    half = lax.axis_size("section") // 2
+    chosen = section < half if late else section >= half
+
+    @pl.when(chosen)
+    def _():
+        turns = [(at, layer) for at in range(len(blocks)) for layer in range(LAYERS)]
+
+        def fetch(step):
+            at, layer = turns[step]
+            index, row, column = blocks[at]
+            return pltpu.make_async_copy(
+                weights[index].at[layer, row : row + width, column : column + width],
+                before_v.at[step % 2],
+                in_sem.at[step % 2],
+            )
+
+        def keep(step):
+            at, layer = turns[step]
+            return pltpu.make_async_copy(
+                after_v.at[step % 2], turned.at[at, layer], out_sem.at[step % 2]
+            )
+
+        fetch(0).start()
+        for step in range(len(turns)):
+            fetch(step).wait()
+            if step + 1 < len(turns):
+                fetch(step + 1).start()
+            if step > 1:
+                keep(step - 2).wait()
+            after_v[step % 2] = before_v[step % 2].T
+            keep(step).start()
+        keep(len(turns) - 2).wait()
+        keep(len(turns) - 1).wait()
+
+
+def turn_weights(weights, turned, late):
+    width = weights[1].shape[-1]
+    return pl.pallas_call(
+        partial(turn_kernel, weight_blocks(weights), width, late),
+        out_shape=pltpu.HBM(turned.shape, BF16),
+        in_specs=[ANY] * 4 + [HBM],
+        out_specs=HBM,
+        scratch_shapes=[
+            pltpu.VMEM((2, width, width), BF16),
+            pltpu.VMEM((2, width, width), BF16),
+            pltpu.SemaphoreType.DMA((2,)),
+            pltpu.SemaphoreType.DMA((2,)),
+        ],
+        input_output_aliases={4: 0},
+        compiler_params=pltpu.CompilerParams(vmem_limit_bytes=SCOPED),
+        name="turn_weights",
+    )(*map(in_hbm, weights), in_hbm(turned))
 
 
 def in_hbm(value):
@@ -355,13 +437,13 @@
             gc = jnp.zeros((length, feature), F32)
             for index in range(hidden_count):
                 span = slice(index * feature, (index + 1) * feature)
-                gu = (d_v[layer, :, span].astype(F32) * mm_nt(gw, wc[index][layer])).astype(BF16)
+                gu = (d_v[layer, :, span].astype(F32) * mm(gw, wc[index][layer])).astype(BF16)
                 gu_v[layer, :, span] = gu
                 small_v[layer, 8 + index : 9 + index, :] = column_sum(gu)
             put(layer, 1, "gu", gu_v).start()
             for index in range(hidden_count):
                 span = slice(index * feature, (index + 1) * feature)
-                gc = gc + mm_nt(gu_v[layer, :, span], we[index][layer])
+                gc = gc + mm(gu_v[layer, :, span], we[index][layer])
             saved_copy(layer, 1).wait()
             normed, scale = norm_parts(g_v[layer])
             small_v[layer, 4:5, :] = column_sum(gc * normed)
@@ -372,7 +454,7 @@
             gz_v[layer] = gz
             put(layer, 2, "gz", gz_v).start()
             small_v[layer, 6:7, :] = column_sum(gz)
-            go_v[...] = mm_nt(gz, wo[layer]).astype(BF16)
+            go_v[...] = mm(gz, wo[layer]).astype(BF16)
             saved_copy(layer, 2).wait()
             for start in range(0, feature, PAIR):
                 queries = stack_halves(t_v[layer, :, start : start + PAIR])
@@ -395,7 +477,7 @@
             ga = jnp.zeros((length, feature), F32)
             for index in range(joint_count):
                 span = slice(index * feature, (index + 1) * feature)
-                ga = ga + mm_nt(gt_v[layer, :, span], wj[index][layer])
+                ga = ga + mm(gt_v[layer, :, span], wj[index][layer])
             saved_copy(layer, 3).wait()
             normed, scale = norm_parts(h_v[layer])
             small_v[layer, 0:1, :] = column_sum(ga * normed)
@@ -569,9 +651,13 @@
         jax.ShapeDtypeStruct((LAYERS, rows, 16, feature), F32),
         edge_shape,
     )
-    made = empty_arrays(forward_shapes + backward_shapes + (row_shape, row_shape))
+    width = output_weight.shape[-1]
+    turned_shape = jax.ShapeDtypeStruct(
+        (len(weight_blocks(weights)), LAYERS, width, width), BF16
+    )
+    made = empty_arrays(forward_shapes + backward_shapes + (turned_shape, row_shape, row_shape))
     forward_stash = made[: len(forward_shapes)]
-    backward_stash = made[len(forward_shapes) : -2]
+    backward_stash = made[len(forward_shapes) : -3]
     ticks = rows + 2 * (sections - 1)
     onward = [(i, i + 1) for i in range(sections - 1)]
     back = [(i + 1, i) for i in range(sections - 1)]
@@ -585,6 +671,8 @@
     vectors, allowed, even, arrives, first, where, weights = lax.optimization_barrier(
         ((vecs, bj, be), allowed, even, arrives, first, (section, group, member), weights)
     )
+    turned = turn_weights(weights, made[-3], False)
+    weights, turned = lax.optimization_barrier((weights, turned))
     loaded = load_weights(weights)
     chunk = min(ticks, UNROLL)
     rounds = -(-ticks // chunk)
@@ -629,6 +717,8 @@
         forward_stash,
     )
     sh, sg, sa, st, so, sc, sm, sd, final_rows = forward_stash
+    weights, turned, _ = lax.optimization_barrier((weights, turned, walked))
+    loaded = load_turned(turn_weights(weights, turned, True))
     backward_stash, walked = run(
         lambda tick, source, arrived, stash: backward_step(
             branch_scale, tick, source, arrived, allowed, loaded, vectors[0], (sh, sg, st, sd), stash

time: 836 us -> 773 us (0.925)
  waiting for transfers between devices: 193 us -> 134 us
  Pallas kernels: 405 us -> 395 us
    ppermute x42, waiting for transfers between devices: 186 us -> 126 us  [turn(): arriving = lax.ppermute(sent, 'section', pairs)]
    pallas_call x22, Pallas kernels: 248 us -> 195 us  [backward_step(): pl.pallas_call(partial(backward_kernel, branch_scale, joint_count, hidden...]
    pallas_call x0 -> x3, Pallas kernels: none -> 41.4 us  [the longest x2 32.1 us: turn_weights(): pl.pallas_call(partial(turn_kernel, weight_blocks(weights), width, late),...]
    unnamed x193 -> x263, local copies, waits for them, and re-layouts: 21.9 us -> 28.7 us
  transfers between devices with their start and end apart: 52 -> 52, of which waited for: 24 -> 27; matrix products, arithmetic and copies ran while one was open for 8% -> 9% of each run, Pallas kernels for 46% -> 50%
where the time goes in v4:
time: 773 us; the launch traced here: 761 us
  Pallas kernels  395 us (51%)
  waiting for transfers between devices  134 us (17%)
  starting transfers between devices  126 us (16%)
  matrix products  55.2 us (7%)
  local copies, waits for them, and re-layouts  37.7 us (5%)
  other arithmetic  9.58 us (1%)
    pallas_call x22, Pallas kernels, backward_step(): pl.pallas_call(partial(backward_kernel, branch_scale, joint_count, hidden...  195 us
    pallas_call x22, Pallas kernels, forward_step(): pl.pallas_call(partial(forward_kernel, branch_scale, joint_count, hidden_...  150 us
    ppermute x42, waiting for transfers between devices, turn(): arriving = lax.ppermute(sent, 'section', pairs)  126 us
    ppermute x42, starting transfers between devices, turn(): arriving = lax.ppermute(sent, 'section', pairs)  117 us
    dot_general x8, matrix products, part(): return jnp.einsum('lrd,lre->lde', mine, right, preferred_element_type=F32)  55.2 us
    pallas_call x2, Pallas kernels, turn_weights(): pl.pallas_call(partial(turn_kernel, weight_blocks(weights), width, late),...  32.1 us
    unnamed x263, local copies, waits for them, and re-layouts  28.7 us
  transfers between devices with their start and end apart: 52, of which 27 were waited for; matrix products, arithmetic and copies ran while one was open for 9% of the time, Pallas kernels for 50%

profile of v4, /device:TPU:0, one launch (start us, length us, event | category | flops | bytes accessed | tf_op | source)
XLA Modules:
  0.0 761.2 jit_solution(7425179861622858507)
XLA Ops:
  14.3 9.6 %load_weights.1 = (bf16[2,768,768]{2,1,0:T(8,128)(2,1)S(1)}, bf16[2,768,768]{2,1,0:T(8,128)(2,1)S(1)}, bf16[2,768,768]{2,1,0:T(8,128)(2,1)S(1)}, bf16[2,768,768]...) custom-call(bf16[2,768,2304]{2,1,0:T(8,128)(2,1)} %refs_0_.2, ...), custom_call_target="tpu_custom_call" | custom-call | tf_op jit(solution)/shard_map/load_weights/pallas_call | solution.py:105
  23.9 12.4 %forward_step.22 = (f32[2,8,128,768]{3,2,1,0:T(8,128)}, f32[2,8,128,768]{3,2,1,0:T(8,128)}, bf16[2,8,128,768]{3,2,1,0:T(8,128)(2,1)}, bf16[2,8,128,2304]{3,2,1,0...) custom-call(s32[1]{0:T(128)} %constant.91.clone.1.tick, ...), custom_call_target="tpu_custom_call", output_to_operand_aliasing={{0}: (19, {}), {1}: (20, {}), {2}: (21, {}), {3}: (22, {}),... | custom-call | flops 3623878656 | bytes 28311552 | tf_op jit(solution)/shard_map/forward_step/pallas_call | solution.py:347
  37.7 13.3 %forward_step.23 = (f32[2,8,128,768]{3,2,1,0:T(8,128)}, f32[2,8,128,768]{3,2,1,0:T(8,128)}, bf16[2,8,128,768]{3,2,1,0:T(8,128)(2,1)}, bf16[2,8,128,2304]{3,2,1,0...) custom-call(s32[1]{0:T(128)} %get-tuple-element.562.tick, ...), custom_call_target="tpu_custom_call", output_to_operand_aliasing={{0}: (19, {}), {1}: (20, {}), {2}: (21, {}), {3}: (22, {}),... | custom-call | flops 3623878656 | bytes 28311552 | tf_op jit(solution)/shard_map/forward_step/pallas_call | solution.py:347
  52.3 12.7 %forward_step.24 = (f32[2,8,128,768]{3,2,1,0:T(8,128)}, f32[2,8,128,768]{3,2,1,0:T(8,128)}, bf16[2,8,128,768]{3,2,1,0:T(8,128)(2,1)}, bf16[2,8,128,2304]{3,2,1,0...) custom-call(s32[1]{0:T(128)} %get-tuple-element.573.tick, ...), custom_call_target="tpu_custom_call", output_to_operand_aliasing={{0}: (19, {}), {1}: (20, {}), {2}: (21, {}), {3}: (22, {}),... | custom-call | flops 3623878656 | bytes 28311552 | tf_op jit(solution)/shard_map/forward_step/pallas_call | solution.py:347
  66.4 12.7 %forward_step.25 = (f32[2,8,128,768]{3,2,1,0:T(8,128)}, f32[2,8,128,768]{3,2,1,0:T(8,128)}, bf16[2,8,128,768]{3,2,1,0:T(8,128)(2,1)}, bf16[2,8,128,2304]{3,2,1,0...) custom-call(s32[1]{0:T(128)} %get-tuple-element.584.tick, ...), custom_call_target="tpu_custom_call", output_to_operand_aliasing={{0}: (19, {}), {1}: (20, {}), {2}: (21, {}), {3}: (22, {}),... | custom-call | flops 3623878656 | bytes 28311552 | tf_op jit(solution)/shard_map/forward_step/pallas_call | solution.py:347
  84.9 13.0 %forward_step.26 = (f32[2,8,128,768]{3,2,1,0:T(8,128)}, f32[2,8,128,768]{3,2,1,0:T(8,128)}, bf16[2,8,128,768]{3,2,1,0:T(8,128)(2,1)}, bf16[2,8,128,2304]{3,2,1,0...) custom-call(s32[1]{0:T(128)} %get-tuple-element.595.tick, ...), custom_call_target="tpu_custom_call", output_to_operand_aliasing={{0}: (19, {}), {1}: (20, {}), {2}: (21, {}), {3}: (22, {}),... | custom-call | flops 3623878656 | bytes 28311552 | tf_op jit(solution)/shard_map/forward_step/pallas_call | solution.py:347
  99.2 12.7 %forward_step.27 = (f32[2,8,128,768]{3,2,1,0:T(8,128)}, f32[2,8,128,768]{3,2,1,0:T(8,128)}, bf16[2,8,128,768]{3,2,1,0:T(8,128)(2,1)}, bf16[2,8,128,2304]{3,2,1,0...) custom-call(s32[1]{0:T(128)} %get-tuple-element.606.tick, ...), custom_call_target="tpu_custom_call", output_to_operand_aliasing={{0}: (19, {}), {1}: (20, {}), {2}: (21, {}), {3}: (22, {}),... | custom-call | flops 3623878656 | bytes 28311552 | tf_op jit(solution)/shard_map/forward_step/pallas_call | solution.py:347
  113.2 12.7 %forward_step.28 = (f32[2,8,128,768]{3,2,1,0:T(8,128)}, f32[2,8,128,768]{3,2,1,0:T(8,128)}, bf16[2,8,128,768]{3,2,1,0:T(8,128)(2,1)}, bf16[2,8,128,2304]{3,2,1,0...) custom-call(s32[1]{0:T(128)} %get-tuple-element.617.tick, ...), custom_call_target="tpu_custom_call", output_to_operand_aliasing={{0}: (19, {}), {1}: (20, {}), {2}: (21, {}), {3}: (22, {}),... | custom-call | flops 3623878656 | bytes 28311552 | tf_op jit(solution)/shard_map/forward_step/pallas_call | solution.py:347
  127.3 12.7 %forward_step.29 = (f32[2,8,128,768]{3,2,1,0:T(8,128)}, f32[2,8,128,768]{3,2,1,0:T(8,128)}, bf16[2,8,128,768]{3,2,1,0:T(8,128)(2,1)}, bf16[2,8,128,2304]{3,2,1,0...) custom-call(s32[1]{0:T(128)} %get-tuple-element.628.tick, ...), custom_call_target="tpu_custom_call", output_to_operand_aliasing={{0}: (19, {}), {1}: (20, {}), {2}: (21, {}), {3}: (22, {}),... | custom-call | flops 3623878656 | bytes 28311552 | tf_op jit(solution)/shard_map/forward_step/pallas_call | solution.py:347
  141.4 10.0 %forward_step.30 = (f32[2,8,128,768]{3,2,1,0:T(8,128)}, f32[2,8,128,768]{3,2,1,0:T(8,128)}, bf16[2,8,128,768]{3,2,1,0:T(8,128)(2,1)}, bf16[2,8,128,2304]{3,2,1,0...) custom-call(s32[1]{0:T(128)} %get-tuple-element.639.tick, ...), custom_call_target="tpu_custom_call", output_to_operand_aliasing={{0}: (19, {}), {1}: (20, {}), {2}: (21, {}), {3}: (22, {}),... | custom-call | flops 3623878656 | bytes 28311552 | tf_op jit(solution)/shard_map/forward_step/pallas_call | solution.py:347
  156.8 12.5 %collective-permute-start.12 = (f32[128,768]{1,0:T(8,128)S(1)}, f32[128,768]{1,0:T(8,128)S(1)}, u32[]{:S(2)}, u32[]{:S(2)}) collective-permute-start(f32[128,768]{1,0:T(8,128)S(1)} %get-tuple-element.673), channel_id=1, source_target_pairs={{0,4},{4,8},{8,12},{12,16},{16,20},{20,24},{24,28},{1,5},{5,9},{9,... | collective-permute-start | bytes 1179656 | tf_op jit(solution)/shard_map/ppermute | solution.py:698
  186.4 10.2 %forward_step.34 = (f32[2,8,128,768]{3,2,1,0:T(8,128)}, f32[2,8,128,768]{3,2,1,0:T(8,128)}, bf16[2,8,128,768]{3,2,1,0:T(8,128)(2,1)}, bf16[2,8,128,2304]{3,2,1,0...) custom-call(s32[1]{0:T(128)} %get-tuple-element.683.tick, ...), custom_call_target="tpu_custom_call", output_to_operand_aliasing={{0}: (19, {}), {1}: (20, {}), {2}: (21, {}), {3}: (22, {}),... | custom-call | flops 3623878656 | bytes 28311552 | tf_op jit(solution)/shard_map/forward_step/pallas_call | solution.py:347
  196.6 12.5 %collective-permute-start.15 = (f32[128,768]{1,0:T(8,128)S(1)}, f32[128,768]{1,0:T(8,128)S(1)}, u32[]{:S(2)}, u32[]{:S(2)}) collective-permute-start(f32[128,768]{1,0:T(8,128)S(1)} %get-tuple-element.706), channel_id=1, source_target_pairs={{0,4},{4,8},{8,12},{12,16},{16,20},{20,24},{24,28},{1,5},{5,9},{9,... | collective-permute-start | bytes 1179656 | tf_op jit(solution)/shard_map/ppermute | solution.py:698
  234.6 10.1 %forward_step.38 = (f32[2,8,128,768]{3,2,1,0:T(8,128)}, f32[2,8,128,768]{3,2,1,0:T(8,128)}, bf16[2,8,128,768]{3,2,1,0:T(8,128)(2,1)}, bf16[2,8,128,2304]{3,2,1,0...) custom-call(s32[1]{0:T(128)} %get-tuple-element.727.tick, ...), custom_call_target="tpu_custom_call", output_to_operand_aliasing={{0}: (19, {}), {1}: (20, {}), {2}: (21, {}), {3}: (22, {}),... | custom-call | flops 3623878656 | bytes 28311552 | tf_op jit(solution)/shard_map/forward_step/pallas_call | solution.py:347
  272.1 32.1 %turn_weights.3.source = bf16[12,2,768,768]{3,2,1,0:T(8,128)(2,1)} custom-call(bf16[2,768,2304]{2,1,0:T(8,128)(2,1)} %refs_0_.2, bf16[2,768,768]{2,1,0:T(8,128)(2,1)} %refs_1_.2, bf16[2,768,3072]{2,1,0:T(8,128)(2,1)} %refs_2_.2, bf16[2,3072,768]{2,1,0:T(8,128)(2,1)} %refs_3_.2, ...), custom_call_target="tpu_custom_call", output_to_operand_aliasing={{}: (4, {})} | custom-call | tf_op jit(solution)/shard_map/turn_weights/pallas_call | solution.py:181
  304.2 9.2 %load_turned.1 = (bf16[2,768,768]{2,1,0:T(8,128)(2,1)S(1)}, bf16[2,768,768]{2,1,0:T(8,128)(2,1)S(1)}, bf16[2,768,768]{2,1,0:T(8,128)(2,1)S(1)}, bf16[2,768,768]{...) custom-call(bf16[12,2,768,768]{3,2,1,0:T(8,128)(2,1)} %turn_weights., ...), custom_call_target="tpu_custom_call" | custom-call | tf_op jit(solution)/shard_map/load_turned/pallas_call | solution.py:130
  355.3 9.4 %backward_step.24 = (bf16[2,8,128,768]{3,2,1,0:T(8,128)(2,1)}, bf16[2,8,128,3072]{3,2,1,0:T(8,128)(2,1)}, bf16[2,8,128,768]{3,2,1,0:T(8,128)(2,1)}, bf16[2,8,128...) custom-call(s32[1]{0:T(128)} %get-tuple-element.810.tick, ...), custom_call_target="tpu_custom_call", output_to_operand_aliasing={{0}: (21, {}), {1}: (22, {}), {2}: (23, {}), {3}: (24, {}),... | custom-call | flops 3623878656 | bytes 28311552 | tf_op jit(solution)/shard_map/backward_step/pallas_call | solution.py:532
  383.2 9.3 %backward_step.27 = (bf16[2,8,128,768]{3,2,1,0:T(8,128)(2,1)}, bf16[2,8,128,3072]{3,2,1,0:T(8,128)(2,1)}, bf16[2,8,128,768]{3,2,1,0:T(8,128)(2,1)}, bf16[2,8,128...) custom-call(s32[1]{0:T(128)} %get-tuple-element.834.tick, ...), custom_call_target="tpu_custom_call", output_to_operand_aliasing={{0}: (21, {}), {1}: (22, {}), {2}: (23, {}), {3}: (24, {}),... | custom-call | flops 3623878656 | bytes 28311552 | tf_op jit(solution)/shard_map/backward_step/pallas_call | solution.py:532
  411.3 9.5 %backward_step.30 = (bf16[2,8,128,768]{3,2,1,0:T(8,128)(2,1)}, bf16[2,8,128,3072]{3,2,1,0:T(8,128)(2,1)}, bf16[2,8,128,768]{3,2,1,0:T(8,128)(2,1)}, bf16[2,8,128...) custom-call(s32[1]{0:T(128)} %get-tuple-element.858.tick, ...), custom_call_target="tpu_custom_call", output_to_operand_aliasing={{0}: (21, {}), {1}: (22, {}), {2}: (23, {}), {3}: (24, {}),... | custom-call | flops 3623878656 | bytes 28311552 | tf_op jit(solution)/shard_map/backward_step/pallas_call | solution.py:532
  438.0 9.3 %backward_step.33 = (bf16[2,8,128,768]{3,2,1,0:T(8,128)(2,1)}, bf16[2,8,128,3072]{3,2,1,0:T(8,128)(2,1)}, bf16[2,8,128,768]{3,2,1,0:T(8,128)(2,1)}, bf16[2,8,128...) custom-call(s32[1]{0:T(128)} %get-tuple-element.882.tick, ...), custom_call_target="tpu_custom_call", output_to_operand_aliasing={{0}: (21, {}), {1}: (22, {}), {2}: (23, {}), {3}: (24, {}),... | custom-call | flops 3623878656 | bytes 28311552 | tf_op jit(solution)/shard_map/backward_step/pallas_call | solution.py:532
  460.1 55.0 %collective-permute-done.36.arrived = f32[128,768]{1,0:T(8,128)S(1)} collective-permute-done((f32[128,768]{1,0:T(8,128)S(1)}, f32[128,768]{1,0:T(8,128)S(1)}, u32[]{:S(2)}, u32[]{:S(2)}) %collective-permute-start.36) | collective-permute-done | bytes 393248 | tf_op jit(solution)/shard_map/ppermute | solution.py:698
  515.2 18.5 %backward_step.36 = (bf16[2,8,128,768]{3,2,1,0:T(8,128)(2,1)}, bf16[2,8,128,3072]{3,2,1,0:T(8,128)(2,1)}, bf16[2,8,128,768]{3,2,1,0:T(8,128)(2,1)}, bf16[2,8,128...) custom-call(s32[1]{0:T(128)} %get-tuple-element.906.tick, ...), custom_call_target="tpu_custom_call", output_to_operand_aliasing={{0}: (21, {}), {1}: (22, {}), {2}: (23, {}), {3}: (24, {}),... | custom-call | flops 3623878656 | bytes 28311552 | tf_op jit(solution)/shard_map/backward_step/pallas_call | solution.py:532
  535.9 17.7 %backward_step.37 = (bf16[2,8,128,768]{3,2,1,0:T(8,128)(2,1)}, bf16[2,8,128,3072]{3,2,1,0:T(8,128)(2,1)}, bf16[2,8,128,768]{3,2,1,0:T(8,128)(2,1)}, bf16[2,8,128...) custom-call(s32[1]{0:T(128)} %get-tuple-element.914.tick, ...), custom_call_target="tpu_custom_call", output_to_operand_aliasing={{0}: (21, {}), {1}: (22, {}), {2}: (23, {}), {3}: (24, {}),... | custom-call | flops 3623878656 | bytes 28311552 | tf_op jit(solution)/shard_map/backward_step/pallas_call | solution.py:532
  556.6 17.7 %backward_step.38 = (bf16[2,8,128,768]{3,2,1,0:T(8,128)(2,1)}, bf16[2,8,128,3072]{3,2,1,0:T(8,128)(2,1)}, bf16[2,8,128,768]{3,2,1,0:T(8,128)(2,1)}, bf16[2,8,128...) custom-call(s32[1]{0:T(128)} %get-tuple-element.922.tick, ...), custom_call_target="tpu_custom_call", output_to_operand_aliasing={{0}: (21, {}), {1}: (22, {}), {2}: (23, {}), {3}: (24, {}),... | custom-call | flops 3623878656 | bytes 28311552 | tf_op jit(solution)/shard_map/backward_step/pallas_call | solution.py:532
  576.1 18.2 %backward_step.39 = (bf16[2,8,128,768]{3,2,1,0:T(8,128)(2,1)}, bf16[2,8,128,3072]{3,2,1,0:T(8,128)(2,1)}, bf16[2,8,128,768]{3,2,1,0:T(8,128)(2,1)}, bf16[2,8,128...) custom-call(s32[1]{0:T(128)} %get-tuple-element.930.tick, ...), custom_call_target="tpu_custom_call", output_to_operand_aliasing={{0}: (21, {}), {1}: (22, {}), {2}: (23, {}), {3}: (24, {}),... | custom-call | flops 3623878656 | bytes 28311552 | tf_op jit(solution)/shard_map/backward_step/pallas_call | solution.py:532
  596.1 17.7 %backward_step.40 = (bf16[2,8,128,768]{3,2,1,0:T(8,128)(2,1)}, bf16[2,8,128,3072]{3,2,1,0:T(8,128)(2,1)}, bf16[2,8,128,768]{3,2,1,0:T(8,128)(2,1)}, bf16[2,8,128...) custom-call(s32[1]{0:T(128)} %get-tuple-element.938.tick, ...), custom_call_target="tpu_custom_call", output_to_operand_aliasing={{0}: (21, {}), {1}: (22, {}), {2}: (23, {}), {3}: (24, {}),... | custom-call | flops 3623878656 | bytes 28311552 | tf_op jit(solution)/shard_map/backward_step/pallas_call | solution.py:532
  616.2 17.7 %backward_step.41 = (bf16[2,8,128,768]{3,2,1,0:T(8,128)(2,1)}, bf16[2,8,128,3072]{3,2,1,0:T(8,128)(2,1)}, bf16[2,8,128,768]{3,2,1,0:T(8,128)(2,1)}, bf16[2,8,128...) custom-call(s32[1]{0:T(128)} %get-tuple-element.946.tick, ...), custom_call_target="tpu_custom_call", output_to_operand_aliasing={{0}: (21, {}), {1}: (22, {}), {2}: (23, {}), {3}: (24, {}),... | custom-call | flops 3623878656 | bytes 28311552 | tf_op jit(solution)/shard_map/backward_step/pallas_call | solution.py:532
  635.7 17.9 %backward_step.42 = (bf16[2,8,128,768]{3,2,1,0:T(8,128)(2,1)}, bf16[2,8,128,3072]{3,2,1,0:T(8,128)(2,1)}, bf16[2,8,128,768]{3,2,1,0:T(8,128)(2,1)}, bf16[2,8,128...) custom-call(s32[1]{0:T(128)} %get-tuple-element.954.tick, ...), custom_call_target="tpu_custom_call", output_to_operand_aliasing={{0}: (21, {}), {1}: (22, {}), {2}: (23, {}), {3}: (24, {}),... | custom-call | flops 3623878656 | bytes 28311552 | tf_op jit(solution)/shard_map/backward_step/pallas_call | solution.py:532
  658.8 17.4 %backward_step.43 = (bf16[2,8,128,768]{3,2,1,0:T(8,128)(2,1)}, bf16[2,8,128,3072]{3,2,1,0:T(8,128)(2,1)}, bf16[2,8,128,768]{3,2,1,0:T(8,128)(2,1)}, bf16[2,8,128...) custom-call(s32[1]{0:T(128)} %get-tuple-element.962.tick, ...), custom_call_target="tpu_custom_call", output_to_operand_aliasing={{0}: (21, {}), {1}: (22, {}), {2}: (23, {}), {3}: (24, {}),... | custom-call | flops 3623878656 | bytes 28311552 | tf_op jit(solution)/shard_map/backward_step/pallas_call | solution.py:532
  693.1 10.1 %fusion.15 = f32[2,192,3072]{2,1,0:T(8,128)} fusion(bf16[2,1024,3072]{2,1,0:T(8,128)(2,1)} %bitcast.37, bf16[2,1024,768]{2,1,0:T(8,128)(2,1)} %bitcast.53, s32[]{:T(128)S(6)} %select_n.158), kind=kOutput, calls=%fused_computation.18 | convolution fusion | flops 2415919104 | bytes 18350084 | tf_op jit(solution)/shard_map/lrd,lre->lde/dot_general | solution.py:757
  736.1 9.2 %convolution_add_fusion = f32[2,192,2304]{2,1,0:T(8,128)} fusion(f32[2,192,2304]{2,1,0:T(8,128)} %collective-permute-done.48, bf16[2,1024,2304]{2,1,0:T(8,128)(2,1)} %bitcast.43, bf16[2,1024,768]{2,1,0:T(8,128)(2,1)} %bitcast.50, s32[]{:T(128)S(6)} %select_n.165), kind=kOutput, calls=%fused_computation | convolution fusion | flops 1812824064 | bytes 17563652 | tf_op jit(solution)/shard_map/lrd,lre->lde/dot_general | solution.py:757
  745.3 8.7 %fusion.4 = f32[2,768,768]{2,1,0:T(8,128)} fusion(f32[2,768,768]{2,1,0:T(8,128)} %collective-permute-done.51, bf16[2,1024,768]{2,1,0:T(8,128)(2,1)S(1)} %bitcast.56, bf16[2,1024,3072]{2,1,0:T(8,128)(2,1)} %bitcast.42, s32[]{:T(128)S(6)} %select_n.166), kind=kOutput, calls=%fused_computation.6 | convolution fusion | flops 2417098752 | bytes 15728644 | tf_op jit(solution)/shard_map/lrd,lre->lde/dot_general | solution.py:757
  (440 shorter events, 286.3 us)
Async XLA Ops:
  7.3 77.6 %collective-permute-start.4 = (f32[4,128,768]{2,1,0:T(8,128)}, f32[4,128,768]{2,1,0:T(8,128)}, u32[]{:S(2)}, u32[]{:S(2)}) collective-permute-start(f32[4,128,768]{2,1,0:T(8,128)} %fusion.7.tokens.seeds), channel_id=1, source_target_pairs={{2,0},{3,1},{0,2},{1,3},{30,28},{31,29},{28,30},{29,31}} | collective-permute-start | bytes 4718600 | tf_op jit(solution)/shard_map/ppermute | solution.py:606
  9.2 28.5 %collective-permute-start.1 = (f32[128,768]{1,0:T(8,128)}, f32[128,768]{1,0:T(8,128)}, u32[]{:S(2)}, u32[]{:S(2)}) collective-permute-start(f32[128,768]{1,0:T(8,128)} %get-tuple-element.563), channel_id=1, source_target_pairs={{0,4},{4,8},{8,12},{12,16},{16,20},{20,24},{24,28},{1,5},{5,9},{9,... | collective-permute-start | bytes 1179656 | tf_op jit(solution)/shard_map/ppermute | solution.py:698
  36.4 15.9 %collective-permute-start.2 = (f32[128,768]{1,0:T(8,128)S(1)}, f32[128,768]{1,0:T(8,128)S(1)}, u32[]{:S(2)}, u32[]{:S(2)}) collective-permute-start(f32[128,768]{1,0:T(8,128)S(1)} %get-tuple-element.574), channel_id=1, source_target_pairs={{0,4},{4,8},{8,12},{12,16},{16,20},{20,24},{24,28},{1,5},{5,9},{9,... | collective-permute-start | bytes 1179656 | tf_op jit(solution)/shard_map/ppermute | solution.py:698
  51.0 15.4 %collective-permute-start.3 = (f32[128,768]{1,0:T(8,128)S(1)}, f32[128,768]{1,0:T(8,128)S(1)}, u32[]{:S(2)}, u32[]{:S(2)}) collective-permute-start(f32[128,768]{1,0:T(8,128)S(1)} %get-tuple-element.585), channel_id=1, source_target_pairs={{0,4},{4,8},{8,12},{12,16},{16,20},{20,24},{24,28},{1,5},{5,9},{9,... | collective-permute-start | bytes 1179656 | tf_op jit(solution)/shard_map/ppermute | solution.py:698
  65.0 19.8 %collective-permute-start.5 = (f32[128,768]{1,0:T(8,128)S(1)}, f32[128,768]{1,0:T(8,128)S(1)}, u32[]{:S(2)}, u32[]{:S(2)}) collective-permute-start(f32[128,768]{1,0:T(8,128)S(1)} %get-tuple-element.596), channel_id=1, source_target_pairs={{0,4},{4,8},{8,12},{12,16},{16,20},{20,24},{24,28},{1,5},{5,9},{9,... | collective-permute-start | bytes 1179656 | tf_op jit(solution)/shard_map/ppermute | solution.py:698
  79.1 20.1 %collective-permute-start.6 = (f32[128,768]{1,0:T(8,128)S(1)}, f32[128,768]{1,0:T(8,128)S(1)}, u32[]{:S(2)}, u32[]{:S(2)}) collective-permute-start(f32[128,768]{1,0:T(8,128)S(1)} %get-tuple-element.607), channel_id=1, source_target_pairs={{0,4},{4,8},{8,12},{12,16},{16,20},{20,24},{24,28},{1,5},{5,9},{9,... | collective-permute-start | bytes 1179656 | tf_op jit(solution)/shard_map/ppermute | solution.py:698
  97.9 15.4 %collective-permute-start.7 = (f32[128,768]{1,0:T(8,128)S(1)}, f32[128,768]{1,0:T(8,128)S(1)}, u32[]{:S(2)}, u32[]{:S(2)}) collective-permute-start(f32[128,768]{1,0:T(8,128)S(1)} %get-tuple-element.618), channel_id=1, source_target_pairs={{0,4},{4,8},{8,12},{12,16},{16,20},{20,24},{24,28},{1,5},{5,9},{9,... | collective-permute-start | bytes 1179656 | tf_op jit(solution)/shard_map/ppermute | solution.py:698
  111.9 15.4 %collective-permute-start.8 = (f32[128,768]{1,0:T(8,128)S(1)}, f32[128,768]{1,0:T(8,128)S(1)}, u32[]{:S(2)}, u32[]{:S(2)}) collective-permute-start(f32[128,768]{1,0:T(8,128)S(1)} %get-tuple-element.629), channel_id=1, source_target_pairs={{0,4},{4,8},{8,12},{12,16},{16,20},{20,24},{24,28},{1,5},{5,9},{9,... | collective-permute-start | bytes 1179656 | tf_op jit(solution)/shard_map/ppermute | solution.py:698
  126.0 15.4 %collective-permute-start.9 = (f32[128,768]{1,0:T(8,128)S(1)}, f32[128,768]{1,0:T(8,128)S(1)}, u32[]{:S(2)}, u32[]{:S(2)}) collective-permute-start(f32[128,768]{1,0:T(8,128)S(1)} %get-tuple-element.640), channel_id=1, source_target_pairs={{0,4},{4,8},{8,12},{12,16},{16,20},{20,24},{24,28},{1,5},{5,9},{9,... | collective-permute-start | bytes 1179656 | tf_op jit(solution)/shard_map/ppermute | solution.py:698
  151.4 17.8 %collective-permute-start.11 = (f32[128,768]{1,0:T(8,128)S(1)}, f32[128,768]{1,0:T(8,128)S(1)}, u32[]{:S(2)}, u32[]{:S(2)}) collective-permute-start(f32[128,768]{1,0:T(8,128)S(1)} %get-tuple-element.662), channel_id=1, source_target_pairs={{0,4},{4,8},{8,12},{12,16},{16,20},{20,24},{24,28},{1,5},{5,9},{9,... | collective-permute-start | bytes 1179656 | tf_op jit(solution)/shard_map/ppermute | solution.py:698
  156.8 22.0 %collective-permute-start.12 = (f32[128,768]{1,0:T(8,128)S(1)}, f32[128,768]{1,0:T(8,128)S(1)}, u32[]{:S(2)}, u32[]{:S(2)}) collective-permute-start(f32[128,768]{1,0:T(8,128)S(1)} %get-tuple-element.673), channel_id=1, source_target_pairs={{0,4},{4,8},{8,12},{12,16},{16,20},{20,24},{24,28},{1,5},{5,9},{9,... | collective-permute-start | bytes 1179656 | tf_op jit(solution)/shard_map/ppermute | solution.py:698
  170.6 15.7 %collective-permute-start.13 = (f32[128,768]{1,0:T(8,128)S(1)}, f32[128,768]{1,0:T(8,128)S(1)}, u32[]{:S(2)}, u32[]{:S(2)}) collective-permute-start(f32[128,768]{1,0:T(8,128)S(1)} %get-tuple-element.684), channel_id=1, source_target_pairs={{0,4},{4,8},{8,12},{12,16},{16,20},{20,24},{24,28},{1,5},{5,9},{9,... | collective-permute-start | bytes 1179656 | tf_op jit(solution)/shard_map/ppermute | solution.py:698
  180.1 29.0 %collective-permute-start.14 = (f32[128,768]{1,0:T(8,128)S(1)}, f32[128,768]{1,0:T(8,128)S(1)}, u32[]{:S(2)}, u32[]{:S(2)}) collective-permute-start(f32[128,768]{1,0:T(8,128)S(1)} %get-tuple-element.695), channel_id=1, source_target_pairs={{0,4},{4,8},{8,12},{12,16},{16,20},{20,24},{24,28},{1,5},{5,9},{9,... | collective-permute-start | bytes 1179656 | tf_op jit(solution)/shard_map/ppermute | solution.py:698
  196.6 22.0 %collective-permute-start.15 = (f32[128,768]{1,0:T(8,128)S(1)}, f32[128,768]{1,0:T(8,128)S(1)}, u32[]{:S(2)}, u32[]{:S(2)}) collective-permute-start(f32[128,768]{1,0:T(8,128)S(1)} %get-tuple-element.706), channel_id=1, source_target_pairs={{0,4},{4,8},{8,12},{12,16},{16,20},{20,24},{24,28},{1,5},{5,9},{9,... | collective-permute-start | bytes 1179656 | tf_op jit(solution)/shard_map/ppermute | solution.py:698
  210.5 16.5 %collective-permute-start.16 = (f32[128,768]{1,0:T(8,128)S(1)}, f32[128,768]{1,0:T(8,128)S(1)}, u32[]{:S(2)}, u32[]{:S(2)}) collective-permute-start(f32[128,768]{1,0:T(8,128)S(1)} %get-tuple-element.717), channel_id=1, source_target_pairs={{0,4},{4,8},{8,12},{12,16},{16,20},{20,24},{24,28},{1,5},{5,9},{9,... | collective-permute-start | bytes 1179656 | tf_op jit(solution)/shard_map/ppermute | solution.py:698
  228.3 20.8 %collective-permute-start.18 = (f32[128,768]{1,0:T(8,128)S(1)}, f32[128,768]{1,0:T(8,128)S(1)}, u32[]{:S(2)}, u32[]{:S(2)}) collective-permute-start(f32[128,768]{1,0:T(8,128)S(1)} %get-tuple-element.739), channel_id=1, source_target_pairs={{0,4},{4,8},{8,12},{12,16},{16,20},{20,24},{24,28},{1,5},{5,9},{9,... | collective-permute-start | bytes 1179656 | tf_op jit(solution)/shard_map/ppermute | solution.py:698
  255.8 59.2 %collective-permute-start.21 = (f32[128,768]{1,0:T(8,128)S(1)}, f32[128,768]{1,0:T(8,128)}, u32[]{:S(2)}, u32[]{:S(2)}) collective-permute-start(f32[128,768]{1,0:T(8,128)S(1)} %get-tuple-element.772), channel_id=1, source_target_pairs={{0,4},{4,8},{8,12},{12,16},{16,20},{20,24},{24,28},{1,5},{5,9},{9,... | collective-permute-start | bytes 1179656 | tf_op jit(solution)/shard_map/ppermute | solution.py:698
  263.5 60.4 %collective-permute-start.22 = (f32[128,768]{1,0:T(8,128)}, f32[128,768]{1,0:T(8,128)S(1)}, u32[]{:S(2)}, u32[]{:S(2)}) collective-permute-start(f32[128,768]{1,0:T(8,128)} %get-tuple-element.783), channel_id=1, source_target_pairs={{0,4},{4,8},{8,12},{12,16},{16,20},{20,24},{24,28},{1,5},{5,9},{9,... | collective-permute-start | bytes 1179656 | tf_op jit(solution)/shard_map/ppermute | solution.py:698
  270.8 67.9 %collective-permute-start.23 = (f32[128,768]{1,0:T(8,128)}, f32[128,768]{1,0:T(8,128)}, u32[]{:S(2)}, u32[]{:S(2)}) collective-permute-start(f32[128,768]{1,0:T(8,128)} %get-tuple-element.563), channel_id=1, source_target_pairs={{4,0},{8,4},{12,8},{16,12},{20,16},{24,20},{28,24},{5,1},{9,5},{13... | collective-permute-start | bytes 1179656 | tf_op jit(solution)/shard_map/ppermute | solution.py:698
  337.2 18.0 %collective-permute-start.24 = (f32[128,768]{1,0:T(8,128)}, f32[128,768]{1,0:T(8,128)S(1)}, u32[]{:S(2)}, u32[]{:S(2)}) collective-permute-start(f32[128,768]{1,0:T(8,128)} %get-tuple-element.811), channel_id=1, source_target_pairs={{4,0},{8,4},{12,8},{16,12},{20,16},{24,20},{28,24},{5,1},{9,5},{13... | collective-permute-start | bytes 1179656 | tf_op jit(solution)/shard_map/ppermute | solution.py:698
  347.8 21.7 %collective-permute-start.25 = (f32[128,768]{1,0:T(8,128)S(1)}, f32[128,768]{1,0:T(8,128)S(1)}, u32[]{:S(2)}, u32[]{:S(2)}) collective-permute-start(f32[128,768]{1,0:T(8,128)S(1)} %get-tuple-element.819), channel_id=1, source_target_pairs={{4,0},{8,4},{12,8},{16,12},{20,16},{24,20},{28,24},{5,1},{9,5},{13... | collective-permute-start | bytes 1179656 | tf_op jit(solution)/shard_map/ppermute | solution.py:698
  450.2 65.0 %collective-permute-start.36 = (f32[128,768]{1,0:T(8,128)S(1)}, f32[128,768]{1,0:T(8,128)S(1)}, u32[]{:S(2)}, u32[]{:S(2)}) collective-permute-start(f32[128,768]{1,0:T(8,128)S(1)} %get-tuple-element.907), channel_id=1, source_target_pairs={{4,0},{8,4},{12,8},{16,12},{20,16},{24,20},{28,24},{5,1},{9,5},{13... | collective-permute-start | bytes 1179656 | tf_op jit(solution)/shard_map/ppermute | solution.py:698
  458.6 77.3 %collective-permute-start.37 = (f32[128,768]{1,0:T(8,128)S(1)}, f32[128,768]{1,0:T(8,128)S(1)}, u32[]{:S(2)}, u32[]{:S(2)}) collective-permute-start(f32[128,768]{1,0:T(8,128)S(1)} %get-tuple-element.915), channel_id=1, source_target_pairs={{4,0},{8,4},{12,8},{16,12},{20,16},{24,20},{28,24},{5,1},{9,5},{13... | collective-permute-start | bytes 1179656 | tf_op jit(solution)/shard_map/ppermute | solution.py:698
  533.7 22.8 %collective-permute-start.38 = (f32[128,768]{1,0:T(8,128)S(1)}, f32[128,768]{1,0:T(8,128)S(1)}, u32[]{:S(2)}, u32[]{:S(2)}) collective-permute-start(f32[128,768]{1,0:T(8,128)S(1)} %get-tuple-element.923), channel_id=1, source_target_pairs={{4,0},{8,4},{12,8},{16,12},{20,16},{24,20},{28,24},{5,1},{9,5},{13... | collective-permute-start | bytes 1179656 | tf_op jit(solution)/shard_map/ppermute | solution.py:698
  553.6 22.4 %collective-permute-start.39 = (f32[128,768]{1,0:T(8,128)S(1)}, f32[128,768]{1,0:T(8,128)S(1)}, u32[]{:S(2)}, u32[]{:S(2)}) collective-permute-start(f32[128,768]{1,0:T(8,128)S(1)} %get-tuple-element.931), channel_id=1, source_target_pairs={{4,0},{8,4},{12,8},{16,12},{20,16},{24,20},{28,24},{5,1},{9,5},{13... | collective-permute-start | bytes 1179656 | tf_op jit(solution)/shard_map/ppermute | solution.py:698
  574.2 21.9 %collective-permute-start.40 = (f32[128,768]{1,0:T(8,128)S(1)}, f32[128,768]{1,0:T(8,128)S(1)}, u32[]{:S(2)}, u32[]{:S(2)}) collective-permute-start(f32[128,768]{1,0:T(8,128)S(1)} %get-tuple-element.939), channel_id=1, source_target_pairs={{4,0},{8,4},{12,8},{16,12},{20,16},{24,20},{28,24},{5,1},{9,5},{13... | collective-permute-start | bytes 1179656 | tf_op jit(solution)/shard_map/ppermute | solution.py:698
  594.3 21.9 %collective-permute-start.41 = (f32[128,768]{1,0:T(8,128)S(1)}, f32[128,768]{1,0:T(8,128)S(1)}, u32[]{:S(2)}, u32[]{:S(2)}) collective-permute-start(f32[128,768]{1,0:T(8,128)S(1)} %get-tuple-element.947), channel_id=1, source_target_pairs={{4,0},{8,4},{12,8},{16,12},{20,16},{24,20},{28,24},{5,1},{9,5},{13... | collective-permute-start | bytes 1179656 | tf_op jit(solution)/shard_map/ppermute | solution.py:698
  613.8 21.9 %collective-permute-start.42 = (f32[128,768]{1,0:T(8,128)S(1)}, f32[128,768]{1,0:T(8,128)S(1)}, u32[]{:S(2)}, u32[]{:S(2)}) collective-permute-start(f32[128,768]{1,0:T(8,128)S(1)} %get-tuple-element.955), channel_id=1, source_target_pairs={{4,0},{8,4},{12,8},{16,12},{20,16},{24,20},{28,24},{5,1},{9,5},{13... | collective-permute-start | bytes 1179656 | tf_op jit(solution)/shard_map/ppermute | solution.py:698
  633.9 25.0 %collective-permute-start.43 = (f32[128,768]{1,0:T(8,128)S(1)}, f32[128,768]{1,0:T(8,128)S(1)}, u32[]{:S(2)}, u32[]{:S(2)}) collective-permute-start(f32[128,768]{1,0:T(8,128)S(1)} %get-tuple-element.963), channel_id=1, source_target_pairs={{4,0},{8,4},{12,8},{16,12},{20,16},{24,20},{28,24},{5,1},{9,5},{13... | collective-permute-start | bytes 1179656 | tf_op jit(solution)/shard_map/ppermute | solution.py:698
  703.3 42.0 %collective-permute-start.51 = (f32[2,768,768]{2,1,0:T(8,128)}, f32[2,768,768]{2,1,0:T(8,128)}, u32[]{:S(2)}, u32[]{:S(2)}) collective-permute-start(f32[2,768,768]{2,1,0:T(8,128)} %fusion.2), channel_id=1, source_target_pairs={{0,1},{1,0},{2,3},{3,2},{4,5},{5,4},{6,7},{7,6},{8,9},{9,8},{10,11... | collective-permute-start | bytes 14155784 | tf_op jit(solution)/shard_map/ppermute | solution.py:742
  712.5 23.5 %collective-permute-start.48 = (f32[2,192,2304]{2,1,0:T(8,128)}, f32[2,192,2304]{2,1,0:T(8,128)}, u32[]{:S(2)}, u32[]{:S(2)}) collective-permute-start(f32[2,192,2304]{2,1,0:T(8,128)} %fusion.13), channel_id=1, source_target_pairs={{0,1},{1,0},{2,3},{3,2},{4,5},{5,4},{6,7},{7,6},{8,9},{9,8},{10,11... | collective-permute-start | bytes 10616840 | tf_op jit(solution)/shard_map/ppermute | solution.py:742
  712.5 41.5 %collective-permute-start.50 = (f32[2,192,3072]{2,1,0:T(8,128)}, f32[2,192,3072]{2,1,0:T(8,128)}, u32[]{:S(2)}, u32[]{:S(2)}) collective-permute-start(f32[2,192,3072]{2,1,0:T(8,128)} %fusion.15), channel_id=1, source_target_pairs={{0,1},{1,0},{2,3},{3,2},{4,5},{5,4},{6,7},{7,6},{8,9},{9,8},{10,11... | collective-permute-start | bytes 14155784 | tf_op jit(solution)/shard_map/ppermute | solution.py:742
  (150 other events, 2004.7 us)

commit v5 on v4

--- a/solution.py
+++ b/solution.py
@@ -10,7 +10,7 @@
 HEAD_DIM = 64
 LAYERS = 2
 PAIR = 2 * HEAD_DIM
-SCOPED = 10368 * 1024
+SCOPED = 10752 * 1024
 EPS = 1e-05
 BF16 = jnp.bfloat16
 F32 = jnp.float32
@@ -139,7 +139,7 @@
 
 
 def turn_kernel(blocks, width, late, *refs):
-    weights, turned, before_v, after_v, in_sem, out_sem = refs[:4], *refs[5:]
+    weights, turned, before_v, after_v, in_sem, out_sem = refs[:4], *refs[6:]
     section = lax.axis_index("section")
     half = lax.axis_size("section") // 2
     chosen = section < half if late else section >= half
@@ -176,12 +176,12 @@
         keep(len(turns) - 1).wait()
 
 
-def turn_weights(weights, turned, late):
+def turn_weights(weights, turned, tick, late):
     width = weights[1].shape[-1]
     return pl.pallas_call(
         partial(turn_kernel, weight_blocks(weights), width, late),
         out_shape=pltpu.HBM(turned.shape, BF16),
-        in_specs=[ANY] * 4 + [HBM],
+        in_specs=[ANY] * 4 + [HBM, ANY],
         out_specs=HBM,
         scratch_shapes=[
             pltpu.VMEM((2, width, width), BF16),
@@ -192,7 +192,7 @@
         input_output_aliases={4: 0},
         compiler_params=pltpu.CompilerParams(vmem_limit_bytes=SCOPED),
         name="turn_weights",
-    )(*map(in_hbm, weights), in_hbm(turned))
+    )(*map(in_hbm, weights), in_hbm(turned), tick)
 
 
 def in_hbm(value):
@@ -671,7 +671,7 @@
     vectors, allowed, even, arrives, first, where, weights = lax.optimization_barrier(
         ((vecs, bj, be), allowed, even, arrives, first, (section, group, member), weights)
     )
-    turned = turn_weights(weights, made[-3], False)
+    turned = turn_weights(weights, made[-3], jnp.zeros((1,), jnp.int32), False)
     weights, turned = lax.optimization_barrier((weights, turned))
     loaded = load_weights(weights)
     chunk = min(ticks, UNROLL)
@@ -695,7 +695,8 @@
         def turn(carry, source_of):
             stash, sent, arrived, tick = carry
             for index in range(chunk):
-                arriving = lax.ppermute(sent, "section", pairs)
+                idle = rounds == 1 and index == 0
+                arriving = arrived if idle else lax.ppermute(sent, "section", pairs)
                 stash, sent, tick = step(tick, source_of(index), arrived, stash)
                 arrived = arriving
             return stash, sent, arrived, tick
@@ -717,8 +718,7 @@
         forward_stash,
     )
     sh, sg, sa, st, so, sc, sm, sd, final_rows = forward_stash
-    weights, turned, _ = lax.optimization_barrier((weights, turned, walked))
-    loaded = load_turned(turn_weights(weights, turned, True))
+    loaded = load_turned(turn_weights(weights, turned, walked, True))
     backward_stash, walked = run(
         lambda tick, source, arrived, stash: backward_step(
             branch_scale, tick, source, arrived, allowed, loaded, vectors[0], (sh, sg, st, sd), stash

time: 773 us -> 769 us (level)
  local copies, waits for them, and re-layouts: 37.7 us -> 19.9 us
  Pallas kernels: 395 us -> 409 us
  starting transfers between devices: 126 us -> 137 us
  waiting for transfers between devices: 134 us -> 125 us
    unnamed x263 -> x197, local copies, waits for them, and re-layouts: 28.7 us -> 11 us
    ppermute x42 -> x40, starting transfers between devices: 117 us -> 127 us  [turn(): arriving = arrived if idle else lax.ppermute(sent, 'section', pairs)]
    ppermute x42 -> x40, waiting for transfers between devices: 126 us -> 117 us  [turn(): arriving = arrived if idle else lax.ppermute(sent, 'section', pairs)]
  transfers between devices with their start and end apart: 52 -> 50, of which waited for: 27 -> 26; matrix products, arithmetic and copies ran while one was open for 9% -> 8% of each run, Pallas kernels for 50% -> 45%
where the time goes in v5:
time: 769 us; the launch traced here: 757 us
  Pallas kernels  409 us (53%)
  starting transfers between devices  137 us (18%)
  waiting for transfers between devices  125 us (16%)
  matrix products  55.1 us (7%)
  local copies, waits for them, and re-layouts  19.9 us (3%)
  other arithmetic  8.46 us (1%)
    pallas_call x22, Pallas kernels, backward_step(): pl.pallas_call(partial(backward_kernel, branch_scale, joint_count, hidden...  201 us
    pallas_call x22, Pallas kernels, forward_step(): pl.pallas_call(partial(forward_kernel, branch_scale, joint_count, hidden_...  156 us
    ppermute x40, starting transfers between devices, turn(): arriving = arrived if idle else lax.ppermute(sent, 'section', pairs)  127 us
    ppermute x40, waiting for transfers between devices, turn(): arriving = arrived if idle else lax.ppermute(sent, 'section', pairs)  117 us
    dot_general x8, matrix products, part(): return jnp.einsum('lrd,lre->lde', mine, right, preferred_element_type=F32)  55.1 us
    pallas_call x2, Pallas kernels, turn_weights(): pl.pallas_call(partial(turn_kernel, weight_blocks(weights), width, late),...  32.6 us
  transfers between devices with their start and end apart: 50, of which 26 were waited for; matrix products, arithmetic and copies ran while one was open for 8% of the time, Pallas kernels for 45%

profile of v5, /device:TPU:0, one launch (start us, length us, event | category | flops | bytes accessed | tf_op | source)
XLA Modules:
  0.0 756.8 jit_solution(2172493365390799695)
XLA Ops:
  9.2 9.6 %load_weights.1 = (bf16[2,768,768]{2,1,0:T(8,128)(2,1)S(1)}, bf16[2,768,768]{2,1,0:T(8,128)(2,1)S(1)}, bf16[2,768,768]{2,1,0:T(8,128)(2,1)S(1)}, bf16[2,768,768]...) custom-call(bf16[2,768,2304]{2,1,0:T(8,128)(2,1)} %refs_0_.2, ...), custom_call_target="tpu_custom_call" | custom-call | tf_op jit(solution)/shard_map/load_weights/pallas_call | solution.py:105
  18.8 12.2 %forward_step.22 = (f32[2,8,128,768]{3,2,1,0:T(8,128)}, f32[2,8,128,768]{3,2,1,0:T(8,128)}, bf16[2,8,128,768]{3,2,1,0:T(8,128)(2,1)}, bf16[2,8,128,2304]{3,2,1,0...) custom-call(s32[1]{0:T(128)} %constant.91.clone.1.refs_5_.tick, ...), custom_call_target="tpu_custom_call", output_to_operand_aliasing={{0}: (19, {}), {1}: (20, {}), {2}: (21, {}), {3}: (22, {}),... | custom-call | flops 3623878656 | bytes 28311552 | tf_op jit(solution)/shard_map/forward_step/pallas_call | solution.py:347
  32.4 13.0 %forward_step.23 = (f32[2,8,128,768]{3,2,1,0:T(8,128)}, f32[2,8,128,768]{3,2,1,0:T(8,128)}, bf16[2,8,128,768]{3,2,1,0:T(8,128)(2,1)}, bf16[2,8,128,2304]{3,2,1,0...) custom-call(s32[1]{0:T(128)} %get-tuple-element.542.tick, ...), custom_call_target="tpu_custom_call", output_to_operand_aliasing={{0}: (19, {}), {1}: (20, {}), {2}: (21, {}), {3}: (22, {}),... | custom-call | flops 3623878656 | bytes 28311552 | tf_op jit(solution)/shard_map/forward_step/pallas_call | solution.py:347
  46.8 12.8 %forward_step.24 = (f32[2,8,128,768]{3,2,1,0:T(8,128)}, f32[2,8,128,768]{3,2,1,0:T(8,128)}, bf16[2,8,128,768]{3,2,1,0:T(8,128)(2,1)}, bf16[2,8,128,2304]{3,2,1,0...) custom-call(s32[1]{0:T(128)} %get-tuple-element.552.tick, ...), custom_call_target="tpu_custom_call", output_to_operand_aliasing={{0}: (19, {}), {1}: (20, {}), {2}: (21, {}), {3}: (22, {}),... | custom-call | flops 3623878656 | bytes 28311552 | tf_op jit(solution)/shard_map/forward_step/pallas_call | solution.py:347
  60.9 12.8 %forward_step.25 = (f32[2,8,128,768]{3,2,1,0:T(8,128)}, f32[2,8,128,768]{3,2,1,0:T(8,128)}, bf16[2,8,128,768]{3,2,1,0:T(8,128)(2,1)}, bf16[2,8,128,2304]{3,2,1,0...) custom-call(s32[1]{0:T(128)} %get-tuple-element.563.tick, ...), custom_call_target="tpu_custom_call", output_to_operand_aliasing={{0}: (19, {}), {1}: (20, {}), {2}: (21, {}), {3}: (22, {}),... | custom-call | flops 3623878656 | bytes 28311552 | tf_op jit(solution)/shard_map/forward_step/pallas_call | solution.py:347
  73.8 13.7 %collective-permute-start.5 = (f32[128,768]{1,0:T(8,128)S(1)}, f32[128,768]{1,0:T(8,128)S(1)}, u32[]{:S(2)}, u32[]{:S(2)}) collective-permute-start(f32[128,768]{1,0:T(8,128)S(1)} %get-tuple-element.586), channel_id=1, source_target_pairs={{0,4},{4,8},{8,12},{12,16},{16,20},{20,24},{24,28},{1,5},{5,9},{9,... | collective-permute-start | bytes 1179656 | tf_op jit(solution)/shard_map/ppermute | solution.py:699
  88.6 12.8 %forward_step.26 = (f32[2,8,128,768]{3,2,1,0:T(8,128)}, f32[2,8,128,768]{3,2,1,0:T(8,128)}, bf16[2,8,128,768]{3,2,1,0:T(8,128)(2,1)}, bf16[2,8,128,2304]{3,2,1,0...) custom-call(s32[1]{0:T(128)} %get-tuple-element.574.tick, ...), custom_call_target="tpu_custom_call", output_to_operand_aliasing={{0}: (19, {}), {1}: (20, {}), {2}: (21, {}), {3}: (22, {}),... | custom-call | flops 3623878656 | bytes 28311552 | tf_op jit(solution)/shard_map/forward_step/pallas_call | solution.py:347
  102.7 12.9 %forward_step.27 = (f32[2,8,128,768]{3,2,1,0:T(8,128)}, f32[2,8,128,768]{3,2,1,0:T(8,128)}, bf16[2,8,128,768]{3,2,1,0:T(8,128)(2,1)}, bf16[2,8,128,2304]{3,2,1,0...) custom-call(s32[1]{0:T(128)} %get-tuple-element.585.tick, ...), custom_call_target="tpu_custom_call", output_to_operand_aliasing={{0}: (19, {}), {1}: (20, {}), {2}: (21, {}), {3}: (22, {}),... | custom-call | flops 3623878656 | bytes 28311552 | tf_op jit(solution)/shard_map/forward_step/pallas_call | solution.py:347
  117.8 12.8 %forward_step.28 = (f32[2,8,128,768]{3,2,1,0:T(8,128)}, f32[2,8,128,768]{3,2,1,0:T(8,128)}, bf16[2,8,128,768]{3,2,1,0:T(8,128)(2,1)}, bf16[2,8,128,2304]{3,2,1,0...) custom-call(s32[1]{0:T(128)} %get-tuple-element.596.tick, ...), custom_call_target="tpu_custom_call", output_to_operand_aliasing={{0}: (19, {}), {1}: (20, {}), {2}: (21, {}), {3}: (22, {}),... | custom-call | flops 3623878656 | bytes 28311552 | tf_op jit(solution)/shard_map/forward_step/pallas_call | solution.py:347
  131.9 12.7 %forward_step.29 = (f32[2,8,128,768]{3,2,1,0:T(8,128)}, f32[2,8,128,768]{3,2,1,0:T(8,128)}, bf16[2,8,128,768]{3,2,1,0:T(8,128)(2,1)}, bf16[2,8,128,2304]{3,2,1,0...) custom-call(s32[1]{0:T(128)} %get-tuple-element.607.tick, ...), custom_call_target="tpu_custom_call", output_to_operand_aliasing={{0}: (19, {}), {1}: (20, {}), {2}: (21, {}), {3}: (22, {}),... | custom-call | flops 3623878656 | bytes 28311552 | tf_op jit(solution)/shard_map/forward_step/pallas_call | solution.py:347
  147.4 12.3 %collective-permute-start.10 = (f32[128,768]{1,0:T(8,128)S(1)}, f32[128,768]{1,0:T(8,128)S(1)}, u32[]{:S(2)}, u32[]{:S(2)}) collective-permute-start(f32[128,768]{1,0:T(8,128)S(1)} %get-tuple-element.641), channel_id=1, source_target_pairs={{0,4},{4,8},{8,12},{12,16},{16,20},{20,24},{24,28},{1,5},{5,9},{9,... | collective-permute-start | bytes 1179656 | tf_op jit(solution)/shard_map/ppermute | solution.py:699
  159.7 10.0 %forward_step.31 = (f32[2,8,128,768]{3,2,1,0:T(8,128)}, f32[2,8,128,768]{3,2,1,0:T(8,128)}, bf16[2,8,128,768]{3,2,1,0:T(8,128)(2,1)}, bf16[2,8,128,2304]{3,2,1,0...) custom-call(s32[1]{0:T(128)} %get-tuple-element.629.tick, ...), custom_call_target="tpu_custom_call", output_to_operand_aliasing={{0}: (19, {}), {1}: (20, {}), {2}: (21, {}), {3}: (22, {}),... | custom-call | flops 3623878656 | bytes 28311552 | tf_op jit(solution)/shard_map/forward_step/pallas_call | solution.py:347
  192.7 12.5 %collective-permute-start.14 = (f32[128,768]{1,0:T(8,128)S(1)}, f32[128,768]{1,0:T(8,128)S(1)}, u32[]{:S(2)}, u32[]{:S(2)}) collective-permute-start(f32[128,768]{1,0:T(8,128)S(1)} %get-tuple-element.685), channel_id=1, source_target_pairs={{0,4},{4,8},{8,12},{12,16},{16,20},{20,24},{24,28},{1,5},{5,9},{9,... | collective-permute-start | bytes 1179656 | tf_op jit(solution)/shard_map/ppermute | solution.py:699
  205.2 10.2 %forward_step.35 = (f32[2,8,128,768]{3,2,1,0:T(8,128)}, f32[2,8,128,768]{3,2,1,0:T(8,128)}, bf16[2,8,128,768]{3,2,1,0:T(8,128)(2,1)}, bf16[2,8,128,2304]{3,2,1,0...) custom-call(s32[1]{0:T(128)} %get-tuple-element.673.tick, ...), custom_call_target="tpu_custom_call", output_to_operand_aliasing={{0}: (19, {}), {1}: (20, {}), {2}: (21, {}), {3}: (22, {}),... | custom-call | flops 3623878656 | bytes 28311552 | tf_op jit(solution)/shard_map/forward_step/pallas_call | solution.py:347
  248.3 9.9 %forward_step.39 = (f32[2,8,128,768]{3,2,1,0:T(8,128)}, f32[2,8,128,768]{3,2,1,0:T(8,128)}, bf16[2,8,128,768]{3,2,1,0:T(8,128)(2,1)}, bf16[2,8,128,2304]{3,2,1,0...) custom-call(s32[1]{0:T(128)} %get-tuple-element.717.tick, ...), custom_call_target="tpu_custom_call", output_to_operand_aliasing={{0}: (19, {}), {1}: (20, {}), {2}: (21, {}), {3}: (22, {}),... | custom-call | flops 3623878656 | bytes 28311552 | tf_op jit(solution)/shard_map/forward_step/pallas_call | solution.py:347
  283.8 10.1 %forward_step.43 = (f32[2,8,128,768]{3,2,1,0:T(8,128)}, f32[2,8,128,768]{3,2,1,0:T(8,128)}, bf16[2,8,128,768]{3,2,1,0:T(8,128)(2,1)}, bf16[2,8,128,2304]{3,2,1,0...) custom-call(s32[1]{0:T(128)} %get-tuple-element.761.tick, ...), custom_call_target="tpu_custom_call", output_to_operand_aliasing={{0}: (19, {}), {1}: (20, {}), {2}: (21, {}), {3}: (22, {}),... | custom-call | flops 3623878656 | bytes 28311552 | tf_op jit(solution)/shard_map/forward_step/pallas_call | solution.py:347
  293.8 32.5 %turn_weights.3.source = bf16[12,2,768,768]{3,2,1,0:T(8,128)(2,1)} custom-call(bf16[2,768,2304]{2,1,0:T(8,128)(2,1)} %refs_0_.2, bf16[2,768,768]{2,1,0:T(8,128)(2,1)} %refs_1_.2, bf16[2,768,3072]{2,1,0:T(8,128)(2,1)} %refs_2_.2, bf16[2,3072,768]{2,1,0:T(8,128)(2,1)} %refs_3_.2, ...), custom_call_target="tpu_custom_call", output_to_operand_aliasing={{}: (4, {})} | custom-call | tf_op jit(solution)/shard_map/turn_weights/pallas_call | solution.py:181
  326.4 9.3 %load_turned.1 = (bf16[2,768,768]{2,1,0:T(8,128)(2,1)S(1)}, bf16[2,768,768]{2,1,0:T(8,128)(2,1)S(1)}, bf16[2,768,768]{2,1,0:T(8,128)(2,1)S(1)}, bf16[2,768,768]{...) custom-call(bf16[12,2,768,768]{3,2,1,0:T(8,128)(2,1)} %turn_weights., ...), custom_call_target="tpu_custom_call" | custom-call | tf_op jit(solution)/shard_map/load_turned/pallas_call | solution.py:130
  351.5 9.5 %collective-permute-done.23.arrived = f32[128,768]{1,0:T(8,128)S(1)} collective-permute-done((f32[128,768]{1,0:T(8,128)S(1)}, f32[128,768]{1,0:T(8,128)S(1)}, u32[]{:S(2)}, u32[]{:S(2)}) %collective-permute-start.23) | collective-permute-done | bytes 393248 | tf_op jit(solution)/shard_map/ppermute | solution.py:699
  375.1 9.5 %backward_step.26 = (bf16[2,8,128,768]{3,2,1,0:T(8,128)(2,1)}, bf16[2,8,128,3072]{3,2,1,0:T(8,128)(2,1)}, bf16[2,8,128,768]{3,2,1,0:T(8,128)(2,1)}, bf16[2,8,128...) custom-call(s32[1]{0:T(128)} %get-tuple-element.818.tick, ...), custom_call_target="tpu_custom_call", output_to_operand_aliasing={{0}: (21, {}), {1}: (22, {}), {2}: (23, {}), {3}: (24, {}),... | custom-call | flops 3623878656 | bytes 28311552 | tf_op jit(solution)/shard_map/backward_step/pallas_call | solution.py:532
  389.1 10.4 %collective-permute-done.26.arrived = f32[128,768]{1,0:T(8,128)S(1)} collective-permute-done((f32[128,768]{1,0:T(8,128)S(1)}, f32[128,768]{1,0:T(8,128)S(1)}, u32[]{:S(2)}, u32[]{:S(2)}) %collective-permute-start.26) | collective-permute-done | bytes 393248 | tf_op jit(solution)/shard_map/ppermute | solution.py:699
  429.0 9.5 %backward_step.32 = (bf16[2,8,128,768]{3,2,1,0:T(8,128)(2,1)}, bf16[2,8,128,3072]{3,2,1,0:T(8,128)(2,1)}, bf16[2,8,128,768]{3,2,1,0:T(8,128)(2,1)}, bf16[2,8,128...) custom-call(s32[1]{0:T(128)} %get-tuple-element.866.tick, ...), custom_call_target="tpu_custom_call", output_to_operand_aliasing={{0}: (21, {}), {1}: (22, {}), {2}: (23, {}), {3}: (24, {}),... | custom-call | flops 3623878656 | bytes 28311552 | tf_op jit(solution)/shard_map/backward_step/pallas_call | solution.py:532
  463.7 54.0 %collective-permute-done.34.arrived = f32[128,768]{1,0:T(8,128)S(1)} collective-permute-done((f32[128,768]{1,0:T(8,128)S(1)}, f32[128,768]{1,0:T(8,128)S(1)}, u32[]{:S(2)}, u32[]{:S(2)}) %collective-permute-start.34) | collective-permute-done | bytes 393248 | tf_op jit(solution)/shard_map/ppermute | solution.py:699
  517.7 17.6 %backward_step.36 = (bf16[2,8,128,768]{3,2,1,0:T(8,128)(2,1)}, bf16[2,8,128,3072]{3,2,1,0:T(8,128)(2,1)}, bf16[2,8,128,768]{3,2,1,0:T(8,128)(2,1)}, bf16[2,8,128...) custom-call(s32[1]{0:T(128)} %get-tuple-element.898.tick, ...), custom_call_target="tpu_custom_call", output_to_operand_aliasing={{0}: (21, {}), {1}: (22, {}), {2}: (23, {}), {3}: (24, {}),... | custom-call | flops 3623878656 | bytes 28311552 | tf_op jit(solution)/shard_map/backward_step/pallas_call | solution.py:532
  538.3 17.6 %backward_step.37 = (bf16[2,8,128,768]{3,2,1,0:T(8,128)(2,1)}, bf16[2,8,128,3072]{3,2,1,0:T(8,128)(2,1)}, bf16[2,8,128,768]{3,2,1,0:T(8,128)(2,1)}, bf16[2,8,128...) custom-call(s32[1]{0:T(128)} %get-tuple-element.906.tick, ...), custom_call_target="tpu_custom_call", output_to_operand_aliasing={{0}: (21, {}), {1}: (22, {}), {2}: (23, {}), {3}: (24, {}),... | custom-call | flops 3623878656 | bytes 28311552 | tf_op jit(solution)/shard_map/backward_step/pallas_call | solution.py:532
  557.3 18.5 %backward_step.38 = (bf16[2,8,128,768]{3,2,1,0:T(8,128)(2,1)}, bf16[2,8,128,3072]{3,2,1,0:T(8,128)(2,1)}, bf16[2,8,128,768]{3,2,1,0:T(8,128)(2,1)}, bf16[2,8,128...) custom-call(s32[1]{0:T(128)} %get-tuple-element.914.tick, ...), custom_call_target="tpu_custom_call", output_to_operand_aliasing={{0}: (21, {}), {1}: (22, {}), {2}: (23, {}), {3}: (24, {}),... | custom-call | flops 3623878656 | bytes 28311552 | tf_op jit(solution)/shard_map/backward_step/pallas_call | solution.py:532
  577.2 17.6 %backward_step.39 = (bf16[2,8,128,768]{3,2,1,0:T(8,128)(2,1)}, bf16[2,8,128,3072]{3,2,1,0:T(8,128)(2,1)}, bf16[2,8,128,768]{3,2,1,0:T(8,128)(2,1)}, bf16[2,8,128...) custom-call(s32[1]{0:T(128)} %get-tuple-element.922.tick, ...), custom_call_target="tpu_custom_call", output_to_operand_aliasing={{0}: (21, {}), {1}: (22, {}), {2}: (23, {}), {3}: (24, {}),... | custom-call | flops 3623878656 | bytes 28311552 | tf_op jit(solution)/shard_map/backward_step/pallas_call | solution.py:532
  598.3 17.6 %backward_step.40 = (bf16[2,8,128,768]{3,2,1,0:T(8,128)(2,1)}, bf16[2,8,128,3072]{3,2,1,0:T(8,128)(2,1)}, bf16[2,8,128,768]{3,2,1,0:T(8,128)(2,1)}, bf16[2,8,128...) custom-call(s32[1]{0:T(128)} %get-tuple-element.930.tick, ...), custom_call_target="tpu_custom_call", output_to_operand_aliasing={{0}: (21, {}), {1}: (22, {}), {2}: (23, {}), {3}: (24, {}),... | custom-call | flops 3623878656 | bytes 28311552 | tf_op jit(solution)/shard_map/backward_step/pallas_call | solution.py:532
  617.8 18.3 %backward_step.41 = (bf16[2,8,128,768]{3,2,1,0:T(8,128)(2,1)}, bf16[2,8,128,3072]{3,2,1,0:T(8,128)(2,1)}, bf16[2,8,128,768]{3,2,1,0:T(8,128)(2,1)}, bf16[2,8,128...) custom-call(s32[1]{0:T(128)} %get-tuple-element.938.tick, ...), custom_call_target="tpu_custom_call", output_to_operand_aliasing={{0}: (21, {}), {1}: (22, {}), {2}: (23, {}), {3}: (24, {}),... | custom-call | flops 3623878656 | bytes 28311552 | tf_op jit(solution)/shard_map/backward_step/pallas_call | solution.py:532
  637.5 17.2 %backward_step.42 = (bf16[2,8,128,768]{3,2,1,0:T(8,128)(2,1)}, bf16[2,8,128,3072]{3,2,1,0:T(8,128)(2,1)}, bf16[2,8,128,768]{3,2,1,0:T(8,128)(2,1)}, bf16[2,8,128...) custom-call(s32[1]{0:T(128)} %get-tuple-element.946.tick, ...), custom_call_target="tpu_custom_call", output_to_operand_aliasing={{0}: (21, {}), {1}: (22, {}), {2}: (23, {}), {3}: (24, {}),... | custom-call | flops 3623878656 | bytes 28311552 | tf_op jit(solution)/shard_map/backward_step/pallas_call | solution.py:532
  654.8 17.4 %backward_step.43 = (bf16[2,8,128,768]{3,2,1,0:T(8,128)(2,1)}, bf16[2,8,128,3072]{3,2,1,0:T(8,128)(2,1)}, bf16[2,8,128,768]{3,2,1,0:T(8,128)(2,1)}, bf16[2,8,128...) custom-call(s32[1]{0:T(128)} %get-tuple-element.954.tick, ...), custom_call_target="tpu_custom_call", output_to_operand_aliasing={{0}: (21, {}), {1}: (22, {}), {2}: (23, {}), {3}: (24, {}),... | custom-call | flops 3623878656 | bytes 28311552 | tf_op jit(solution)/shard_map/backward_step/pallas_call | solution.py:532
  688.9 10.1 %fusion.15 = f32[2,192,3072]{2,1,0:T(8,128)} fusion(bf16[2,1024,3072]{2,1,0:T(8,128)(2,1)} %bitcast.37, bf16[2,1024,768]{2,1,0:T(8,128)(2,1)} %bitcast.53, s32[]{:T(128)S(6)} %select_n.158), kind=kOutput, calls=%fused_computation.18 | convolution fusion | flops 2415919104 | bytes 18350084 | tf_op jit(solution)/shard_map/lrd,lre->lde/dot_general | solution.py:757
  (370 shorter events, 276.6 us)
Async XLA Ops:
  6.2 81.3 %collective-permute-start.3 = (f32[4,128,768]{2,1,0:T(8,128)S(1)}, f32[4,128,768]{2,1,0:T(8,128)S(1)}, u32[]{:S(2)}, u32[]{:S(2)}) collective-permute-start(f32[4,128,768]{2,1,0:T(8,128)S(1)} %fusion.7.tokens.seeds), channel_id=1, source_target_pairs={{2,0},{3,1},{0,2},{1,3},{30,28},{31,29},{28,30},{29,31}} | collective-permute-start | bytes 4718600 | tf_op jit(solution)/shard_map/ppermute | solution.py:606
  31.1 15.7 %collective-permute-start.1 = (f32[128,768]{1,0:T(8,128)S(1)}, f32[128,768]{1,0:T(8,128)S(1)}, u32[]{:S(2)}, u32[]{:S(2)}) collective-permute-start(f32[128,768]{1,0:T(8,128)S(1)} %get-tuple-element.553), channel_id=1, source_target_pairs={{0,4},{4,8},{8,12},{12,16},{16,20},{20,24},{24,28},{1,5},{5,9},{9,... | collective-permute-start | bytes 1179656 | tf_op jit(solution)/shard_map/ppermute | solution.py:699
  45.4 15.5 %collective-permute-start.2 = (f32[128,768]{1,0:T(8,128)S(1)}, f32[128,768]{1,0:T(8,128)S(1)}, u32[]{:S(2)}, u32[]{:S(2)}) collective-permute-start(f32[128,768]{1,0:T(8,128)S(1)} %get-tuple-element.564), channel_id=1, source_target_pairs={{0,4},{4,8},{8,12},{12,16},{16,20},{20,24},{24,28},{1,5},{5,9},{9,... | collective-permute-start | bytes 1179656 | tf_op jit(solution)/shard_map/ppermute | solution.py:699
  59.6 27.9 %collective-permute-start.4 = (f32[128,768]{1,0:T(8,128)S(1)}, f32[128,768]{1,0:T(8,128)S(1)}, u32[]{:S(2)}, u32[]{:S(2)}) collective-permute-start(f32[128,768]{1,0:T(8,128)S(1)} %get-tuple-element.575), channel_id=1, source_target_pairs={{0,4},{4,8},{8,12},{12,16},{16,20},{20,24},{24,28},{1,5},{5,9},{9,... | collective-permute-start | bytes 1179656 | tf_op jit(solution)/shard_map/ppermute | solution.py:699
  73.8 29.0 %collective-permute-start.5 = (f32[128,768]{1,0:T(8,128)S(1)}, f32[128,768]{1,0:T(8,128)S(1)}, u32[]{:S(2)}, u32[]{:S(2)}) collective-permute-start(f32[128,768]{1,0:T(8,128)S(1)} %get-tuple-element.586), channel_id=1, source_target_pairs={{0,4},{4,8},{8,12},{12,16},{16,20},{20,24},{24,28},{1,5},{5,9},{9,... | collective-permute-start | bytes 1179656 | tf_op jit(solution)/shard_map/ppermute | solution.py:699
  101.4 16.4 %collective-permute-start.6 = (f32[128,768]{1,0:T(8,128)S(1)}, f32[128,768]{1,0:T(8,128)S(1)}, u32[]{:S(2)}, u32[]{:S(2)}) collective-permute-start(f32[128,768]{1,0:T(8,128)S(1)} %get-tuple-element.597), channel_id=1, source_target_pairs={{0,4},{4,8},{8,12},{12,16},{16,20},{20,24},{24,28},{1,5},{5,9},{9,... | collective-permute-start | bytes 1179656 | tf_op jit(solution)/shard_map/ppermute | solution.py:699
  115.7 16.3 %collective-permute-start.7 = (f32[128,768]{1,0:T(8,128)S(1)}, f32[128,768]{1,0:T(8,128)S(1)}, u32[]{:S(2)}, u32[]{:S(2)}) collective-permute-start(f32[128,768]{1,0:T(8,128)S(1)} %get-tuple-element.608), channel_id=1, source_target_pairs={{0,4},{4,8},{8,12},{12,16},{16,20},{20,24},{24,28},{1,5},{5,9},{9,... | collective-permute-start | bytes 1179656 | tf_op jit(solution)/shard_map/ppermute | solution.py:699
  130.6 15.4 %collective-permute-start.8 = (f32[128,768]{1,0:T(8,128)S(1)}, f32[128,768]{1,0:T(8,128)S(1)}, u32[]{:S(2)}, u32[]{:S(2)}) collective-permute-start(f32[128,768]{1,0:T(8,128)S(1)} %get-tuple-element.619), channel_id=1, source_target_pairs={{0,4},{4,8},{8,12},{12,16},{16,20},{20,24},{24,28},{1,5},{5,9},{9,... | collective-permute-start | bytes 1179656 | tf_op jit(solution)/shard_map/ppermute | solution.py:699
  144.7 15.0 %collective-permute-start.9 = (f32[128,768]{1,0:T(8,128)S(1)}, f32[128,768]{1,0:T(8,128)S(1)}, u32[]{:S(2)}, u32[]{:S(2)}) collective-permute-start(f32[128,768]{1,0:T(8,128)S(1)} %get-tuple-element.630), channel_id=1, source_target_pairs={{0,4},{4,8},{8,12},{12,16},{16,20},{20,24},{24,28},{1,5},{5,9},{9,... | collective-permute-start | bytes 1179656 | tf_op jit(solution)/shard_map/ppermute | solution.py:699
  147.4 26.6 %collective-permute-start.10 = (f32[128,768]{1,0:T(8,128)S(1)}, f32[128,768]{1,0:T(8,128)S(1)}, u32[]{:S(2)}, u32[]{:S(2)}) collective-permute-start(f32[128,768]{1,0:T(8,128)S(1)} %get-tuple-element.641), channel_id=1, source_target_pairs={{0,4},{4,8},{8,12},{12,16},{16,20},{20,24},{24,28},{1,5},{5,9},{9,... | collective-permute-start | bytes 1179656 | tf_op jit(solution)/shard_map/ppermute | solution.py:699
  175.4 15.9 %collective-permute-start.12 = (f32[128,768]{1,0:T(8,128)S(1)}, f32[128,768]{1,0:T(8,128)S(1)}, u32[]{:S(2)}, u32[]{:S(2)}) collective-permute-start(f32[128,768]{1,0:T(8,128)S(1)} %get-tuple-element.663), channel_id=1, source_target_pairs={{0,4},{4,8},{8,12},{12,16},{16,20},{20,24},{24,28},{1,5},{5,9},{9,... | collective-permute-start | bytes 1179656 | tf_op jit(solution)/shard_map/ppermute | solution.py:699
  184.9 20.3 %collective-permute-start.13 = (f32[128,768]{1,0:T(8,128)S(1)}, f32[128,768]{1,0:T(8,128)S(1)}, u32[]{:S(2)}, u32[]{:S(2)}) collective-permute-start(f32[128,768]{1,0:T(8,128)S(1)} %get-tuple-element.674), channel_id=1, source_target_pairs={{0,4},{4,8},{8,12},{12,16},{16,20},{20,24},{24,28},{1,5},{5,9},{9,... | collective-permute-start | bytes 1179656 | tf_op jit(solution)/shard_map/ppermute | solution.py:699
  192.7 30.7 %collective-permute-start.14 = (f32[128,768]{1,0:T(8,128)S(1)}, f32[128,768]{1,0:T(8,128)S(1)}, u32[]{:S(2)}, u32[]{:S(2)}) collective-permute-start(f32[128,768]{1,0:T(8,128)S(1)} %get-tuple-element.685), channel_id=1, source_target_pairs={{0,4},{4,8},{8,12},{12,16},{16,20},{20,24},{24,28},{1,5},{5,9},{9,... | collective-permute-start | bytes 1179656 | tf_op jit(solution)/shard_map/ppermute | solution.py:699
  215.4 17.5 %collective-permute-start.15 = (f32[128,768]{1,0:T(8,128)S(1)}, f32[128,768]{1,0:T(8,128)S(1)}, u32[]{:S(2)}, u32[]{:S(2)}) collective-permute-start(f32[128,768]{1,0:T(8,128)S(1)} %get-tuple-element.696), channel_id=1, source_target_pairs={{0,4},{4,8},{8,12},{12,16},{16,20},{20,24},{24,28},{1,5},{5,9},{9,... | collective-permute-start | bytes 1179656 | tf_op jit(solution)/shard_map/ppermute | solution.py:699
  224.8 16.5 %collective-permute-start.16 = (f32[128,768]{1,0:T(8,128)S(1)}, f32[128,768]{1,0:T(8,128)S(1)}, u32[]{:S(2)}, u32[]{:S(2)}) collective-permute-start(f32[128,768]{1,0:T(8,128)S(1)} %get-tuple-element.707), channel_id=1, source_target_pairs={{0,4},{4,8},{8,12},{12,16},{16,20},{20,24},{24,28},{1,5},{5,9},{9,... | collective-permute-start | bytes 1179656 | tf_op jit(solution)/shard_map/ppermute | solution.py:699
  242.7 20.5 %collective-permute-start.18 = (f32[128,768]{1,0:T(8,128)S(1)}, f32[128,768]{1,0:T(8,128)S(1)}, u32[]{:S(2)}, u32[]{:S(2)}) collective-permute-start(f32[128,768]{1,0:T(8,128)S(1)} %get-tuple-element.729), channel_id=1, source_target_pairs={{0,4},{4,8},{8,12},{12,16},{16,20},{20,24},{24,28},{1,5},{5,9},{9,... | collective-permute-start | bytes 1179656 | tf_op jit(solution)/shard_map/ppermute | solution.py:699
  350.2 18.2 %collective-permute-start.24 = (f32[128,768]{1,0:T(8,128)S(1)}, f32[128,768]{1,0:T(8,128)S(1)}, u32[]{:S(2)}, u32[]{:S(2)}) collective-permute-start(f32[128,768]{1,0:T(8,128)S(1)} %get-tuple-element.819), channel_id=1, source_target_pairs={{4,0},{8,4},{12,8},{16,12},{20,16},{24,20},{28,24},{5,1},{9,5},{13... | collective-permute-start | bytes 1179656 | tf_op jit(solution)/shard_map/ppermute | solution.py:699
  362.5 23.4 %collective-permute-start.25 = (f32[128,768]{1,0:T(8,128)S(1)}, f32[128,768]{1,0:T(8,128)S(1)}, u32[]{:S(2)}, u32[]{:S(2)}) collective-permute-start(f32[128,768]{1,0:T(8,128)S(1)} %get-tuple-element.827), channel_id=1, source_target_pairs={{4,0},{8,4},{12,8},{16,12},{20,16},{24,20},{28,24},{5,1},{9,5},{13... | collective-permute-start | bytes 1179656 | tf_op jit(solution)/shard_map/ppermute | solution.py:699
  384.6 14.9 %collective-permute-start.26 = (f32[128,768]{1,0:T(8,128)S(1)}, f32[128,768]{1,0:T(8,128)S(1)}, u32[]{:S(2)}, u32[]{:S(2)}) collective-permute-start(f32[128,768]{1,0:T(8,128)S(1)} %get-tuple-element.835), channel_id=1, source_target_pairs={{4,0},{8,4},{12,8},{16,12},{20,16},{24,20},{28,24},{5,1},{9,5},{13... | collective-permute-start | bytes 1179656 | tf_op jit(solution)/shard_map/ppermute | solution.py:699
  387.5 17.1 %collective-permute-start.27 = (f32[128,768]{1,0:T(8,128)S(1)}, f32[128,768]{1,0:T(8,128)S(1)}, u32[]{:S(2)}, u32[]{:S(2)}) collective-permute-start(f32[128,768]{1,0:T(8,128)S(1)} %get-tuple-element.843), channel_id=1, source_target_pairs={{4,0},{8,4},{12,8},{16,12},{20,16},{24,20},{28,24},{5,1},{9,5},{13... | collective-permute-start | bytes 1179656 | tf_op jit(solution)/shard_map/ppermute | solution.py:699
  426.4 14.8 %collective-permute-start.31 = (f32[128,768]{1,0:T(8,128)S(1)}, f32[128,768]{1,0:T(8,128)S(1)}, u32[]{:S(2)}, u32[]{:S(2)}) collective-permute-start(f32[128,768]{1,0:T(8,128)S(1)} %get-tuple-element.875), channel_id=1, source_target_pairs={{4,0},{8,4},{12,8},{16,12},{20,16},{24,20},{28,24},{5,1},{9,5},{13... | collective-permute-start | bytes 1179656 | tf_op jit(solution)/shard_map/ppermute | solution.py:699
  450.4 67.3 %collective-permute-start.34 = (f32[128,768]{1,0:T(8,128)S(1)}, f32[128,768]{1,0:T(8,128)S(1)}, u32[]{:S(2)}, u32[]{:S(2)}) collective-permute-start(f32[128,768]{1,0:T(8,128)S(1)} %get-tuple-element.899), channel_id=1, source_target_pairs={{4,0},{8,4},{12,8},{16,12},{20,16},{24,20},{28,24},{5,1},{9,5},{13... | collective-permute-start | bytes 1179656 | tf_op jit(solution)/shard_map/ppermute | solution.py:699
  462.4 75.9 %collective-permute-start.35 = (f32[128,768]{1,0:T(8,128)S(1)}, f32[128,768]{1,0:T(8,128)S(1)}, u32[]{:S(2)}, u32[]{:S(2)}) collective-permute-start(f32[128,768]{1,0:T(8,128)S(1)} %get-tuple-element.907), channel_id=1, source_target_pairs={{4,0},{8,4},{12,8},{16,12},{20,16},{24,20},{28,24},{5,1},{9,5},{13... | collective-permute-start | bytes 1179656 | tf_op jit(solution)/shard_map/ppermute | solution.py:699
  535.4 21.9 %collective-permute-start.36 = (f32[128,768]{1,0:T(8,128)S(1)}, f32[128,768]{1,0:T(8,128)S(1)}, u32[]{:S(2)}, u32[]{:S(2)}) collective-permute-start(f32[128,768]{1,0:T(8,128)S(1)} %get-tuple-element.915), channel_id=1, source_target_pairs={{4,0},{8,4},{12,8},{16,12},{20,16},{24,20},{28,24},{5,1},{9,5},{13... | collective-permute-start | bytes 1179656 | tf_op jit(solution)/shard_map/ppermute | solution.py:699
  556.0 21.2 %collective-permute-start.37 = (f32[128,768]{1,0:T(8,128)S(1)}, f32[128,768]{1,0:T(8,128)S(1)}, u32[]{:S(2)}, u32[]{:S(2)}) collective-permute-start(f32[128,768]{1,0:T(8,128)S(1)} %get-tuple-element.923), channel_id=1, source_target_pairs={{4,0},{8,4},{12,8},{16,12},{20,16},{24,20},{28,24},{5,1},{9,5},{13... | collective-permute-start | bytes 1179656 | tf_op jit(solution)/shard_map/ppermute | solution.py:699
  575.8 22.4 %collective-permute-start.38 = (f32[128,768]{1,0:T(8,128)S(1)}, f32[128,768]{1,0:T(8,128)S(1)}, u32[]{:S(2)}, u32[]{:S(2)}) collective-permute-start(f32[128,768]{1,0:T(8,128)S(1)} %get-tuple-element.931), channel_id=1, source_target_pairs={{4,0},{8,4},{12,8},{16,12},{20,16},{24,20},{28,24},{5,1},{9,5},{13... | collective-permute-start | bytes 1179656 | tf_op jit(solution)/shard_map/ppermute | solution.py:699
  594.9 22.9 %collective-permute-start.39 = (f32[128,768]{1,0:T(8,128)S(1)}, f32[128,768]{1,0:T(8,128)S(1)}, u32[]{:S(2)}, u32[]{:S(2)}) collective-permute-start(f32[128,768]{1,0:T(8,128)S(1)} %get-tuple-element.939), channel_id=1, source_target_pairs={{4,0},{8,4},{12,8},{16,12},{20,16},{24,20},{28,24},{5,1},{9,5},{13... | collective-permute-start | bytes 1179656 | tf_op jit(solution)/shard_map/ppermute | solution.py:699
  615.9 21.5 %collective-permute-start.40 = (f32[128,768]{1,0:T(8,128)S(1)}, f32[128,768]{1,0:T(8,128)S(1)}, u32[]{:S(2)}, u32[]{:S(2)}) collective-permute-start(f32[128,768]{1,0:T(8,128)S(1)} %get-tuple-element.947), channel_id=1, source_target_pairs={{4,0},{8,4},{12,8},{16,12},{20,16},{24,20},{28,24},{5,1},{9,5},{13... | collective-permute-start | bytes 1179656 | tf_op jit(solution)/shard_map/ppermute | solution.py:699
  636.1 18.7 %collective-permute-start.41 = (f32[128,768]{1,0:T(8,128)S(1)}, f32[128,768]{1,0:T(8,128)S(1)}, u32[]{:S(2)}, u32[]{:S(2)}) collective-permute-start(f32[128,768]{1,0:T(8,128)S(1)} %get-tuple-element.955), channel_id=1, source_target_pairs={{4,0},{8,4},{12,8},{16,12},{20,16},{24,20},{28,24},{5,1},{9,5},{13... | collective-permute-start | bytes 1179656 | tf_op jit(solution)/shard_map/ppermute | solution.py:699
  699.0 42.0 %collective-permute-start.49 = (f32[2,768,768]{2,1,0:T(8,128)}, f32[2,768,768]{2,1,0:T(8,128)}, u32[]{:S(2)}, u32[]{:S(2)}) collective-permute-start(f32[2,768,768]{2,1,0:T(8,128)} %fusion.2), channel_id=1, source_target_pairs={{0,1},{1,0},{2,3},{3,2},{4,5},{5,4},{6,7},{7,6},{8,9},{9,8},{10,11... | collective-permute-start | bytes 14155784 | tf_op jit(solution)/shard_map/ppermute | solution.py:742
  708.3 23.5 %collective-permute-start.46 = (f32[2,192,2304]{2,1,0:T(8,128)}, f32[2,192,2304]{2,1,0:T(8,128)}, u32[]{:S(2)}, u32[]{:S(2)}) collective-permute-start(f32[2,192,2304]{2,1,0:T(8,128)} %fusion.13), channel_id=1, source_target_pairs={{0,1},{1,0},{2,3},{3,2},{4,5},{5,4},{6,7},{7,6},{8,9},{9,8},{10,11... | collective-permute-start | bytes 10616840 | tf_op jit(solution)/shard_map/ppermute | solution.py:742
  708.3 41.4 %collective-permute-start.48 = (f32[2,192,3072]{2,1,0:T(8,128)}, f32[2,192,3072]{2,1,0:T(8,128)}, u32[]{:S(2)}, u32[]{:S(2)}) collective-permute-start(f32[2,192,3072]{2,1,0:T(8,128)} %fusion.15), channel_id=1, source_target_pairs={{0,1},{1,0},{2,3},{3,2},{4,5},{5,4},{6,7},{7,6},{8,9},{9,8},{10,11... | collective-permute-start | bytes 14155784 | tf_op jit(solution)/shard_map/ppermute | solution.py:742
  (115 other events, 1581.1 us)
